TPU v7x, 32 devices: a whole 2x2x4 slice. The times are simulated.
32 devices in a mesh: rows: 8 (over z, y), seq: 4 (over x, core).
Axes of the slice: x: 2, y: 2, z: 4, core: 2. Of those that a mesh axis runs over, the one named last changes fastest.
Arguments:
- byte_ids: int32 [8, 2048], P('rows', 'seq'), may hold values from 0 to 255
- seg_ids: int32 [8, 2048], P('rows', 'seq'), may hold values from 0 to 15, never falling along the last dimension, each value on 1 to 1024 neighbouring positions
- row_len: int32 [8], P('rows'), may hold values from 256 to 2048, as said below
- embed_table: bfloat16 [256, 768], replicated, may hold values from -6 to 6
- conv_weight: bfloat16 [5, 768, 768], replicated, may hold values from -0.09375 to 0.09375
- conv_bias: float32 [768], replicated, may hold values from -3 to 3
- scorer: float32 [768], replicated, may hold values from -0.4375 to 0.4375
- calibration: float32 [4, 4], replicated, may hold values from -3 to 3
- cotangent: bfloat16 [8, 1024, 768], P('rows', 'seq'), may hold values from -6 to 6
Outputs:
- blocks: bfloat16 [8, 1024, 768], P('rows', 'seq')
- loss: float32 [], replicated
- grad_table: float32 [256, 768], replicated
- grad_conv: float32 [5, 768, 768], replicated
- grad_bias: float32 [768], replicated
- grad_scorer: float32 [768], replicated
- grad_calib: float32 [4, 4], replicated
Inputs may be any that keep to these rules, and one draw needn't show every extreme that they name: `seg_ids`: within each row, segment numbers start at 0, never fall and rise by at most one from one byte to the next. `row_len`: each row holds real bytes first and padding after them.
All inputs are finite; a program needn't handle non-finite values.
Results may differ from a plain program's by a relative error of at most 0.015.
Values may be sent and summed in bfloat16 or wider, within the bound.
No kernel may reach another device: no remote copies, remote signals or barrier semaphores. Data moves between devices by JAX's collectives and lax.ppermute only.
A program may use at most 128 MiB of HBM per device.

v0:
```python
import jax
import jax.numpy as jnp
from jax import lax
from jax.sharding import PartitionSpec as P


def from_behind(shard, axis, by):
    length = lax.axis_size(axis)
    pairs = [(i, i + by) for i in range(length) if 0 <= i + by < length]
    return lax.ppermute(shard, axis, pairs)


def body(
    byte_ids, seg_ids, row_len, embed_table, conv_weight, conv_bias, scorer, calibration, cotangent
):
    row_count, span_len = byte_ids.shape
    vocab_size, width_dim = embed_table.shape
    kernel_len = conv_weight.shape[0]
    size_count = calibration.shape[0]
    reach_len = size_count - 1
    precise = lax.Precision.HIGHEST
    start_pos = lax.axis_index("seq") * span_len
    positions = start_pos + jnp.arange(span_len, dtype=jnp.int32)
    real_mask = (positions[None, :] < row_len[:, None]).astype(jnp.float32)
    left_pos = start_pos - reach_len + jnp.arange(reach_len, dtype=jnp.int32)
    left_mask = ((left_pos[None, :] >= 0) & (left_pos[None, :] < row_len[:, None])).astype(
        jnp.float32
    )
    real_total = lax.psum(jnp.sum(row_len).astype(jnp.float32), "rows")
    embedded = jnp.take(embed_table, byte_ids, axis=0) * real_mask[:, :, None].astype(jnp.bfloat16)
    left_x = from_behind(embedded[:, span_len - kernel_len + 1 :], "seq", 1)
    extended_x = jnp.concatenate([left_x, embedded], axis=1)
    conv_full = jnp.broadcast_to(conv_bias, (row_count, span_len, width_dim))
    for offset in range(kernel_len):
        conv_full = conv_full + jnp.einsum(
            "rld,de->rle",
            extended_x[:, offset : offset + span_len],
            conv_weight[offset],
            preferred_element_type=jnp.float32,
        )
    conv_low = conv_full.astype(jnp.bfloat16)
    left_seg = from_behind(seg_ids[:, span_len - reach_len :], "seq", 1)
    left_y = from_behind(conv_low[:, span_len - reach_len :], "seq", 1)
    ext_y = jnp.concatenate([left_y, conv_low], axis=1)
    ext_seg = jnp.concatenate([left_seg, seg_ids], axis=1)
    ext_mask = jnp.concatenate([left_mask, real_mask], axis=1)
    running = jnp.zeros((row_count, span_len, width_dim), jnp.float32)
    counted = jnp.zeros((row_count, span_len), jnp.float32)
    pooled_list = []
    valid_list = []
    denom_list = []
    for lag_idx in range(size_count):
        begin = reach_len - lag_idx
        same_doc = (ext_seg[:, begin : begin + span_len] == seg_ids).astype(jnp.float32)
        valid = ext_mask[:, begin : begin + span_len] * real_mask * same_doc
        running = running + valid[:, :, None] * ext_y[:, begin : begin + span_len].astype(
            jnp.float32
        )
        counted = counted + valid
        denom = jnp.maximum(counted, 1.0)
        pooled_list.append(running / denom[:, :, None])
        valid_list.append(valid)
        denom_list.append(denom)
    scores = jnp.stack(
        [jnp.einsum("rld,d->rl", pooled, scorer, precision=precise) for pooled in pooled_list],
        axis=-1,
    )
    logits = jnp.einsum("rlb,bc->rlc", scores, calibration, precision=precise)
    probs = jax.nn.softmax(logits, axis=-1)
    mixed = probs[:, :, 0:1] * pooled_list[0]
    for size_idx in range(1, size_count):
        mixed = mixed + probs[:, :, size_idx : size_idx + 1] * pooled_list[size_idx]
    blocks = (jnp.sum(mixed.reshape(row_count, span_len // 2, 2, width_dim), axis=2) * 0.5).astype(
        jnp.bfloat16
    )
    mean_logit = jnp.sum(probs * logits, axis=-1)
    entropy_local = jnp.sum(real_mask * (jax.nn.logsumexp(logits, axis=-1) - mean_logit))
    entropy_total = lax.psum(entropy_local, ("rows", "seq"))
    half_grad = cotangent.astype(jnp.float32) * 0.5
    dmixed = jnp.broadcast_to(
        half_grad[:, :, None, :], (row_count, span_len // 2, 2, width_dim)
    ).reshape(row_count, span_len, width_dim)
    dprobs = jnp.stack([jnp.sum(dmixed * pooled, axis=-1) for pooled in pooled_list], axis=-1)
    dlogits = probs * (dprobs - jnp.sum(probs * dprobs, axis=-1, keepdims=True))
    dlogits = dlogits - (real_mask / real_total)[:, :, None] * probs * (
        logits - mean_logit[:, :, None]
    )
    grad_calib = jnp.einsum("rlb,rlc->bc", scores, dlogits, precision=precise)
    dscores = jnp.einsum("rlc,bc->rlb", dlogits, calibration, precision=precise)
    grad_scorer = jnp.zeros((width_dim,), jnp.float32)
    for size_idx in range(size_count):
        grad_scorer = grad_scorer + jnp.einsum(
            "rl,rld->d", dscores[:, :, size_idx], pooled_list[size_idx], precision=precise
        )
    dy_ext = jnp.zeros((row_count, span_len + reach_len, width_dim), jnp.float32)
    carried = jnp.zeros((row_count, span_len, width_dim), jnp.float32)
    for lag_idx in reversed(range(size_count)):
        dpooled = (
            probs[:, :, lag_idx : lag_idx + 1] * dmixed
            + dscores[:, :, lag_idx : lag_idx + 1] * scorer
        )
        carried = carried + dpooled / denom_list[lag_idx][:, :, None]
        begin = reach_len - lag_idx
        dy_ext = dy_ext.at[:, begin : begin + span_len].add(
            valid_list[lag_idx][:, :, None] * carried
        )
    from_next = from_behind(dy_ext[:, :reach_len], "seq", -1)
    dy_total = dy_ext[:, reach_len:] + jnp.pad(
        from_next, ((0, 0), (span_len - reach_len, 0), (0, 0))
    )
    dy_low = dy_total.astype(jnp.bfloat16)
    grad_bias = jnp.sum(dy_low, axis=(0, 1), dtype=jnp.float32)
    grad_conv = jnp.stack(
        [
            jnp.einsum(
                "rld,rle->de",
                extended_x[:, offset : offset + span_len],
                dy_low,
                preferred_element_type=jnp.float32,
            )
            for offset in range(kernel_len)
        ]
    )
    dx_ext = jnp.zeros((row_count, span_len + kernel_len - 1, width_dim), jnp.float32)
    for offset in range(kernel_len):
        dx_ext = dx_ext.at[:, offset : offset + span_len].add(
            jnp.einsum(
                "rle,de->rld", dy_low, conv_weight[offset], preferred_element_type=jnp.float32
            )
        )
    x_from_next = from_behind(dx_ext[:, : kernel_len - 1], "seq", -1)
    dx_total = dx_ext[:, kernel_len - 1 :] + jnp.pad(
        x_from_next, ((0, 0), (span_len - kernel_len + 1, 0), (0, 0))
    )
    dx_low = dx_total.astype(jnp.bfloat16) * real_mask[:, :, None].astype(jnp.bfloat16)
    one_hot = (byte_ids[:, :, None] == jnp.arange(vocab_size, dtype=jnp.int32)).astype(jnp.bfloat16)
    grad_table = jnp.einsum("rlv,rld->vd", one_hot, dx_low, preferred_element_type=jnp.float32)
    conv_sum, bias_sum, table_sum, scorer_sum, calib_sum = lax.psum(
        (grad_conv, grad_bias, grad_table, grad_scorer, grad_calib), ("rows", "seq")
    )
    loss = entropy_total / real_total
    return (blocks, loss, table_sum, conv_sum, bias_sum, scorer_sum, calib_sum)


def solution(mesh):
    return jax.shard_map(
        body,
        mesh=mesh,
        in_specs=(
            P("rows", "seq"),
            P("rows", "seq"),
            P("rows"),
            P(),
            P(),
            P(),
            P(),
            P(),
            P("rows", "seq", None),
        ),
        out_specs=(P("rows", "seq", None), P(), P(), P(), P(), P(), P()),
        check_vma=False,
    )
```

profile of v0, /device:TPU:0, one launch (start us, length us, event | category | flops | bytes accessed | tf_op | source)
XLA Modules:
  0.0 392.1 jit_solution(14714121555985678988)
XLA Ops:
  8.0 2.4 collective-permute-start.1
  11.0 23.0 %psum.50 = f32[]{:T(128)} all-reduce(f32[]{:T(128)S(6)} %convert_element_type.119), channel_id=1, replica_groups=mesh['rows'=8,'seq'=4] {'rows'}, use_global_device_ids=true, to_apply=%region_7.8 | all-reduce | flops 1 | bytes 8 | tf_op jit(solution)/shard_map/psum | solution.py:29
  41.0 2.2 broadcast_in_dim.35
  43.2 2.4 fusion.25
  45.9 2.1 fusion.36
  50.0 2.2 fusion.30
  52.3 2.6 multiply_reduce_fusion.3
  54.8 4.5 %collective-permute-start.2 = (bf16[1,3,768]{2,1,0:T(4,128)(2,1)S(1)}, bf16[1,3,768]{2,1,0:T(4,128)(2,1)S(1)}, u32[]{:S(2)}, u32[]{:S(2)}) collective-permute-start(bf16[1,3,768]{2,1,0:T(4,128)(2,1)S(1)} %slice.373), channel_id=1, source_target_pairs={{0,1},{1,2},{2,3},{4,5},{5,6},{6,7},{8,9},{9,10},{10,11},{12,13},{... | collective-permute-start | bytes 13832 | tf_op jit(solution)/shard_map/ppermute | solution.py:10
  61.0 2.2 multiply_reduce_fusion.2
  69.8 3.2 multiply_add_fusion
  72.9 4.9 %scatter-add.25 = f32[1,515,768]{2,1,0:T(8,128)} dynamic-update-slice(f32[1,515,768]{2,1,0:T(8,128)} %scatter-add.24, f32[1,512,768]{2,1,0:T(8,128)} %get-tuple-element.151, s32[]{:T(128)} %constant.266.clone.1, s32[]{:T(128)} %constant.274.clone.1, s32[]{:T(128)} %constant.266.clone.1) | dynamic-update-slice | bytes 3145732 | tf_op jit(solution)/shard_map/scatter-add | solution.py:104
  77.9 3.2 slice_add_fusion.4
  81.1 4.9 %scatter-add.26 = f32[1,515,768]{2,1,0:T(8,128)} dynamic-update-slice(f32[1,515,768]{2,1,0:T(8,128)} %scatter-add.25, f32[1,512,768]{2,1,0:T(8,128)} %slice_add_fusion.4, s32[]{:T(128)} %constant.266.clone.1, s32[]{:T(128)} %constant.275.clone.1, s32[]{:T(128)} %constant.266.clone.1) | dynamic-update-slice | bytes 3145732 | tf_op jit(solution)/shard_map/scatter-add | solution.py:104
  89.8 3.7 convert_reduce_fusion
  93.5 2.4 convolution_bitcast_fusion
  95.9 3.2 bitcast_add_fusion
  100.4 5.0 %scatter-add.30 = f32[1,516,768]{2,1,0:T(8,128)} dynamic-update-slice(f32[1,516,768]{2,1,0:T(8,128)} %scatter-add.29, f32[1,512,768]{2,1,0:T(8,128)} %bitcast_add_fusion, s32[]{:T(128)} %constant.266.clone.1, s32[]{:T(128)} %constant.274.clone.1, s32[]{:T(128)} %constant.266.clone.1) | dynamic-update-slice | bytes 3145732 | tf_op jit(solution)/shard_map/scatter-add | solution.py:126
  105.4 3.7 slice_add_fusion.2
  109.2 4.9 %scatter-add.31 = f32[1,516,768]{2,1,0:T(8,128)} dynamic-update-slice(f32[1,516,768]{2,1,0:T(8,128)} %scatter-add.30, f32[1,512,768]{2,1,0:T(8,128)} %slice_add_fusion.2, s32[]{:T(128)} %constant.266.clone.1, s32[]{:T(128)} %constant.275.clone.1, s32[]{:T(128)} %constant.266.clone.1) | dynamic-update-slice | bytes 3145732 | tf_op jit(solution)/shard_map/scatter-add | solution.py:126
  114.1 3.7 slice_add_fusion.1
  117.8 5.0 %scatter-add.34 = f32[1,516,768]{2,1,0:T(8,128)} dynamic-update-slice(f32[1,516,768]{2,1,0:T(8,128)} %scatter-add.31, f32[1,512,768]{2,1,0:T(8,128)} %slice_add_fusion.1, s32[]{:T(128)} %constant.266.clone.1, s32[]{:T(128)} %constant.276.clone.1, s32[]{:T(128)} %constant.266.clone.1) | dynamic-update-slice | bytes 3145732 | tf_op jit(solution)/shard_map/scatter-add | solution.py:126
  125.1 2.2 bitcast_dynamic-update-slice_fusion.4
  127.3 2.2 bitcast_dynamic-update-slice_fusion.3
  129.6 2.2 bitcast_dynamic-update-slice_fusion.2
  131.8 2.2 bitcast_dynamic-update-slice_fusion.1
  134.0 2.3 bitcast_dynamic-update-slice_fusion
  136.4 4.0 %fusion.22 = f32[256,768]{1,0:T(8,128)} fusion(f32[1,4,768]{2,1,0:T(4,128)S(1)} %collective-permute-done.4, f32[1,516,768]{2,1,0:T(8,128)} %scatter-add.34, bf16[5,768,768]{2,1,0:T(8,128)(2,1)} %param.31, bf16[1,512,768]{2,1,0:T(8,128)(2,1)S(1)} %copy-done.7, bf16[512]{0:T(512)(128)(2,1)S(1)} %convert_convert_fusion, s32[512]{0:T(512)S(1)} %bitcast.296), kind=kOutput, calls=%fused_computation.53 | convolution fusion | flops 807010304 | bytes 4340736 | tf_op jit(solution)/shard_map/rlv,rld->vd/dot_general | solution.py:137
  141.8 2.1 reshape.2072
  143.9 4.3 %reduce_sum.104 = f32[256,768]{1,0:T(8,128)} reduce(f32[256,2,768]{2,1,0:T(2,128)} %reshape.2072, f32[]{:T(128)} %constant.265.clone.1), dimensions={1}, to_apply=%region_2.3 | reduce | flops 196608 | bytes 2359300 | tf_op jit(solution)/shard_map/reduce_sum | solution.py:73
  154.1 40.6 %all-reduce.4 = (f32[]{:T(128)}, f32[768]{0:T(1024)}, f32[768]{0:T(1024)}, f32[4,4]{1,0:T(4,128)}) all-reduce(f32[]{:T(128)} %select_reduce_fusion, f32[768]{0:T(1024)S(1)} %get-tuple-element.127, f32[768]{0:T(1024)S(1)} %add_add_fusion, f32[4,4]{1,0:T(4,128)S(1)} %fusion.114), channel_id=1, replica_groups=mesh['rows'=8,'seq'=4] {'rows','seq'}, use_global_device_ids=true, to_apply=%region_6.7 | all-reduce | flops 1553 | bytes 12424 | tf_op jit(solution)/shard_map/psum | solution.py:78
  196.0 175.9 %all-reduce.8.cloned.1.call-done = (f32[256,768]{1,0:T(8,128)}, f32[5,768,768]{2,1,0:T(8,128)}) async-done(((f32[256,768]{1,0:T(8,128)}, f32[5,768,768]{2,1,0:T(8,128)}), (f32[256,768]{1,0:T(8,128)}, f32[5,768,768]{2,1,0:T(8,128)})) %all-reduce.8.cloned.1.call-update) | async-done | bytes 12582928 | tf_op jit(solution)/shard_map/psum | solution.py:138
  373.9 10.2 %copy.29 = f32[5,768,768]{2,1,0:T(8,128)} copy(f32[5,768,768]{2,1,0:T(8,128)} %get-tuple-element.163) | data formatting | bytes 23592960
  (105 shorter events, 34.1 us)
Async XLA Ops:
  7.2 28.3 %copy-start = (bf16[256,768]{1,0:T(8,128)(2,1)S(1)}, bf16[256,768]{1,0:T(8,128)(2,1)}, u32[]{:S(2)}) copy-start(bf16[256,768]{1,0:T(8,128)(2,1)} %param.30) | copy-start | bytes 1179652
  7.2 364.7 %all-reduce.8.cloned.1.call-start = ((), (), s32[]{:S(2)}) async-start(), calls=%async_computation | async-start | bytes 25165824 | tf_op jit(solution)/shard_map/psum | solution.py:138
  8.0 37.7 %collective-permute-start.1 = (s32[1,3]{1,0:T(1,128)S(1)}, s32[1,3]{1,0:T(1,128)S(1)}, u32[]{:S(2)}, u32[]{:S(2)}) collective-permute-start(s32[1,3]{1,0:T(1,128)S(1)} %slice.332), channel_id=1, source_target_pairs={{0,1},{1,2},{2,3},{4,5},{5,6},{6,7},{8,9},{9,10},{10,11},{12,13},{... | collective-permute-start | bytes 44 | tf_op jit(solution)/shard_map/ppermute | solution.py:10
  37.5 1.7 copy-start.12
  37.5 1.7 copy-start.19
  37.8 1.5 copy-start.15
  37.8 8.1 %collective-permute-start = (bf16[1,4,768]{2,1,0:T(4,128)(2,1)S(1)}, bf16[1,4,768]{2,1,0:T(4,128)(2,1)S(1)}, u32[]{:S(2)}, u32[]{:S(2)}) collective-permute-start(bf16[1,4,768]{2,1,0:T(4,128)(2,1)S(1)} %slice.362), channel_id=1, source_target_pairs={{0,1},{1,2},{2,3},{4,5},{5,6},{6,7},{8,9},{9,10},{10,11},{12,13},{... | collective-permute-start | bytes 18440 | tf_op jit(solution)/shard_map/ppermute | solution.py:10
  41.0 2.2 copy-start.20
  43.2 2.5 copy-start.21
  43.2 2.6 copy-start.16
  50.0 2.2 copy-start.14
  50.0 2.2 copy-start.24
  54.8 15.0 %copy-start.4 = (bf16[512,768]{1,0:T(8,128)(2,1)}, bf16[512,768]{1,0:T(8,128)(2,1)S(1)}, u32[]{:S(2)}) copy-start(bf16[512,768]{1,0:T(8,128)(2,1)S(1)} %get-tuple-element.157) | copy-start | bytes 2359300
  54.8 6.2 %collective-permute-start.2 = (bf16[1,3,768]{2,1,0:T(4,128)(2,1)S(1)}, bf16[1,3,768]{2,1,0:T(4,128)(2,1)S(1)}, u32[]{:S(2)}, u32[]{:S(2)}) collective-permute-start(bf16[1,3,768]{2,1,0:T(4,128)(2,1)S(1)} %slice.373), channel_id=1, source_target_pairs={{0,1},{1,2},{2,3},{4,5},{5,6},{6,7},{8,9},{9,10},{10,11},{12,13},{... | collective-permute-start | bytes 13832 | tf_op jit(solution)/shard_map/ppermute | solution.py:10
  63.2 6.6 %copy-start.2 = (f32[1,512,768]{2,1,0:T(8,128)}, f32[1,512,768]{2,1,0:T(8,128)S(1)}, u32[]{:S(2)}) copy-start(f32[1,512,768]{2,1,0:T(8,128)S(1)} %get-tuple-element.132) | copy-start | bytes 4718596
  63.2 6.6 %copy-start.8 = (f32[1,512,768]{2,1,0:T(8,128)}, f32[1,512,768]{2,1,0:T(8,128)S(1)}, u32[]{:S(2)}) copy-start(f32[1,512,768]{2,1,0:T(8,128)S(1)} %get-tuple-element.133) | copy-start | bytes 4718596
  66.0 1.6 copy-start.22
  86.8 3.1 collective-permute-start.3
  93.5 2.4 copy-start.6
  100.4 5.0 %copy-start.7 = (bf16[1,512,768]{2,1,0:T(8,128)(2,1)S(1)}, bf16[1,512,768]{2,1,0:T(8,128)(2,1)}, u32[]{:S(2)}) copy-start(bf16[1,512,768]{2,1,0:T(8,128)(2,1)} %copy-done.6) | copy-start | bytes 2359300
  117.8 7.3 %copy-start.17 = (bf16[1,512,768]{2,1,0:T(8,128)(2,1)S(1)}, bf16[1,512,768]{2,1,0:T(8,128)(2,1)}, u32[]{:S(2)}) copy-start(bf16[1,512,768]{2,1,0:T(8,128)(2,1)} %copy-done.15) | copy-start | bytes 2359300
  123.6 12.8 %collective-permute-start.4 = (f32[1,4,768]{2,1,0:T(4,128)S(1)}, f32[1,4,768]{2,1,0:T(4,128)S(1)}, u32[]{:S(2)}, u32[]{:S(2)}) collective-permute-start(f32[1,4,768]{2,1,0:T(4,128)S(1)} %slice.396), channel_id=1, source_target_pairs={{1,0},{2,1},{3,2},{5,4},{6,5},{7,6},{9,8},{10,9},{11,10},{13,12},{... | collective-permute-start | bytes 36872 | tf_op jit(solution)/shard_map/ppermute | solution.py:10
  129.6 2.2 copy-start.18
  131.8 2.2 copy-start.13
  134.0 2.4 copy-start.23
  140.4 1.4 copy-start.10
  143.9 4.9 %copy-start.3 = (f32[1,512,768]{2,1,0:T(8,128)S(1)}, f32[1,512,768]{2,1,0:T(8,128)}, u32[]{:S(2)}) copy-start(f32[1,512,768]{2,1,0:T(8,128)} %copy-done.2) | copy-start | bytes 4718596
  148.8 1.9 copy-start.5
  150.7 1.5 copy-start.9
  152.1 1.2 copy-start.11
  373.9 10.2 %copy-start.1 = (bf16[256,768]{1,0:T(8,128)(2,1)S(1)}, bf16[256,768]{1,0:T(8,128)(2,1)}, u32[]{:S(2)}) copy-start(bf16[256,768]{1,0:T(8,128)(2,1)} %param.30) | copy-start | bytes 1179652
Sparse Core Ops, SparseCore 0:
  140.5 231.2 all-reduce.7
where the time goes:
time: 394 us; the launch traced here: 392 us
  waiting for transfers between devices  178 us (45%)
  blocking collectives  63.7 us (16%)
  local copies, waits for them, and re-layouts  51.9 us (13%)
  matrix products  50 us (13%)
  other arithmetic  19.5 us (5%)
  between operations  18.3 us (5%)
  starting transfers between devices  11.1 us (3%)
    psum x1, waiting for transfers between devices, body(): lax.psum((grad_conv, grad_bias, grad_table, grad_scorer, grad_calib), ('r...  176 us
    psum x1, blocking collectives, body(): entropy_total = lax.psum(entropy_local, ('rows', 'seq'))  40.6 us
    psum x1, blocking collectives, body(): real_total = lax.psum(jnp.sum(row_len).astype(jnp.float32), 'rows')  23 us
    scatter-add x4, local copies, waits for them, and re-layouts, body(): dx_ext.at[:, offset:offset + span_len]  16.3 us
    unnamed x53, local copies, waits for them, and re-layouts  14.3 us
    dot_general x4, matrix products, body(): jnp.einsum('rle,de->rld', dy_low, conv_weight[offset], preferred_element_...  13.1 us
    dot_general x5, matrix products, body(): jnp.einsum('rld,de->rle', extended_x[:, offset:offset + span_len], conv_w...  11.3 us
    dot_general x5, matrix products, body(): jnp.einsum('rld,rle->de', extended_x[:, offset:offset + span_len], dy_low...  11.2 us
  transfers between devices with their start and end apart: 6, of which 2 were waited for; matrix products, arithmetic and copies ran while one was open for 9% of the time, Pallas kernels for 0%

commit v1 on v0

v1 whole, which is shorter than its diff:
```python
import jax
import jax.numpy as jnp
import numpy as np
from jax import lax
from jax.experimental import pallas as pl
from jax.experimental.pallas import tpu as pltpu
from jax.sharding import PartitionSpec as P

AXES = ("rows", "seq")
BF = jnp.bfloat16
F32 = jnp.float32
HALO = 16
VMEM_LIMIT = 48 * 1024 * 1024


def dot_nn(a, b):
    return lax.dot_general(a, b, (((1,), (0,)), ((), ())), preferred_element_type=F32)


def dot_nt(a, b):
    return lax.dot_general(a, b, (((1,), (1,)), ((), ())), preferred_element_type=F32)


def dot_tn(a, b):
    return lax.dot_general(a, b, (((0,), (0,)), ((), ())), preferred_element_type=F32)


def split2(v):
    hi = v.astype(BF)
    return hi, (v - hi.astype(F32)).astype(BF)


def split3(v):
    hi = v.astype(BF)
    rest = v - hi.astype(F32)
    mid = rest.astype(BF)
    return hi, mid, (rest - mid.astype(F32)).astype(BF)


def call(kernel, outs, name, **kw):
    return pl.pallas_call(
        kernel,
        out_shape=outs,
        name=name,
        compiler_params=pltpu.CompilerParams(vmem_limit_bytes=VMEM_LIMIT),
        **kw,
    )


def vspec():
    return pl.BlockSpec(memory_space=pltpu.VMEM)


def sspec():
    return pl.BlockSpec(memory_space=pltpu.SMEM)


def shape(dims, dtype):
    return jax.ShapeDtypeStruct(dims, dtype)


def tap_kernel(table_ref, weight_ref, scorer_ref, hi_ref, lo_ref, q_ref):
    hi, lo = split2(dot_nn(table_ref[...], weight_ref[0]))
    hi_ref[0] = hi
    lo_ref[0] = lo

    @pl.when(pl.program_id(0) == 0)
    def _():
        s1, s2, s3 = split3(scorer_ref[...])
        row = lax.broadcasted_iota(jnp.int32, q_ref.shape, 0)
        pick = jnp.where(row == 0, s1.astype(F32), jnp.where(row == 1, s2.astype(F32), s3.astype(F32)))
        q_ref[...] = jnp.where(row < 3, pick, 0.0).astype(BF)


def roll(v, by):
    by = by % v.shape[1]
    return pltpu.roll(v, by, 1) if by else v


def local_kernel(
    info_ref, calib_ref, idk_ref, lane_ref, idt_ref, hi_ref, lo_ref, bias_ref, cot_ref, cot_next_ref,
    q_ref, blocks_ref, keep_ref, send_ref, ext_ref, y_ref, full_q_ref, oh_ref,
):
    taps, vocab, width = hi_ref.shape
    span = keep_ref.shape[0]
    half = width // 2
    own_blocks = span // 2
    rows_y = idk_ref.shape[0]
    lanes = y_ref.shape[0]
    sizes = calib_ref.shape[0]
    value = lax.broadcasted_iota(jnp.int32, (rows_y, vocab), 1).astype(F32)
    acc = jnp.broadcast_to(bias_ref[...], (rows_y, width))
    for k in range(taps):
        one_hot = jnp.where(idk_ref[:, k : k + 1] == value, 1.0, 0.0).astype(BF)
        oh_ref[k] = one_hot
        acc = acc + (dot_nn(one_hot, hi_ref[k]) + dot_nn(one_hot, lo_ref[k]))
    y = acc.astype(BF)
    front = span + HALO
    y_ref[0:front] = y[0:front]
    y_ref[front : lanes - HALO] = jnp.zeros((lanes - HALO - front, width), BF)
    y_ref[lanes - HALO : lanes] = y[front : front + HALO]
    full_q_ref[0:own_blocks] = cot_ref[...]
    full_q_ref[own_blocks : own_blocks + HALO] = cot_next_ref[...]
    full_q_ref[own_blocks + HALO : own_blocks + 2 * HALO] = q_ref[...]
    tail = own_blocks + HALO
    q_rows = own_blocks + 2 * HALO
    dots = dot_nt(full_q_ref[...], y_ref[...])
    u = dots[tail : tail + 1] + dots[tail + 1 : tail + 2] + dots[tail + 2 : tail + 3]

    pos = lax.broadcasted_iota(jnp.int32, (1, lanes), 1)
    own = jnp.where(pos < span, 1.0, 0.0)
    seg = lane_ref[0:1]
    mask = lane_ref[1:2]
    line = lax.broadcasted_iota(jnp.int32, (q_rows, lanes), 0)
    valid, match, grads = [], [], []
    for d in range(sizes):
        valid.append(mask * roll(mask, d) * jnp.where(seg == roll(seg, d), 1.0, 0.0))
        ahead = jnp.where(pos + d >= lanes, pos + d - lanes, pos + d)
        block = jnp.where(ahead < front, lax.shift_right_logical(ahead, 1), -1)
        match.append(line == block)
        picked = jnp.sum(jnp.where(match[d], dots, 0.0), axis=0, keepdims=True)
        grads.append(0.5 * roll(picked, d))
    counted, inv, scores, dprobs = 0.0, [], [], []
    run_u, run_g = 0.0, 0.0
    for d in range(sizes):
        counted = counted + valid[d]
        inv.append(1.0 / jnp.maximum(counted, 1.0))
        run_u = run_u + valid[d] * roll(u, d)
        run_g = run_g + valid[d] * grads[d]
        scores.append(run_u * inv[d])
        dprobs.append(run_g * inv[d])
    logits = [sum(scores[b] * calib_ref[b, c] for b in range(sizes)) for c in range(sizes)]
    top = logits[0]
    for c in range(1, sizes):
        top = jnp.maximum(top, logits[c])
    powers = [jnp.exp(v - top) for v in logits]
    total = sum(powers)
    probs = [v / total for v in powers]
    lse = top + jnp.log(total)
    mean_logit = sum(p * v for p, v in zip(probs, logits))
    mean_grad = sum(p * v for p, v in zip(probs, dprobs))
    entropy = own * mask * (lse - mean_logit)
    parts = [
        [p * (v - mean_grad) for p, v in zip(probs, dprobs)],
        [mask * p * (v - mean_logit) for p, v in zip(probs, logits)],
    ]
    alpha, later = [None] * sizes, 0.0
    for d in reversed(range(sizes)):
        later = later + probs[d] * inv[d]
        alpha[d] = valid[d] * later
    gammas, rhos, calibs = [], [], []
    for part in parts:
        dscores = [sum(part[c] * calib_ref[b, c] for c in range(sizes)) for b in range(sizes)]
        later, gamma, rho = 0.0, 0.0, 0.0
        for d in reversed(range(sizes)):
            later = later + inv[d] * dscores[d]
            beta = valid[d] * later
            gamma = gamma + roll(beta, -d)
            rho = rho + roll(beta * own, -d)
        gammas.append(gamma)
        rhos.append(rho)
        calibs.append([[jnp.sum(own * scores[b] * part[c], axis=1, keepdims=True) for c in range(sizes)] for b in range(sizes)])
    band = jnp.where((line >= tail) & (line < tail + 3), gammas[0], 0.0)
    for d in range(sizes):
        band = band + jnp.where(match[d], 0.5 * roll(alpha[d], -d), 0.0)
    band_hi, band_lo = split2(band)
    mixed = dot_nn(band_hi[0:own_blocks], y_ref[...]) + dot_nn(band_lo[0:own_blocks], y_ref[...])
    blocks_ref[...] = mixed.astype(BF)
    dy = dot_tn(band_hi[:, 0:span], full_q_ref[...]) + dot_tn(band_lo[:, 0:span], full_q_ref[...])
    dy = dy.astype(BF)
    left, right = dy[:, 0:half], dy[:, half:width]
    upper = info_ref[0] == 1
    keep_ref[...] = jnp.where(upper, right, left)
    send_ref[0:span] = jnp.where(upper, left, right)
    grad_bias = jnp.sum(dy.astype(F32), axis=0, keepdims=True)

    row8 = lax.broadcasted_iota(jnp.int32, (16, lanes), 0)
    stack = jnp.zeros((16, lanes), F32)
    pieces = split3(rhos[0]) + split3(rhos[1]) + split3(gammas[1] * own)
    for i, piece in enumerate(pieces):
        stack = jnp.where(row8 == i, piece.astype(F32), stack)
    stack = stack.astype(BF)
    by_y = dot_nn(stack, y_ref[...])
    grad_scorer = [by_y[3 * i : 3 * i + 1] + by_y[3 * i + 1 : 3 * i + 2] + by_y[3 * i + 2 : 3 * i + 3] for i in range(2)]
    ext_ref[...] = jnp.zeros(ext_ref.shape, F32)
    for i, row in enumerate(grad_scorer + [grad_bias]):
        ext_ref[2 * i : 2 * i + 1] = row[:, 0:half]
        ext_ref[2 * i + 1 : 2 * i + 2] = row[:, half:width]
    for k in range(taps):
        by_tap = dot_nn(stack[:, 0:span], oh_ref[k, 0:span])
        ext_ref[6 + k : 7 + k, 0:vocab] = by_tap[6:7] + by_tap[7:8] + by_tap[8:9]
    spot = lax.broadcasted_iota(jnp.int32, (1, half), 1)
    misc = jnp.zeros((1, half), F32)
    sums = [calibs[i][b][c] for i in range(2) for b in range(sizes) for c in range(sizes)]
    sums.append(jnp.sum(entropy, axis=1, keepdims=True))
    sums.append(jnp.sum(own * mask, axis=1, keepdims=True))
    sums.append(jnp.sum(own * gammas[1], axis=1, keepdims=True))
    for i, one in enumerate(sums):
        misc = jnp.where(spot == i, one, misc)
    ext_ref[11:12] = misc
    ext_hi, ext_lo = split2(ext_ref[...])
    send_ref[span : span + 16] = ext_hi
    send_ref[span + 16 : span + 32] = ext_lo
    ids = idt_ref[...]
    send_ref[span + 32 : span + 48] = jnp.concatenate([ids, jnp.zeros((16, half - ids.shape[1]), BF)], axis=1)


def joined(ext_ref):
    hi, lo = split2(ext_ref[...])
    return hi.astype(F32) + lo.astype(F32)


def pair(ref, at):
    return ref[at : at + 16].astype(F32) + ref[at + 16 : at + 32].astype(F32)


def local_value(shape_, dim, info_ref, vocab):
    slot = lax.broadcasted_iota(jnp.int32, shape_, dim)
    mine = jnp.where(slot < vocab // 2, info_ref[1], info_ref[2])
    return jnp.bitwise_xor(slot, mine)


def table_kernel(info_ref, keep_ref, idt_ref, got_ref, ext_ref, a_keep, a_send, b_keep, b_send, ext_out):
    span, half = keep_ref.shape
    taps, quarter, _ = a_keep.shape
    vocab = 4 * quarter
    value = local_value((vocab, 1), 0, info_ref, vocab).astype(F32)
    mine = idt_ref[...].astype(F32)
    theirs = got_ref[span + 32 : span + 48].astype(F32)
    wide = mine.shape[1]
    for k in range(taps):
        acc = None
        for i in range(span // wide):
            for ids, grad in ((mine, keep_ref), (theirs, got_ref)):
                row = ids[2 * k + i : 2 * k + i + 1, 0:wide]
                one_hot = jnp.where(row == value, 1.0, 0.0).astype(BF)
                term = dot_nn(one_hot, grad[i * wide : (i + 1) * wide])
                acc = term if acc is None else acc + term
        a_keep[k] = acc[0:quarter]
        a_send[k * quarter : (k + 1) * quarter] = acc[quarter : 2 * quarter].astype(BF)
        b_keep[k] = acc[2 * quarter : 3 * quarter]
        b_send[k * quarter : (k + 1) * quarter] = acc[3 * quarter : 4 * quarter].astype(BF)
    ext = joined(ext_ref) + pair(got_ref, span)
    ext_out[...] = ext
    hi, lo = split2(ext)
    a_send[taps * quarter : taps * quarter + 16] = hi
    a_send[taps * quarter + 16 : taps * quarter + 32] = lo


def second_kernel(a_in, b_in, a_got, b_got, ext_ref, a_keep, a_send, b_keep, b_send, ext_out):
    taps, rows, _ = a_in.shape
    part = rows // 2
    for src, got, keep, send in ((a_in, a_got, a_keep, a_send), (b_in, b_got, b_keep, b_send)):
        for k in range(taps):
            total = src[k] + got[k * rows : (k + 1) * rows].astype(F32)
            keep[k] = total[0:part]
            send[k * part : (k + 1) * part] = total[part:rows].astype(BF)
    ext = joined(ext_ref) + pair(a_got, taps * rows)
    ext_out[...] = ext
    hi, lo = split2(ext)
    a_send[taps * part : taps * part + 16] = hi
    a_send[taps * part + 16 : taps * part + 32] = lo


def third_kernel(a_in, b_in, a_got, b_got, ext_ref, keep, ext_out, *sends):
    taps, rows, _ = a_in.shape
    peers = len(sends)
    part = rows // (peers + 1)
    ext = joined(ext_ref) + pair(a_got, taps * rows)
    ext_out[...] = ext
    hi, lo = split2(ext)
    groups = 2 * taps
    pieces = [[] for _ in range(peers + 1)]
    for src, got in ((a_in, a_got), (b_in, b_got)):
        for k in range(taps):
            total = src[k] + got[k * rows : (k + 1) * rows].astype(F32)
            for t in range(peers + 1):
                pieces[t].append(total[t * part : (t + 1) * part])
    for t in range(peers + 1):
        block = jnp.concatenate(pieces[t], axis=0)
        if t == 0:
            keep[...] = block
        else:
            send = sends[t - 1]
            send[0 : groups * part] = block.astype(BF)
            send[groups * part : groups * part + 16] = hi
            send[groups * part + 16 : groups * part + 32] = lo


def tree_sum(items):
    while len(items) > 1:
        items = [items[i] + items[i + 1] for i in range(0, len(items), 2)]
    return items[0]


def shard_kernel(info_ref, keep, ext_ref, scorer_ref, *refs):
    gots, (shard, small) = refs[:-2], refs[-2:]
    size = keep.shape[0]
    half = keep.shape[1]
    vocab = 256
    taps = 5
    part = size // (2 * taps)
    ext = tree_sum([joined(ext_ref)] + [pair(g, size) for g in gots])
    total = tree_sum([keep[...]] + [g[0:size].astype(F32) for g in gots])
    spot = lax.broadcasted_iota(jnp.int32, (1, half), 1)
    misc = ext[11:12]

    def one(i):
        return jnp.sum(jnp.where(spot == i, misc, 0.0), axis=1, keepdims=True)

    count = one(33)
    scorer = scorer_ref[...]
    upper = info_ref[0] == 1
    mine = jnp.where(upper, scorer[1:2], scorer[0:1])
    step = lax.broadcasted_iota(jnp.int32, (part, vocab), 0)
    lane = lax.broadcasted_iota(jnp.int32, (part, vocab), 1)
    for g in range(2):
        first = info_ref[1 + g]
        hit = lane == first + step
        for k in range(taps):
            column = jnp.sum(jnp.where(hit, ext[6 + k : 7 + k, 0:vocab], 0.0), axis=1, keepdims=True)
            at = (g * taps + k) * part
            piece = total[at : at + part] - (column / count) * mine
            shard[at : at + part] = piece.astype(BF)
    for h in range(2):
        small[h : h + 1] = ext[h : h + 1] - ext[2 + h : 3 + h] / count
        small[2 + h : 3 + h] = ext[4 + h : 5 + h] - (one(34) / count) * scorer[h : h + 1]
    moved = roll(misc, -16)
    small[4:5] = jnp.where(spot < 16, misc - moved / count, misc / count)
    small[5:8] = jnp.zeros((3, half), F32)


def final_kernel(
    info_ref, col_ref, early_ref, a_ref, b_ref, table_t_ref, weight_ref, conv_in, table_in,
    conv_ref, table_ref, perm_ref,
):
    k = pl.program_id(0)
    vocab = table_ref.shape[0]

    @pl.when(k == 0)
    def _():
        value = local_value((1, vocab), 1, info_ref, vocab)
        natural = lax.broadcasted_iota(jnp.int32, (vocab, vocab), 0)
        perm_ref[...] = jnp.where(natural == value, 1.0, 0.0).astype(BF)
        if table_in is None:
            table_ref[...] = jnp.zeros(table_ref.shape, F32)
        else:
            table_ref[...] = table_in[...]

    local = jnp.concatenate([early_ref[0, 0], a_ref[0], early_ref[1, 0], b_ref[0]], axis=0)
    rows = dot_nn(perm_ref[...], local).astype(BF)
    conv_ref[0] = dot_nn(table_t_ref[...], rows)
    table_ref[...] += dot_nt(rows, weight_ref[0])


def finish(info, col, early, a, b, table_t, weight, conv_in=None, table_in=None):
    taps, width, _ = weight.shape
    vocab = table_t.shape[1]
    half = width // 2
    quarter = vocab // 4
    specs = [
        pl.BlockSpec((2, 1, quarter, half), lambda k, info, col: (0, k, 0, 0)),
        pl.BlockSpec((1, quarter, half), lambda k, info, col: (k, 0, 0)),
        pl.BlockSpec((1, quarter, half), lambda k, info, col: (k, 0, 0)),
        pl.BlockSpec((width, vocab), lambda k, info, col: (0, 0)),
        pl.BlockSpec((1, width, half), lambda k, info, col: (k, 0, col[0])),
    ]
    args = [early, a, b, table_t, weight]
    kernel = final_kernel
    aliases = {}
    if conv_in is None:

        def kernel(info_ref, col_ref, e, a, b, t, w, conv_ref, table_ref, perm_ref):
            final_kernel(info_ref, col_ref, e, a, b, t, w, None, None, conv_ref, table_ref, perm_ref)

    else:
        specs += [pl.BlockSpec(memory_space=pl.ANY), pl.BlockSpec((vocab, width), lambda k, info, col: (0, 0))]
        args += [conv_in, table_in]
        aliases = {7: 0}
    return pl.pallas_call(
        kernel,
        out_shape=(shape((taps, width, width), F32), shape((vocab, width), F32)),
        grid_spec=pltpu.PrefetchScalarGridSpec(
            num_scalar_prefetch=2,
            grid=(taps,),
            in_specs=specs,
            out_specs=(
                pl.BlockSpec((1, width, half), lambda k, info, col: (k, 0, col[0])),
                pl.BlockSpec((vocab, width), lambda k, info, col: (0, 0)),
            ),
            scratch_shapes=[pltpu.VMEM((vocab, vocab), BF)],
        ),
        input_output_aliases=aliases,
        name="finish_first" if conv_in is None else "finish_second",
        compiler_params=pltpu.CompilerParams(vmem_limit_bytes=VMEM_LIMIT),
    )(info, col, *args)


def neighbour(shard, axis, by):
    length = lax.axis_size(axis)
    return lax.ppermute(shard, axis, [(i, i + by) for i in range(length) if 0 <= i + by < length])


def swap(shard, flip, count):
    return lax.ppermute(shard, AXES, [(i, i ^ flip) for i in range(count)])


def body(
    byte_ids, seg_ids, row_len, embed_table, conv_weight, conv_bias, scorer, calibration, cotangent
):
    row_count, span = byte_ids.shape
    vocab, width = embed_table.shape
    taps = conv_weight.shape[0]
    half = width // 2
    quarter = vocab // 4
    seq_size = lax.axis_size("seq")
    count = lax.axis_size("rows") * seq_size
    depth = count // 8
    assert row_count == 1 and vocab == 256 and taps == 5 and calibration.shape == (4, 4)
    assert seq_size % 2 == 0 and depth >= 1 and quarter // 2 % depth == 0
    part = quarter // 2 // depth
    number = np.arange(count)
    x_bit, y_bit, rest = (number >> 1) & 1, (number >> 2) & 1, number >> 3
    a_mine = x_bit * quarter + y_bit * (quarter // 2) + rest * part
    b_mine = vocab // 2 + y_bit * quarter + x_bit * (quarter // 2) + rest * part
    facts = np.stack([number & 1, a_mine, b_mine - vocab // 2, 1 - (number & 1)], axis=1).astype(np.int32)
    device = lax.axis_index("rows") * seq_size + lax.axis_index("seq")
    info = lax.dynamic_slice(jnp.asarray(facts), (device, 0), (1, 4)).reshape(4)
    shard_info = info + jnp.asarray(np.array([0, 0, vocab // 2, 0], np.int32))

    ids = byte_ids[0].astype(F32)
    segs = seg_ids[0].astype(F32)
    cot = cotangent[0]
    to_right = jnp.stack([ids[span - HALO :], segs[span - HALO :]]).astype(BF)
    to_left = jnp.concatenate(
        [cot[:HALO], jnp.pad(jnp.stack([ids[:HALO], segs[:HALO]]).astype(BF), ((0, HALO - 2), (0, width - HALO)))]
    )
    from_left = neighbour(to_right, "seq", 1)
    from_right = neighbour(to_left, "seq", -1)

    hi, lo, q_rows = pl.pallas_call(
        tap_kernel,
        out_shape=(shape((taps, vocab, width), BF), shape((taps, vocab, width), BF), shape((16, width), BF)),
        grid=(taps,),
        in_specs=[
            pl.BlockSpec((vocab, width), lambda k: (0, 0)),
            pl.BlockSpec((1, width, width), lambda k: (k, 0, 0)),
            pl.BlockSpec((1, width), lambda k: (0, 0)),
        ],
        out_specs=(
            pl.BlockSpec((1, vocab, width), lambda k: (k, 0, 0)),
            pl.BlockSpec((1, vocab, width), lambda k: (k, 0, 0)),
            pl.BlockSpec((16, width), lambda k: (0, 0)),
        ),
        name="taps",
        compiler_params=pltpu.CompilerParams(vmem_limit_bytes=VMEM_LIMIT),
    )(embed_table, conv_weight, scorer[None])

    start = lax.axis_index("seq") * span
    near_left = from_left.astype(F32)
    near_right = from_right[HALO : HALO + 2, :HALO].astype(F32)
    line_ids = jnp.concatenate([near_left[0], ids, near_right[0]])
    line_segs = jnp.concatenate([near_left[1], segs, near_right[1]])
    line_pos = start - HALO + jnp.arange(span + 2 * HALO, dtype=jnp.int32)
    real = (line_pos >= 0) & (line_pos < row_len[0])
    known = jnp.where(real, line_ids, -1.0)
    padded = jnp.concatenate([jnp.full((taps - 1,), -1.0, F32), known])
    shifted = [padded[k : k + span + 2 * HALO] for k in range(taps)]
    idk = jnp.stack([jnp.concatenate([s[HALO:], s[:HALO]]) for s in shifted] + [jnp.zeros((span + 2 * HALO,), F32)] * (8 - taps), axis=1)
    idt = jnp.stack([s[HALO : HALO + span] for s in shifted]).astype(BF).reshape(2 * taps, span // 2)
    idt = jnp.pad(idt, ((0, 16 - 2 * taps), (0, 0)))
    lanes = span + 128
    gap = jnp.zeros((lanes - span - 2 * HALO,), F32)

    def lane_row(v):
        return jnp.concatenate([v[HALO:], gap, v[:HALO]])

    lane = jnp.stack([lane_row(line_segs), lane_row(real.astype(F32))] + [jnp.zeros((lanes,), F32)] * 6)

    blocks, keep, send, ext = call(
        local_kernel,
        (
            shape((span // 2, width), BF),
            shape((span, half), BF),
            shape((span + 48, half), BF),
            shape((16, half), F32),
        ),
        "local",
        in_specs=[sspec(), sspec()] + [vspec()] * 9,
        out_specs=(vspec(),) * 4,
        scratch_shapes=[
            pltpu.VMEM((lanes, width), BF),
            pltpu.VMEM((span // 2 + 2 * HALO, width), BF),
            pltpu.VMEM((taps, span + 2 * HALO, vocab), BF),
        ],
    )(info, calibration, idk, lane, idt, hi, lo, conv_bias[None], cot, from_right[:HALO], q_rows)

    got = swap(send, 1, count)
    a_keep, a_send, b_keep, b_send, ext = call(
        table_kernel,
        (
            shape((taps, quarter, half), F32),
            shape((taps * quarter + 32, half), BF),
            shape((taps, quarter, half), F32),
            shape((taps * quarter, half), BF),
            shape((16, half), F32),
        ),
        "by_value",
        in_specs=[sspec()] + [vspec()] * 4,
        out_specs=(vspec(),) * 5,
    )(info, keep, idt, got, ext)

    a_got, b_got = swap(a_send, 2, count), swap(b_send, 4, count)
    eighth = quarter // 2
    a_keep, a_send, b_keep, b_send, ext = call(
        second_kernel,
        (
            shape((taps, eighth, half), F32),
            shape((taps * eighth + 32, half), BF),
            shape((taps, eighth, half), F32),
            shape((taps * eighth, half), BF),
            shape((16, half), F32),
        ),
        "second",
        in_specs=[vspec()] * 5,
        out_specs=(vspec(),) * 5,
    )(a_keep, b_keep, a_got, b_got, ext)

    a_got, b_got = swap(a_send, 4, count), swap(b_send, 2, count)
    size = 2 * taps * part
    outs = call(
        third_kernel,
        (shape((size, half), F32), shape((16, half), F32)) + (shape((size + 32, half), BF),) * (depth - 1),
        "third",
        in_specs=[vspec()] * 5,
        out_specs=(vspec(),) * (depth + 1),
    )(a_keep, b_keep, a_got, b_got, ext)
    mine, ext, sends = outs[0], outs[1], outs[2:]
    gots = [swap(s, 8 * (t + 1), count) for t, s in enumerate(sends)]
    shard, small = call(
        shard_kernel,
        (shape((size, half), BF), shape((8, half), F32)),
        "shard",
        in_specs=[sspec()] + [vspec()] * (3 + len(gots)),
        out_specs=(vspec(),) * 2,
    )(shard_info, mine, ext, scorer.reshape(2, half), *gots)

    gathered = [shard] + [swap(shard, 8 * t, count) for t in range(1, depth)]
    ab = jnp.concatenate([g.reshape(2, taps, part, half) for g in gathered], axis=2)
    a_got, b_got = swap(ab[0], 4, count), swap(ab[1], 2, count)
    early = jnp.concatenate([ab, jnp.stack([a_got, b_got])], axis=2)
    a_got, b_got = swap(early[0], 2, count), swap(early[1], 4, count)
    early_far = swap(early, 1, count)
    a_far, b_far = swap(a_got, 1, count), swap(b_got, 1, count)

    table_t = embed_table.T
    conv, table = finish(info, info[0:1], early, a_got, b_got, table_t, conv_weight)
    conv, table = finish(info, info[3:4], early_far, a_far, b_far, table_t, conv_weight, conv, table)
    grad_scorer = small[0:2].reshape(width)
    grad_bias = small[2:4].reshape(width)
    grad_calib = small[4, 0:16].reshape(4, 4)
    loss = small[4, 32]
    return (blocks[None], loss, table, conv, grad_bias, grad_scorer, grad_calib)


def solution(mesh):
    return jax.shard_map(
        body,
        mesh=mesh,
        in_specs=(
            P("rows", "seq"),
            P("rows", "seq"),
            P("rows"),
            P(),
            P(),
            P(),
            P(),
            P(),
            P("rows", "seq", None),
        ),
        out_specs=(P("rows", "seq", None), P(), P(), P(), P(), P(), P()),
        check_vma=False,
    )
```

time: 394 us -> 103 us (0.26)
  waiting for transfers between devices: 178 us -> 29.4 us
  blocking collectives: 63.7 us -> 0 us
  matrix products: 50 us -> 0 us
  local copies, waits for them, and re-layouts: 51.9 us -> 10.9 us
  Pallas kernels: 0 us -> 31.7 us
  between operations: 18.3 us -> 1.56 us
  other arithmetic: 19.5 us -> 2.86 us
  starting transfers between devices: 11.1 us -> 25.6 us
    psum x1 -> x0, waiting for transfers between devices: 176 us -> none  [body(): lax.psum((grad_conv, grad_bias, grad_table, grad_scorer, grad_calib), ('r...]
    psum x2 -> x0, blocking collectives: 63.7 us -> none  [the longest x1 40.6 us: body(): entropy_total = lax.psum(entropy_local, ('rows', 'seq'))]
    dot_general x26 -> x0, matrix products: 50 us -> none  [the longest x4 13.1 us: body(): jnp.einsum('rle,de->rld', dy_low, conv_weight[offset], preferred_element_...]
    pallas_call x0 -> x8, Pallas kernels: none -> 31.7 us  [the longest x2 16.7 us: finish(): pl.pallas_call(kernel, out_shape=(shape((taps, width, width), F32), shape...]
    ppermute x5 -> x20, waiting for transfers between devices: 1.78 us -> 29.4 us  [the longest x18 29.4 us: swap(): return lax.ppermute(shard, AXES, [(i, i ^ flip) for i in range(count)])]
    scatter-add x7 -> x0, local copies, waits for them, and re-layouts: 27.4 us -> none  [the longest x4 16.3 us: body(): dx_ext.at[:, offset:offset + span_len]]
    ppermute x5 -> x20, starting transfers between devices: 11.1 us -> 25.6 us  [the longest x18 21.9 us: swap(): return lax.ppermute(shard, AXES, [(i, i ^ flip) for i in range(count)])]
    reduce_sum x6 -> x0, other arithmetic: 10.8 us -> none  [the longest x1 4.26 us: body(): jnp.sum(mixed.reshape(row_count, span_len // 2, 2, width_dim), axis=2) * 0.5]
  transfers between devices with their start and end apart: 6 -> 20, of which waited for: 2 -> 11; matrix products, arithmetic and copies ran while one was open for 9% -> 7% of each run, Pallas kernels for 0% -> 13%
where the time goes in v1:
time: 103 us; the launch traced here: 102 us
  Pallas kernels  31.7 us (31%)
  waiting for transfers between devices  29.4 us (29%)
  starting transfers between devices  25.6 us (25%)
  local copies, waits for them, and re-layouts  10.9 us (11%)
  other arithmetic  2.86 us (3%)
  between operations  1.56 us (2%)
    ppermute x18, waiting for transfers between devices, swap(): return lax.ppermute(shard, AXES, [(i, i ^ flip) for i in range(count)])  29.4 us
    ppermute x18, starting transfers between devices, swap(): return lax.ppermute(shard, AXES, [(i, i ^ flip) for i in range(count)])  21.9 us
    pallas_call x2, Pallas kernels, finish(): pl.pallas_call(kernel, out_shape=(shape((taps, width, width), F32), shape...  16.7 us
    pallas_call x1, Pallas kernels, body(): call(local_kernel, (shape((span // 2, width), BF), shape((span, half), BF...  6.75 us
    pallas_call x1, Pallas kernels, body(): pl.pallas_call(tap_kernel, out_shape=(shape((taps, vocab, width), BF), sh...  5.39 us
    unnamed x21, local copies, waits for them, and re-layouts  4.04 us
    ppermute x2, starting transfers between devices, neighbour(): lax.ppermute(shard, axis, [(i, i + by) for i in range(length) if 0 <= i +...  3.69 us
    pallas_call x1, Pallas kernels, body(): call(table_kernel, (shape((taps, quarter, half), F32), shape((taps * quar...  2.07 us
  transfers between devices with their start and end apart: 20, of which 11 were waited for; matrix products, arithmetic and copies ran while one was open for 7% of the time, Pallas kernels for 13%

profile of v1, /device:TPU:0, one launch (start us, length us, event | category | flops | bytes accessed | tf_op | source)
XLA Modules:
  0.0 102.0 jit_solution(3918397354595106423)
XLA Ops:
  2.1 2.4 %collective-permute-start = (bf16[2,16]{1,0:T(2,128)(2,1)S(1)}, bf16[2,16]{1,0:T(2,128)(2,1)S(1)}, u32[]{:S(2)}, u32[]{:S(2)}) collective-permute-start(bf16[2,16]{1,0:T(2,128)(2,1)S(1)} %pad_maximum_fusion.9), channel_id=1, source_target_pairs={{0,1},{1,2},{2,3},{4,5},{5,6},{6,7},{8,9},{9,10},{10,11},{12,13},{... | collective-permute-start | bytes 200 | tf_op jit(solution)/shard_map/ppermute | solution.py:401
  5.3 1.3 %collective-permute-start.1 = (bf16[32,768]{1,0:T(8,128)(2,1)S(1)}, bf16[32,768]{1,0:T(8,128)(2,1)S(1)}, u32[]{:S(2)}, u32[]{:S(2)}) collective-permute-start(bf16[32,768]{1,0:T(8,128)(2,1)S(1)} %pad_maximum_fusion.1), channel_id=1, source_target_pairs={{1,0},{2,1},{3,2},{5,4},{6,5},{7,6},{9,8},{10,9},{11,10},{13,12},{... | collective-permute-start | bytes 147464 | tf_op jit(solution)/shard_map/ppermute | solution.py:401
  9.6 1.0 copy-done.2
  10.6 5.4 %taps.1 = (bf16[5,256,768]{2,1,0:T(8,128)(2,1)S(1)}, bf16[5,256,768]{2,1,0:T(8,128)(2,1)S(1)}, bf16[16,768]{1,0:T(8,128)(2,1)S(1)}) custom-call(bf16[256,768]{1,0:T(8,128)(2,1)S(1)} %copy-done.2, bf16[5,768,768]{2,1,0:T(8,128)(2,1)} %weight_ref.3, f32[1,768]{1,0:T(1,128)S(1)} %broadcast_in_dim.18.scorer_ref), custom_call_target="tpu_custom_call" | custom-call | tf_op jit(solution)/shard_map/taps/pallas_call | solution.py:441
  16.0 1.3 %copy-done = bf16[5,256,768]{2,1,0:T(8,128)(2,1)} copy-done((bf16[5,256,768]{2,1,0:T(8,128)(2,1)}, bf16[5,256,768]{2,1,0:T(8,128)(2,1)S(1)}, u32[]{:S(2)}) %copy-start) | copy-done | bytes 1966104
  18.6 1.5 %copy-done.1 = bf16[5,256,768]{2,1,0:T(8,128)(2,1)S(1)} copy-done((bf16[5,256,768]{2,1,0:T(8,128)(2,1)S(1)}, bf16[5,256,768]{2,1,0:T(8,128)(2,1)}, u32[]{:S(2)}) %copy-start.1) | copy-done | bytes 1966104
  20.1 6.8 %local.1 = (bf16[256,768]{1,0:T(8,128)(2,1)}, bf16[512,384]{1,0:T(8,128)(2,1)S(1)}, bf16[560,384]{1,0:T(8,128)(2,1)S(1)}, f32[16,384]{1,0:T(8,128)S(1)}) custom-call(s32[4]{0:T(128)S(1)} %get-tuple-element.68.info_ref, f32[4,4]{1,0:T(4,128)S(1)} %copy-done.5, f32[544,8]{1,0:T(8,128)S(1)} %copy.26.idk_ref, f32[8,640]{1,0:T(8,128)S(1)} %maximum_maximum_fusion.lane_ref, ...), custom_call_target="tpu_custom_call" | custom-call | tf_op jit(solution)/shard_map/local/pallas_call | solution.py:480
  26.9 3.3 %collective-permute-start.2 = (bf16[560,384]{1,0:T(8,128)(2,1)S(1)}, bf16[560,384]{1,0:T(8,128)(2,1)S(1)}, u32[]{:S(2)}, u32[]{:S(2)}) collective-permute-start(bf16[560,384]{1,0:T(8,128)(2,1)S(1)} %get-tuple-element.40), channel_id=1, source_target_pairs={{0,1},{1,0},{2,3},{3,2},{4,5},{5,4},{6,7},{7,6},{8,9},{9,8},{10,11... | collective-permute-start | bytes 1290248 | tf_op jit(solution)/shard_map/ppermute | solution.py:405
  30.2 1.4 %collective-permute-done.2.got_ref = bf16[560,384]{1,0:T(8,128)(2,1)S(1)} collective-permute-done((bf16[560,384]{1,0:T(8,128)(2,1)S(1)}, bf16[560,384]{1,0:T(8,128)(2,1)S(1)}, u32[]{:S(2)}, u32[]{:S(2)}) %collective-permute-start.2) | collective-permute-done | bytes 430112 | tf_op jit(solution)/shard_map/ppermute | solution.py:405
  31.6 2.1 %by_value.1 = (f32[5,64,384]{2,1,0:T(8,128)S(1)}, bf16[352,384]{1,0:T(8,128)(2,1)S(1)}, f32[5,64,384]{2,1,0:T(8,128)S(1)}, bf16[320,384]{1,0:T(8,128)(2,1)S(1)}, f32[16,384]{1,0:T(8,128)S(1)}) custom-call(s32[4]{0:T(128)S(1)} %get-tuple-element.68.info_ref, bf16[512,384]{1,0:T(8,128)(2,1)S(1)} %get-tuple-element.39.keep_ref, ...), custom_call_target="tpu_custom_call" | custom-call | tf_op jit(solution)/shard_map/by_value/pallas_call | solution.py:499
  33.6 2.1 %collective-permute-start.3 = (bf16[352,384]{1,0:T(8,128)(2,1)S(1)}, bf16[352,384]{1,0:T(8,128)(2,1)S(1)}, u32[]{:S(2)}, u32[]{:S(2)}) collective-permute-start(bf16[352,384]{1,0:T(8,128)(2,1)S(1)} %get-tuple-element.44), channel_id=1, source_target_pairs={{0,2},{1,3},{2,0},{3,1},{4,6},{5,7},{6,4},{7,5},{8,10},{9,11},{10,... | collective-permute-start | bytes 811016 | tf_op jit(solution)/shard_map/ppermute | solution.py:405
  35.7 1.5 %collective-permute-start.4 = (bf16[320,384]{1,0:T(8,128)(2,1)S(1)}, bf16[320,384]{1,0:T(8,128)(2,1)S(1)}, u32[]{:S(2)}, u32[]{:S(2)}) collective-permute-start(bf16[320,384]{1,0:T(8,128)(2,1)S(1)} %get-tuple-element.45), channel_id=1, source_target_pairs={{0,4},{1,5},{2,6},{3,7},{4,0},{5,1},{6,2},{7,3},{8,12},{9,13},{10,... | collective-permute-start | bytes 737288 | tf_op jit(solution)/shard_map/ppermute | solution.py:405
  37.2 6.2 %collective-permute-done.4.b_got = bf16[320,384]{1,0:T(8,128)(2,1)S(1)} collective-permute-done((bf16[320,384]{1,0:T(8,128)(2,1)S(1)}, bf16[320,384]{1,0:T(8,128)(2,1)S(1)}, u32[]{:S(2)}, u32[]{:S(2)}) %collective-permute-start.4) | collective-permute-done | bytes 245792 | tf_op jit(solution)/shard_map/ppermute | solution.py:405
  43.5 1.6 %collective-permute-start.5 = (bf16[192,384]{1,0:T(8,128)(2,1)S(1)}, bf16[192,384]{1,0:T(8,128)(2,1)S(1)}, u32[]{:S(2)}, u32[]{:S(2)}) collective-permute-start(bf16[192,384]{1,0:T(8,128)(2,1)S(1)} %get-tuple-element.49), channel_id=1, source_target_pairs={{0,4},{1,5},{2,6},{3,7},{4,0},{5,1},{6,2},{7,3},{8,12},{9,13},{10,... | collective-permute-start | bytes 442376 | tf_op jit(solution)/shard_map/ppermute | solution.py:405
  45.1 0.8 collective-permute-start.6
  45.9 4.1 %collective-permute-done.6.b_got = bf16[160,384]{1,0:T(8,128)(2,1)S(1)} collective-permute-done((bf16[160,384]{1,0:T(8,128)(2,1)S(1)}, bf16[160,384]{1,0:T(8,128)(2,1)S(1)}, u32[]{:S(2)}, u32[]{:S(2)}) %collective-permute-start.6) | collective-permute-done | bytes 122912 | tf_op jit(solution)/shard_map/ppermute | solution.py:405
  50.1 1.6 %collective-permute-start.7 = (bf16[112,384]{1,0:T(8,128)(2,1)S(1)}, bf16[112,384]{1,0:T(8,128)(2,1)S(1)}, u32[]{:S(2)}, u32[]{:S(2)}) collective-permute-start(bf16[112,384]{1,0:T(8,128)(2,1)S(1)} %get-tuple-element.54), channel_id=1, source_target_pairs={{0,8},{1,9},{2,10},{3,11},{4,12},{5,13},{6,14},{7,15},{8,0},{9,1},... | collective-permute-start | bytes 258056 | tf_op jit(solution)/shard_map/ppermute | solution.py:405
  51.7 2.6 %collective-permute-start.8 = (bf16[112,384]{1,0:T(8,128)(2,1)S(1)}, bf16[112,384]{1,0:T(8,128)(2,1)S(1)}, u32[]{:S(2)}, u32[]{:S(2)}) collective-permute-start(bf16[112,384]{1,0:T(8,128)(2,1)S(1)} %get-tuple-element.55), channel_id=1, source_target_pairs={{0,16},{1,17},{2,18},{3,19},{4,20},{5,21},{6,22},{7,23},{8,24},{9,... | collective-permute-start | bytes 258056 | tf_op jit(solution)/shard_map/ppermute | solution.py:405
  55.2 3.6 %collective-permute-done.8.refs_1_ = bf16[112,384]{1,0:T(8,128)(2,1)S(1)} collective-permute-done((bf16[112,384]{1,0:T(8,128)(2,1)S(1)}, bf16[112,384]{1,0:T(8,128)(2,1)S(1)}, u32[]{:S(2)}, u32[]{:S(2)}) %collective-permute-start.8) | collective-permute-done | bytes 86048 | tf_op jit(solution)/shard_map/ppermute | solution.py:405
  58.8 1.8 %collective-permute-done.9.refs_2_ = bf16[112,384]{1,0:T(8,128)(2,1)S(1)} collective-permute-done((bf16[112,384]{1,0:T(8,128)(2,1)S(1)}, bf16[112,384]{1,0:T(8,128)(2,1)S(1)}, u32[]{:S(2)}, u32[]{:S(2)}) %collective-permute-start.9) | collective-permute-done | bytes 86048 | tf_op jit(solution)/shard_map/ppermute | solution.py:405
  61.3 1.1 %collective-permute-start.12 = (bf16[80,384]{1,0:T(8,128)(2,1)S(1)}, bf16[80,384]{1,0:T(8,128)(2,1)S(1)}, u32[]{:S(2)}, u32[]{:S(2)}) collective-permute-start(bf16[80,384]{1,0:T(8,128)(2,1)S(1)} %get-tuple-element.58), channel_id=1, source_target_pairs={{0,24},{1,25},{2,26},{3,27},{4,28},{5,29},{6,30},{7,31},{8,16},{9,... | collective-permute-start | bytes 184328 | tf_op jit(solution)/shard_map/ppermute | solution.py:405
  62.4 1.2 %collective-permute-start.11 = (bf16[80,384]{1,0:T(8,128)(2,1)S(1)}, bf16[80,384]{1,0:T(8,128)(2,1)S(1)}, u32[]{:S(2)}, u32[]{:S(2)}) collective-permute-start(bf16[80,384]{1,0:T(8,128)(2,1)S(1)} %get-tuple-element.58), channel_id=1, source_target_pairs={{0,16},{1,17},{2,18},{3,19},{4,20},{5,21},{6,22},{7,23},{8,24},{9,... | collective-permute-start | bytes 184328 | tf_op jit(solution)/shard_map/ppermute | solution.py:405
  63.6 2.1 %collective-permute-start.10 = (bf16[80,384]{1,0:T(8,128)(2,1)S(1)}, bf16[80,384]{1,0:T(8,128)(2,1)S(1)}, u32[]{:S(2)}, u32[]{:S(2)}) collective-permute-start(bf16[80,384]{1,0:T(8,128)(2,1)S(1)} %get-tuple-element.58), channel_id=1, source_target_pairs={{0,8},{1,9},{2,10},{3,11},{4,12},{5,13},{6,14},{7,15},{8,0},{9,1},... | collective-permute-start | bytes 184328 | tf_op jit(solution)/shard_map/ppermute | solution.py:405
  65.8 1.7 %collective-permute-done.12 = bf16[80,384]{1,0:T(8,128)(2,1)S(1)} collective-permute-done((bf16[80,384]{1,0:T(8,128)(2,1)S(1)}, bf16[80,384]{1,0:T(8,128)(2,1)S(1)}, u32[]{:S(2)}, u32[]{:S(2)}) %collective-permute-start.12) | collective-permute-done | bytes 61472 | tf_op jit(solution)/shard_map/ppermute | solution.py:405
  67.5 1.3 %collective-permute-done.11 = bf16[80,384]{1,0:T(8,128)(2,1)S(1)} collective-permute-done((bf16[80,384]{1,0:T(8,128)(2,1)S(1)}, bf16[80,384]{1,0:T(8,128)(2,1)S(1)}, u32[]{:S(2)}, u32[]{:S(2)}) %collective-permute-start.11) | collective-permute-done | bytes 61472 | tf_op jit(solution)/shard_map/ppermute | solution.py:405
  69.4 0.8 collective-permute-start.14
  70.2 4.8 %collective-permute-done.13 = bf16[5,32,384]{2,1,0:T(8,128)(2,1)S(1)} collective-permute-done((bf16[5,32,384]{2,1,0:T(8,128)(2,1)S(1)}, bf16[5,32,384]{2,1,0:T(8,128)(2,1)S(1)}, u32[]{:S(2)}, u32[]{:S(2)}) %collective-permute-start.13) | collective-permute-done | bytes 122912 | tf_op jit(solution)/shard_map/ppermute | solution.py:405
  75.7 1.6 %collective-permute-start.18 = (bf16[5,64,384]{2,1,0:T(8,128)(2,1)S(1)}, bf16[5,64,384]{2,1,0:T(8,128)(2,1)S(1)}, u32[]{:S(2)}, u32[]{:S(2)}) collective-permute-start(bf16[5,64,384]{2,1,0:T(8,128)(2,1)S(1)} %get-tuple-element.63), channel_id=1, source_target_pairs={{0,4},{1,5},{2,6},{3,7},{4,0},{5,1},{6,2},{7,3},{8,12},{9,13},{10,... | collective-permute-start | bytes 737288 | tf_op jit(solution)/shard_map/ppermute | solution.py:405
  79.5 2.5 %collective-permute-done.18.b = bf16[5,64,384]{2,1,0:T(8,128)(2,1)S(1)} collective-permute-done((bf16[5,64,384]{2,1,0:T(8,128)(2,1)S(1)}, bf16[5,64,384]{2,1,0:T(8,128)(2,1)S(1)}, u32[]{:S(2)}, u32[]{:S(2)}) %collective-permute-start.18) | collective-permute-done | bytes 245792 | tf_op jit(solution)/shard_map/ppermute | solution.py:405
  82.0 1.5 %collective-permute-done.16.a = bf16[5,64,384]{2,1,0:T(8,128)(2,1)S(1)} collective-permute-done((bf16[5,64,384]{2,1,0:T(8,128)(2,1)S(1)}, bf16[5,64,384]{2,1,0:T(8,128)(2,1)S(1)}, u32[]{:S(2)}, u32[]{:S(2)}) %collective-permute-start.16) | collective-permute-done | bytes 245792 | tf_op jit(solution)/shard_map/ppermute | solution.py:405
  85.4 8.2 %finish_first.1 = (f32[5,768,768]{2,1,0:T(8,128)}, f32[256,768]{1,0:T(8,128)S(1)}) custom-call(s32[4]{0:T(128)S(1)} %get-tuple-element.68.info_ref, s32[1]{0:T(128)} %bitcast.24.col_ref, bf16[2,5,64,384]{3,2,1,0:T(8,128)(2,1)S(1)} %maximum_dynamic-update-slice_fusion.e, bf16[5,64,384]{2,1,0:T(8,128)(2,1)S(1)} %collective-permute-done.16.a, ...), custom_call_target="tpu_custom_call" | custom-call | tf_op jit(solution)/shard_map/finish_first/pallas_call | solution.py:380
  93.6 8.4 %finish_second.1 = (f32[5,768,768]{2,1,0:T(8,128)}, f32[256,768]{1,0:T(8,128)}) custom-call(s32[4]{0:T(128)S(1)} %get-tuple-element.68.info_ref, s32[1]{0:T(128)} %bitcast.12.col_ref, bf16[2,5,64,384]{3,2,1,0:T(8,128)(2,1)S(1)} %collective-permute-done.15.early_ref, ...), custom_call_target="tpu_custom_call", output_to_operand_aliasing={{0}: (7, {})} | custom-call | tf_op jit(solution)/shard_map/finish_second/pallas_call | solution.py:380
  (104 shorter events, 12.9 us)
Async XLA Ops:
  0.6 17.9 %copy-start.5 = (f32[4,4]{1,0:T(4,128)S(1)}, f32[4,4]{1,0:T(4,128)}, u32[]{:S(2)}) copy-start(f32[4,4]{1,0:T(4,128)} %calib_ref.1) | copy-start | bytes 196
  2.1 15.1 %collective-permute-start = (bf16[2,16]{1,0:T(2,128)(2,1)S(1)}, bf16[2,16]{1,0:T(2,128)(2,1)S(1)}, u32[]{:S(2)}, u32[]{:S(2)}) collective-permute-start(bf16[2,16]{1,0:T(2,128)(2,1)S(1)} %pad_maximum_fusion.9), channel_id=1, source_target_pairs={{0,1},{1,2},{2,3},{4,5},{5,6},{6,7},{8,9},{9,10},{10,11},{12,13},{... | collective-permute-start | bytes 200 | tf_op jit(solution)/shard_map/ppermute | solution.py:401
  5.3 12.0 %collective-permute-start.1 = (bf16[32,768]{1,0:T(8,128)(2,1)S(1)}, bf16[32,768]{1,0:T(8,128)(2,1)S(1)}, u32[]{:S(2)}, u32[]{:S(2)}) collective-permute-start(bf16[32,768]{1,0:T(8,128)(2,1)S(1)} %pad_maximum_fusion.1), channel_id=1, source_target_pairs={{1,0},{2,1},{3,2},{5,4},{6,5},{7,6},{9,8},{10,9},{11,10},{13,12},{... | collective-permute-start | bytes 147464 | tf_op jit(solution)/shard_map/ppermute | solution.py:401
  9.6 1.0 copy-start.2
  10.6 8.0 %copy-start.4 = (bf16[1,256,768]{2,1,0:T(8,128)(2,1)S(1)}, bf16[1,256,768]{2,1,0:T(8,128)(2,1)}, u32[]{:S(2)}) copy-start(bf16[1,256,768]{2,1,0:T(8,128)(2,1)} %param.19) | copy-start | bytes 1179652
  10.6 44.0 %copy-start.7 = (s32[4]{0:T(128)S(1)}, s32[4]{0:T(128)}, u32[]{:S(2)}) copy-start(s32[4]{0:T(128)} %constant.37.clone) | copy-start | bytes 52
  10.6 44.7 %copy-start.6 = (f32[768]{0:T(1024)S(1)}, f32[768]{0:T(1024)}, u32[]{:S(2)}) copy-start(f32[768]{0:T(1024)} %param.17) | copy-start | bytes 9220
  16.0 1.3 %copy-start = (bf16[5,256,768]{2,1,0:T(8,128)(2,1)}, bf16[5,256,768]{2,1,0:T(8,128)(2,1)S(1)}, u32[]{:S(2)}) copy-start(bf16[5,256,768]{2,1,0:T(8,128)(2,1)S(1)} %get-tuple-element.36.lo_ref) | copy-start | bytes 5898244
  18.0 60.1 %copy-start.3 = (bf16[256,768]{1,0:T(8,128)(2,1)S(1)}, bf16[256,768]{1,0:T(8,128)(2,1)}, u32[]{:S(2)}) copy-start(bf16[256,768]{1,0:T(8,128)(2,1)} %table_ref.1) | copy-start | bytes 1179652
  18.6 1.5 %copy-start.1 = (bf16[5,256,768]{2,1,0:T(8,128)(2,1)S(1)}, bf16[5,256,768]{2,1,0:T(8,128)(2,1)}, u32[]{:S(2)}) copy-start(bf16[5,256,768]{2,1,0:T(8,128)(2,1)} %copy-done) | copy-start | bytes 5898244
  26.9 4.7 %collective-permute-start.2 = (bf16[560,384]{1,0:T(8,128)(2,1)S(1)}, bf16[560,384]{1,0:T(8,128)(2,1)S(1)}, u32[]{:S(2)}, u32[]{:S(2)}) collective-permute-start(bf16[560,384]{1,0:T(8,128)(2,1)S(1)} %get-tuple-element.40), channel_id=1, source_target_pairs={{0,1},{1,0},{2,3},{3,2},{4,5},{5,4},{6,7},{7,6},{8,9},{9,8},{10,11... | collective-permute-start | bytes 1290248 | tf_op jit(solution)/shard_map/ppermute | solution.py:405
  33.6 9.8 %collective-permute-start.3 = (bf16[352,384]{1,0:T(8,128)(2,1)S(1)}, bf16[352,384]{1,0:T(8,128)(2,1)S(1)}, u32[]{:S(2)}, u32[]{:S(2)}) collective-permute-start(bf16[352,384]{1,0:T(8,128)(2,1)S(1)} %get-tuple-element.44), channel_id=1, source_target_pairs={{0,2},{1,3},{2,0},{3,1},{4,6},{5,7},{6,4},{7,5},{8,10},{9,11},{10,... | collective-permute-start | bytes 811016 | tf_op jit(solution)/shard_map/ppermute | solution.py:405
  35.7 7.7 %collective-permute-start.4 = (bf16[320,384]{1,0:T(8,128)(2,1)S(1)}, bf16[320,384]{1,0:T(8,128)(2,1)S(1)}, u32[]{:S(2)}, u32[]{:S(2)}) collective-permute-start(bf16[320,384]{1,0:T(8,128)(2,1)S(1)} %get-tuple-element.45), channel_id=1, source_target_pairs={{0,4},{1,5},{2,6},{3,7},{4,0},{5,1},{6,2},{7,3},{8,12},{9,13},{10,... | collective-permute-start | bytes 737288 | tf_op jit(solution)/shard_map/ppermute | solution.py:405
  43.5 6.5 %collective-permute-start.5 = (bf16[192,384]{1,0:T(8,128)(2,1)S(1)}, bf16[192,384]{1,0:T(8,128)(2,1)S(1)}, u32[]{:S(2)}, u32[]{:S(2)}) collective-permute-start(bf16[192,384]{1,0:T(8,128)(2,1)S(1)} %get-tuple-element.49), channel_id=1, source_target_pairs={{0,4},{1,5},{2,6},{3,7},{4,0},{5,1},{6,2},{7,3},{8,12},{9,13},{10,... | collective-permute-start | bytes 442376 | tf_op jit(solution)/shard_map/ppermute | solution.py:405
  45.1 4.9 %collective-permute-start.6 = (bf16[160,384]{1,0:T(8,128)(2,1)S(1)}, bf16[160,384]{1,0:T(8,128)(2,1)S(1)}, u32[]{:S(2)}, u32[]{:S(2)}) collective-permute-start(bf16[160,384]{1,0:T(8,128)(2,1)S(1)} %get-tuple-element.50), channel_id=1, source_target_pairs={{0,2},{1,3},{2,0},{3,1},{4,6},{5,7},{6,4},{7,5},{8,10},{9,11},{10,... | collective-permute-start | bytes 368648 | tf_op jit(solution)/shard_map/ppermute | solution.py:405
  50.1 5.2 %collective-permute-start.7 = (bf16[112,384]{1,0:T(8,128)(2,1)S(1)}, bf16[112,384]{1,0:T(8,128)(2,1)S(1)}, u32[]{:S(2)}, u32[]{:S(2)}) collective-permute-start(bf16[112,384]{1,0:T(8,128)(2,1)S(1)} %get-tuple-element.54), channel_id=1, source_target_pairs={{0,8},{1,9},{2,10},{3,11},{4,12},{5,13},{6,14},{7,15},{8,0},{9,1},... | collective-permute-start | bytes 258056 | tf_op jit(solution)/shard_map/ppermute | solution.py:405
  51.7 7.1 %collective-permute-start.8 = (bf16[112,384]{1,0:T(8,128)(2,1)S(1)}, bf16[112,384]{1,0:T(8,128)(2,1)S(1)}, u32[]{:S(2)}, u32[]{:S(2)}) collective-permute-start(bf16[112,384]{1,0:T(8,128)(2,1)S(1)} %get-tuple-element.55), channel_id=1, source_target_pairs={{0,16},{1,17},{2,18},{3,19},{4,20},{5,21},{6,22},{7,23},{8,24},{9,... | collective-permute-start | bytes 258056 | tf_op jit(solution)/shard_map/ppermute | solution.py:405
  54.3 6.4 %collective-permute-start.9 = (bf16[112,384]{1,0:T(8,128)(2,1)S(1)}, bf16[112,384]{1,0:T(8,128)(2,1)S(1)}, u32[]{:S(2)}, u32[]{:S(2)}) collective-permute-start(bf16[112,384]{1,0:T(8,128)(2,1)S(1)} %get-tuple-element.56), channel_id=1, source_target_pairs={{0,24},{1,25},{2,26},{3,27},{4,28},{5,29},{6,30},{7,31},{8,16},{9,... | collective-permute-start | bytes 258056 | tf_op jit(solution)/shard_map/ppermute | solution.py:405
  61.3 6.2 %collective-permute-start.12 = (bf16[80,384]{1,0:T(8,128)(2,1)S(1)}, bf16[80,384]{1,0:T(8,128)(2,1)S(1)}, u32[]{:S(2)}, u32[]{:S(2)}) collective-permute-start(bf16[80,384]{1,0:T(8,128)(2,1)S(1)} %get-tuple-element.58), channel_id=1, source_target_pairs={{0,24},{1,25},{2,26},{3,27},{4,28},{5,29},{6,30},{7,31},{8,16},{9,... | collective-permute-start | bytes 184328 | tf_op jit(solution)/shard_map/ppermute | solution.py:405
  62.4 6.3 %collective-permute-start.11 = (bf16[80,384]{1,0:T(8,128)(2,1)S(1)}, bf16[80,384]{1,0:T(8,128)(2,1)S(1)}, u32[]{:S(2)}, u32[]{:S(2)}) collective-permute-start(bf16[80,384]{1,0:T(8,128)(2,1)S(1)} %get-tuple-element.58), channel_id=1, source_target_pairs={{0,16},{1,17},{2,18},{3,19},{4,20},{5,21},{6,22},{7,23},{8,24},{9,... | collective-permute-start | bytes 184328 | tf_op jit(solution)/shard_map/ppermute | solution.py:405
  63.6 5.1 %collective-permute-start.10 = (bf16[80,384]{1,0:T(8,128)(2,1)S(1)}, bf16[80,384]{1,0:T(8,128)(2,1)S(1)}, u32[]{:S(2)}, u32[]{:S(2)}) collective-permute-start(bf16[80,384]{1,0:T(8,128)(2,1)S(1)} %get-tuple-element.58), channel_id=1, source_target_pairs={{0,8},{1,9},{2,10},{3,11},{4,12},{5,13},{6,14},{7,15},{8,0},{9,1},... | collective-permute-start | bytes 184328 | tf_op jit(solution)/shard_map/ppermute | solution.py:405
  68.8 6.3 %collective-permute-start.13 = (bf16[5,32,384]{2,1,0:T(8,128)(2,1)S(1)}, bf16[5,32,384]{2,1,0:T(8,128)(2,1)S(1)}, u32[]{:S(2)}, u32[]{:S(2)}) collective-permute-start(bf16[5,32,384]{2,1,0:T(8,128)(2,1)S(1)} %get-tuple-element.65), channel_id=1, source_target_pairs={{0,4},{1,5},{2,6},{3,7},{4,0},{5,1},{6,2},{7,3},{8,12},{9,13},{10,... | collective-permute-start | bytes 368648 | tf_op jit(solution)/shard_map/ppermute | solution.py:405
  69.4 6.2 %collective-permute-start.14 = (bf16[5,32,384]{2,1,0:T(8,128)(2,1)S(1)}, bf16[5,32,384]{2,1,0:T(8,128)(2,1)S(1)}, u32[]{:S(2)}, u32[]{:S(2)}) collective-permute-start(bf16[5,32,384]{2,1,0:T(8,128)(2,1)S(1)} %get-tuple-element.66), channel_id=1, source_target_pairs={{0,2},{1,3},{2,0},{3,1},{4,6},{5,7},{6,4},{7,5},{8,10},{9,11},{10,... | collective-permute-start | bytes 368648 | tf_op jit(solution)/shard_map/ppermute | solution.py:405
  75.7 6.3 %collective-permute-start.18 = (bf16[5,64,384]{2,1,0:T(8,128)(2,1)S(1)}, bf16[5,64,384]{2,1,0:T(8,128)(2,1)S(1)}, u32[]{:S(2)}, u32[]{:S(2)}) collective-permute-start(bf16[5,64,384]{2,1,0:T(8,128)(2,1)S(1)} %get-tuple-element.63), channel_id=1, source_target_pairs={{0,4},{1,5},{2,6},{3,7},{4,0},{5,1},{6,2},{7,3},{8,12},{9,13},{10,... | collective-permute-start | bytes 737288 | tf_op jit(solution)/shard_map/ppermute | solution.py:405
  77.3 6.2 %collective-permute-start.16 = (bf16[5,64,384]{2,1,0:T(8,128)(2,1)S(1)}, bf16[5,64,384]{2,1,0:T(8,128)(2,1)S(1)}, u32[]{:S(2)}, u32[]{:S(2)}) collective-permute-start(bf16[5,64,384]{2,1,0:T(8,128)(2,1)S(1)} %get-tuple-element.64), channel_id=1, source_target_pairs={{0,2},{1,3},{2,0},{3,1},{4,6},{5,7},{6,4},{7,5},{8,10},{9,11},{10,... | collective-permute-start | bytes 737288 | tf_op jit(solution)/shard_map/ppermute | solution.py:405
  78.1 15.5 %collective-permute-start.15 = (bf16[2,5,64,384]{3,2,1,0:T(8,128)(2,1)S(1)}, bf16[2,5,64,384]{3,2,1,0:T(8,128)(2,1)S(1)}, u32[]{:S(2)}, u32[]{:S(2)}) collective-permute-start(bf16[2,5,64,384]{3,2,1,0:T(8,128)(2,1)S(1)} %maximum_dynamic-update-slice_fusion.e), channel_id=1, source_target_pairs={{0,1},{1,0},{2,3},{3,2},{4,5},{5,4},{6,7},{7,6},{8,9},{9,8},{10,11... | collective-permute-start | bytes 1474568 | tf_op jit(solution)/shard_map/ppermute | solution.py:405
  82.0 11.6 %collective-permute-start.19 = (bf16[5,64,384]{2,1,0:T(8,128)(2,1)S(1)}, bf16[5,64,384]{2,1,0:T(8,128)(2,1)S(1)}, u32[]{:S(2)}, u32[]{:S(2)}) collective-permute-start(bf16[5,64,384]{2,1,0:T(8,128)(2,1)S(1)} %collective-permute-done.18.b), channel_id=1, source_target_pairs={{0,1},{1,0},{2,3},{3,2},{4,5},{5,4},{6,7},{7,6},{8,9},{9,8},{10,11... | collective-permute-start | bytes 737288 | tf_op jit(solution)/shard_map/ppermute | solution.py:405
  83.5 10.1 %collective-permute-start.17 = (bf16[5,64,384]{2,1,0:T(8,128)(2,1)S(1)}, bf16[5,64,384]{2,1,0:T(8,128)(2,1)S(1)}, u32[]{:S(2)}, u32[]{:S(2)}) collective-permute-start(bf16[5,64,384]{2,1,0:T(8,128)(2,1)S(1)} %collective-permute-done.16.a), channel_id=1, source_target_pairs={{0,1},{1,0},{2,3},{3,2},{4,5},{5,4},{6,7},{7,6},{8,9},{9,8},{10,11... | collective-permute-start | bytes 737288 | tf_op jit(solution)/shard_map/ppermute | solution.py:405

commit v2 on v1

v2 whole, which is shorter than its diff:
```python
import functools

import jax
import jax.numpy as jnp
from jax import lax
from jax.experimental import pallas as pl
from jax.experimental.pallas import tpu as pltpu
from jax.sharding import PartitionSpec as P

AXES = ("rows", "seq")
BF = jnp.bfloat16
F32 = jnp.float32
HALO = 16
VMEM_LIMIT = 48 * 1024 * 1024


def dot_nn(a, b):
    return lax.dot_general(a, b, (((1,), (0,)), ((), ())), preferred_element_type=F32)


def dot_nt(a, b):
    return lax.dot_general(a, b, (((1,), (1,)), ((), ())), preferred_element_type=F32)


def dot_tn(a, b):
    return lax.dot_general(a, b, (((0,), (0,)), ((), ())), preferred_element_type=F32)


def split2(v):
    hi = v.astype(BF)
    return hi, (v - hi.astype(F32)).astype(BF)


def split3(v):
    hi = v.astype(BF)
    rest = v - hi.astype(F32)
    mid = rest.astype(BF)
    return hi, mid, (rest - mid.astype(F32)).astype(BF)


def call(kernel, outs, name, **kw):
    return pl.pallas_call(
        kernel,
        out_shape=outs,
        name=name,
        compiler_params=pltpu.CompilerParams(vmem_limit_bytes=VMEM_LIMIT),
        **kw,
    )


def vspec():
    return pl.BlockSpec(memory_space=pltpu.VMEM)


def sspec():
    return pl.BlockSpec(memory_space=pltpu.SMEM)


def shape(dims, dtype):
    return jax.ShapeDtypeStruct(dims, dtype)


def place(seq_size, quarter, part):
    device = lax.axis_index("rows") * seq_size + lax.axis_index("seq")
    x_bit = (device >> 1) & 1
    y_bit = (device >> 2) & 1
    rest = (device >> 3) * part
    a_mine = x_bit * quarter + y_bit * (quarter // 2) + rest
    b_mine = y_bit * quarter + x_bit * (quarter // 2) + rest
    return (device & 1) == 1, a_mine, b_mine


def pack_kernel(ids_ref, seg_ref, cot_ref, right_ref, left_ref):
    span = ids_ref.shape[1]
    width = cot_ref.shape[2]
    row = lax.broadcasted_iota(jnp.int32, (HALO, span), 0)
    ids = ids_ref[...].astype(F32)
    segs = seg_ref[...].astype(F32)
    both = jnp.where(row == 0, ids, jnp.where(row == 1, segs, 0.0)).astype(BF)
    right_ref[...] = both
    left_ref[0:HALO] = cot_ref[0]
    left_ref[HALO : 2 * HALO, 0:span] = both
    left_ref[HALO : 2 * HALO, span:width] = jnp.zeros((HALO, width - span), BF)


def tap_kernel(table_ref, weight_ref, scorer_ref, hi_ref, lo_ref, q_ref):
    hi, lo = split2(dot_nn(table_ref[...], weight_ref[0]))
    hi_ref[...] = hi
    lo_ref[...] = lo

    @pl.when(pl.program_id(0) == 0)
    def _():
        s1, s2, s3 = split3(scorer_ref[...].reshape(1, q_ref.shape[1]))
        row = lax.broadcasted_iota(jnp.int32, q_ref.shape, 0)
        pick = jnp.where(row == 0, s1.astype(F32), jnp.where(row == 1, s2.astype(F32), s3.astype(F32)))
        q_ref[...] = jnp.where(row < 3, pick, 0.0).astype(BF)


def roll(v, by):
    by = by % v.shape[1]
    return pltpu.roll(v, by, 1) if by else v


def local_kernel(
    row_len_ref, calib_ref, ids_ref, seg_ref, from_left_ref, from_right_ref, hi_ref, lo_ref, bias_ref, cot_ref,
    q_ref, blocks_ref, keep_ref, send_ref, ext_ref, idt_ref, y_ref, full_q_ref, oh_ref, *, seq_size, taps,
):
    span = keep_ref.shape[0]
    width = hi_ref.shape[1]
    vocab = hi_ref.shape[0] // taps
    half = width // 2
    own_blocks = span // 2
    lanes = y_ref.shape[0]
    sizes = calib_ref.shape[0]
    front = span + HALO
    upper = place(seq_size, 1, 1)[0]
    spare = lax.broadcasted_iota(jnp.int32, (1, lanes - span), 1)

    def line_up(own, at):
        near_right = from_right_ref[HALO : 2 * HALO, 0 : lanes - span].astype(F32)[at : at + 1]
        near_left = from_left_ref[:, 2 * span - lanes : span].astype(F32)[at : at + 1]
        rest = jnp.where(spare < HALO, near_right, jnp.where(spare >= lanes - span - HALO, near_left, 0.0))
        return jnp.concatenate([own.astype(F32), rest], axis=1)

    pos = lax.broadcasted_iota(jnp.int32, (1, lanes), 1)
    own = jnp.where(pos < span, 1.0, 0.0)
    place_in_row = lax.axis_index("seq") * span + jnp.where(pos < front, pos, pos - lanes)
    near = (pos < front) | (pos >= lanes - HALO)
    mask = jnp.where(near & (place_in_row >= 0) & (place_in_row < row_len_ref[0]), 1.0, 0.0)
    seg = line_up(seg_ref[...], 1)
    known = jnp.where(mask > 0.5, line_up(ids_ref[...], 0), -1.0)
    value = lax.broadcasted_iota(jnp.int32, (vocab, 1), 0).astype(F32)
    row16 = lax.broadcasted_iota(jnp.int32, (16, span // 2), 0)
    idt = jnp.zeros((16, span // 2), F32)
    for k in range(taps):
        moved = roll(known, taps - 1 - k)
        oh_ref[k * vocab : (k + 1) * vocab] = jnp.where(moved == value, 1.0, 0.0).astype(BF)
        for i in range(2):
            idt = jnp.where(row16 == 2 * k + i, moved[:, i * (span // 2) : (i + 1) * (span // 2)], idt)
    idt = idt.astype(BF)
    idt_ref[...] = idt
    y = dot_tn(oh_ref[...], hi_ref[...]) + dot_tn(oh_ref[...], lo_ref[...])
    y_ref[...] = (y + bias_ref[...].reshape(1, width)).astype(BF)
    full_q_ref[0:own_blocks] = cot_ref[0]
    full_q_ref[own_blocks : own_blocks + HALO] = from_right_ref[0:HALO]
    full_q_ref[own_blocks + HALO : own_blocks + 2 * HALO] = q_ref[...]
    tail = own_blocks + HALO
    q_rows = own_blocks + 2 * HALO
    dots = dot_nt(full_q_ref[...], y_ref[...])
    u = dots[tail : tail + 1] + dots[tail + 1 : tail + 2] + dots[tail + 2 : tail + 3]

    line = lax.broadcasted_iota(jnp.int32, (q_rows, lanes), 0)
    valid, match, grads = [], [], []
    for d in range(sizes):
        valid.append(mask * roll(mask, d) * jnp.where(seg == roll(seg, d), 1.0, 0.0))
        ahead = jnp.where(pos + d >= lanes, pos + d - lanes, pos + d)
        block = jnp.where(ahead < front, lax.shift_right_logical(ahead, 1), -1)
        match.append(line == block)
        picked = jnp.sum(jnp.where(match[d], dots, 0.0), axis=0, keepdims=True)
        grads.append(0.5 * roll(picked, d))
    counted, inv, scores, dprobs = 0.0, [], [], []
    run_u, run_g = 0.0, 0.0
    for d in range(sizes):
        counted = counted + valid[d]
        inv.append(1.0 / jnp.maximum(counted, 1.0))
        run_u = run_u + valid[d] * roll(u, d)
        run_g = run_g + valid[d] * grads[d]
        scores.append(run_u * inv[d])
        dprobs.append(run_g * inv[d])
    logits = [sum(scores[b] * calib_ref[b, c] for b in range(sizes)) for c in range(sizes)]
    top = logits[0]
    for c in range(1, sizes):
        top = jnp.maximum(top, logits[c])
    powers = [jnp.exp(v - top) for v in logits]
    total = sum(powers)
    probs = [v / total for v in powers]
    lse = top + jnp.log(total)
    mean_logit = sum(p * v for p, v in zip(probs, logits))
    mean_grad = sum(p * v for p, v in zip(probs, dprobs))
    entropy = own * mask * (lse - mean_logit)
    parts = [
        [p * (v - mean_grad) for p, v in zip(probs, dprobs)],
        [mask * p * (v - mean_logit) for p, v in zip(probs, logits)],
    ]
    alpha, later = [None] * sizes, 0.0
    for d in reversed(range(sizes)):
        later = later + probs[d] * inv[d]
        alpha[d] = valid[d] * later
    gammas, rhos, calibs = [], [], []
    for part in parts:
        dscores = [sum(part[c] * calib_ref[b, c] for c in range(sizes)) for b in range(sizes)]
        later, gamma, rho = 0.0, 0.0, 0.0
        for d in reversed(range(sizes)):
            later = later + inv[d] * dscores[d]
            beta = valid[d] * later
            gamma = gamma + roll(beta, -d)
            rho = rho + roll(beta * own, -d)
        gammas.append(gamma)
        rhos.append(rho)
        calibs.append([[jnp.sum(own * scores[b] * part[c], axis=1, keepdims=True) for c in range(sizes)] for b in range(sizes)])
    band = jnp.where((line >= tail) & (line < tail + 3), gammas[0], 0.0)
    for d in range(sizes):
        band = band + jnp.where(match[d], 0.5 * roll(alpha[d], -d), 0.0)
    band_hi, band_lo = split2(band)
    mixed = dot_nn(band_hi[0:own_blocks], y_ref[...]) + dot_nn(band_lo[0:own_blocks], y_ref[...])
    blocks_ref[0] = mixed.astype(BF)
    dy = dot_tn(band_hi[:, 0:span], full_q_ref[...]) + dot_tn(band_lo[:, 0:span], full_q_ref[...])
    dy = dy.astype(BF)
    left, right = dy[:, 0:half], dy[:, half:width]
    keep_ref[...] = jnp.where(upper, right, left)
    send_ref[0:span] = jnp.where(upper, left, right)
    grad_bias = jnp.sum(dy.astype(F32), axis=0, keepdims=True)

    row8 = lax.broadcasted_iota(jnp.int32, (16, lanes), 0)
    stack = jnp.zeros((16, lanes), F32)
    pieces = split3(rhos[0]) + split3(rhos[1]) + split3(gammas[1] * own)
    for i, piece in enumerate(pieces):
        stack = jnp.where(row8 == i, piece.astype(F32), stack)
    stack = stack.astype(BF)
    by_y = dot_nn(stack, y_ref[...])
    grad_scorer = [by_y[3 * i : 3 * i + 1] + by_y[3 * i + 1 : 3 * i + 2] + by_y[3 * i + 2 : 3 * i + 3] for i in range(2)]
    ext_ref[...] = jnp.zeros(ext_ref.shape, F32)
    for i, row in enumerate(grad_scorer + [grad_bias]):
        ext_ref[2 * i : 2 * i + 1] = row[:, 0:half]
        ext_ref[2 * i + 1 : 2 * i + 2] = row[:, half:width]
    by_tap = dot_nt(stack, oh_ref[...])
    by_tap = by_tap[6:7] + by_tap[7:8] + by_tap[8:9]
    for k in range(taps):
        ext_ref[6 + k : 7 + k, 0:vocab] = by_tap[:, k * vocab : (k + 1) * vocab]
    spot = lax.broadcasted_iota(jnp.int32, (1, half), 1)
    misc = jnp.zeros((1, half), F32)
    sums = [calibs[i][b][c] for i in range(2) for b in range(sizes) for c in range(sizes)]
    sums.append(jnp.sum(entropy, axis=1, keepdims=True))
    sums.append(jnp.sum(own * mask, axis=1, keepdims=True))
    sums.append(jnp.sum(own * gammas[1], axis=1, keepdims=True))
    for i, one in enumerate(sums):
        misc = jnp.where(spot == i, one, misc)
    ext_ref[11:12] = misc
    send_ref[span : span + 16] = coded(ext_ref[...])
    send_ref[span + 16 : span + 32] = jnp.concatenate([idt, jnp.zeros((16, half - idt.shape[1]), BF)], axis=1)


def coded(ext):
    hi = ext.astype(BF).astype(F32)
    row = lax.broadcasted_iota(jnp.int32, ext.shape, 0)
    return jnp.where(row == 12, ext[11:12] - hi[11:12], hi).astype(BF)


def decoded(code):
    wide = code.astype(F32)
    row = lax.broadcasted_iota(jnp.int32, wide.shape, 0)
    return wide + jnp.where(row == 11, wide[12:13], 0.0)


def joined(ext_ref):
    return decoded(coded(ext_ref[...]))


def pair(ref, at):
    return decoded(ref[at : at + 16])


def local_value(shape_, dim, a_mine, b_mine, vocab):
    slot = lax.broadcasted_iota(jnp.int32, shape_, dim)
    return jnp.bitwise_xor(slot, jnp.where(slot < vocab // 2, a_mine, b_mine))


def table_kernel(keep_ref, idt_ref, got_ref, ext_ref, a_keep, a_send, b_keep, b_send, ext_out, *, seq_size, part):
    span, half = keep_ref.shape
    taps, quarter, _ = a_keep.shape
    vocab = 4 * quarter
    _, a_mine, b_mine = place(seq_size, quarter, part)
    value = local_value((vocab, 1), 0, a_mine, b_mine, vocab).astype(F32)
    mine = idt_ref[...].astype(F32)
    theirs = got_ref[span + 16 : span + 32].astype(F32)
    wide = mine.shape[1]
    for k in range(taps):
        acc = None
        for i in range(span // wide):
            for ids, grad in ((mine, keep_ref), (theirs, got_ref)):
                row = ids[2 * k + i : 2 * k + i + 1, 0:wide]
                one_hot = jnp.where(row == value, 1.0, 0.0).astype(BF)
                term = dot_nn(one_hot, grad[i * wide : (i + 1) * wide])
                acc = term if acc is None else acc + term
        a_keep[k] = acc[0:quarter]
        a_send[k * quarter : (k + 1) * quarter] = acc[quarter : 2 * quarter].astype(BF)
        b_keep[k] = acc[2 * quarter : 3 * quarter]
        b_send[k * quarter : (k + 1) * quarter] = acc[3 * quarter : 4 * quarter].astype(BF)
    ext = joined(ext_ref) + pair(got_ref, span)
    ext_out[...] = ext
    a_send[taps * quarter : taps * quarter + 16] = coded(ext)


def second_kernel(a_in, b_in, a_got, b_got, ext_ref, a_keep, a_send, b_keep, b_send, ext_out):
    taps, rows, _ = a_in.shape
    part = rows // 2
    for src, got, keep, send in ((a_in, a_got, a_keep, a_send), (b_in, b_got, b_keep, b_send)):
        for k in range(taps):
            total = src[k] + got[k * rows : (k + 1) * rows].astype(F32)
            keep[k] = total[0:part]
            send[k * part : (k + 1) * part] = total[part:rows].astype(BF)
    ext = joined(ext_ref) + pair(a_got, taps * rows)
    ext_out[...] = ext
    a_send[taps * part : taps * part + 16] = coded(ext)


def third_kernel(a_in, b_in, a_got, b_got, ext_ref, keep, ext_out, *sends):
    taps, rows, _ = a_in.shape
    peers = len(sends)
    part = rows // (peers + 1)
    ext = joined(ext_ref) + pair(a_got, taps * rows)
    ext_out[...] = ext
    groups = 2 * taps
    pieces = [[] for _ in range(peers + 1)]
    for src, got in ((a_in, a_got), (b_in, b_got)):
        for k in range(taps):
            total = src[k] + got[k * rows : (k + 1) * rows].astype(F32)
            for t in range(peers + 1):
                pieces[t].append(total[t * part : (t + 1) * part])
    for t in range(peers + 1):
        block = jnp.concatenate(pieces[t], axis=0)
        if t == 0:
            keep[...] = block
        else:
            send = sends[t - 1]
            send[0 : groups * part] = block.astype(BF)
            send[groups * part : groups * part + 16] = coded(ext)


def tree_sum(items):
    while len(items) > 1:
        items = [items[i] + items[i + 1] for i in range(0, len(items), 2)]
    return items[0]


def shard_kernel(keep, ext_ref, scorer_ref, *refs, seq_size, taps, vocab):
    gots, (shard, loss_ref, bias_ref, grad_scorer_ref, calib_ref) = refs[:-5], refs[-5:]
    size, half = keep.shape
    part = size // (2 * taps)
    upper, a_mine, b_mine = place(seq_size, vocab // 4, part)
    ext = tree_sum([joined(ext_ref)] + [pair(g, size) for g in gots])
    total = tree_sum([keep[...]] + [g[0:size].astype(F32) for g in gots])
    spot = lax.broadcasted_iota(jnp.int32, (1, half), 1)
    misc = ext[11:12]

    def one(i):
        return jnp.sum(jnp.where(spot == i, misc, 0.0), axis=1, keepdims=True)

    count = one(33)
    scorer = scorer_ref[...].reshape(1, 2 * half)
    mine = jnp.where(upper, scorer[:, half:], scorer[:, :half])
    step = lax.broadcasted_iota(jnp.int32, (part, vocab), 0)
    lane = lax.broadcasted_iota(jnp.int32, (part, vocab), 1)
    pieces = []
    for g in range(2):
        hit = lane == step + (a_mine if g == 0 else vocab // 2 + b_mine)
        for k in range(taps):
            column = jnp.sum(jnp.where(hit, ext[6 + k : 7 + k, 0:vocab], 0.0), axis=1, keepdims=True)
            at = (g * taps + k) * part
            pieces.append(total[at : at + part] - (column / count) * mine)
    shard[...] = jnp.concatenate(pieces, axis=0).astype(BF)

    def whole(i):
        return jnp.concatenate([ext[i : i + 1], ext[i + 1 : i + 2]], axis=1)

    grad_scorer_ref[...] = (whole(0) - whole(2) / count).reshape(2 * half)
    bias_ref[...] = (whole(4) - (one(34) / count) * scorer).reshape(2 * half)
    row = lax.broadcasted_iota(jnp.int32, calib_ref.shape, 0)
    col = lax.broadcasted_iota(jnp.int32, calib_ref.shape, 1)
    out = jnp.zeros(calib_ref.shape, F32)
    for b in range(4):
        for c in range(4):
            out = jnp.where((row == b) & (col == c), one(4 * b + c) - one(16 + 4 * b + c) / count, out)
    calib_ref[...] = out
    loss_ref[...] = one(32) / count


def gather_kernel(*refs, taps):
    shards, (a_ref, b_ref) = refs[:-2], refs[-2:]
    part = shards[0].shape[0] // (2 * taps)
    wide = [s[...].astype(F32) for s in shards]
    for g, out in enumerate((a_ref, b_ref)):
        rows = [w[(g * taps + k) * part : (g * taps + k + 1) * part] for k in range(taps) for w in wide]
        out[...] = jnp.concatenate(rows, axis=0).astype(BF)


def double_kernel(a_ref, b_ref, a_got, b_got, early_ref, a_out, b_out, *, taps):
    rows = a_ref.shape[0] // taps
    for g, (src, got, out) in enumerate(((a_ref, a_got, a_out), (b_ref, b_got, b_out))):
        for k in range(taps):
            at = 2 * rows * k
            for first, ref in ((at, src), (at + rows, got)):
                piece = ref[k * rows : (k + 1) * rows]
                out[first : first + rows] = piece
                early_ref[g, first : first + rows] = piece


def order_kernel(table_ref, after_ref, out_ref, *, seq_size, part):
    del after_ref
    vocab = table_ref.shape[0]
    _, a_mine, b_mine = place(seq_size, vocab // 4, part)
    value = local_value((1, vocab), 1, a_mine, b_mine, vocab)
    natural = lax.broadcasted_iota(jnp.int32, (vocab, vocab), 0)
    out_ref[...] = dot_tn(table_ref[...], jnp.where(natural == value, 1.0, 0.0).astype(BF)).astype(BF)


def final_kernel(
    early, a_late, b_late, far_early, far_a, far_b, table_t_ref, weight_ref, conv_ref, table_ref, buffer, sem, *, seq_size, part,
):
    taps, width, _ = weight_ref.shape
    vocab = table_t_ref.shape[1]
    quarter = vocab // 4
    upper, a_mine, b_mine = place(seq_size, quarter, part)

    def rows_of(k):
        at = k * quarter
        near = [early[0, at : at + quarter], a_late[at : at + quarter], early[1, at : at + quarter], b_late[at : at + quarter]]
        far = [far_early[0, at : at + quarter], far_a[at : at + quarter], far_early[1, at : at + quarter], far_b[at : at + quarter]]
        near, far = jnp.concatenate(near, axis=0), jnp.concatenate(far, axis=0)
        return jnp.concatenate([jnp.where(upper, far, near), jnp.where(upper, near, far)], axis=1)

    rows = []
    for k in range(taps):
        rows.append(rows_of(k))
        buffer[k] = dot_nn(table_t_ref[...], rows[k])
        pltpu.make_async_copy(buffer.at[k], conv_ref.at[k], sem.at[k]).start()
    acc = dot_nt(rows[0], weight_ref[0])
    for k in range(1, taps):
        acc = acc + dot_nt(rows[k], weight_ref[k])
    for at in range(0, vocab, part):
        to = (at ^ a_mine) if at < vocab // 2 else vocab // 2 + ((at - vocab // 2) ^ b_mine)
        table_ref[pl.ds(pl.multiple_of(to, part), part)] = acc[at : at + part]
    for k in range(taps):
        pltpu.make_async_copy(buffer.at[k], conv_ref.at[k], sem.at[k]).wait()


def neighbour(shard, axis, by):
    length = lax.axis_size(axis)
    return lax.ppermute(shard, axis, [(i, i + by) for i in range(length) if 0 <= i + by < length])


def swap(shard, flip, count):
    return lax.ppermute(shard, AXES, [(i, i ^ flip) for i in range(count)])


def body(
    byte_ids, seg_ids, row_len, embed_table, conv_weight, conv_bias, scorer, calibration, cotangent
):
    row_count, span = byte_ids.shape
    vocab, width = embed_table.shape
    taps = conv_weight.shape[0]
    half = width // 2
    quarter = vocab // 4
    seq_size = lax.axis_size("seq")
    count = lax.axis_size("rows") * seq_size
    depth = count // 8
    assert row_count == 1 and vocab == 256 and taps == 5 and calibration.shape == (4, 4)
    assert seq_size % 2 == 0 and depth >= 1 and quarter // 2 % depth == 0
    part = quarter // 2 // depth
    eighth = quarter // 2
    size = 2 * taps * part
    lanes = span + 128

    to_right, to_left = pl.pallas_call(
        pack_kernel,
        out_shape=(shape((HALO, span), BF), shape((2 * HALO, width), BF)),
        grid=(1,),
        in_specs=[
            pl.BlockSpec((1, span), lambda i: (0, 0)),
            pl.BlockSpec((1, span), lambda i: (0, 0)),
            pl.BlockSpec((1, HALO, width), lambda i: (0, 0, 0)),
        ],
        out_specs=(pl.BlockSpec((HALO, span), lambda i: (0, 0)), pl.BlockSpec((2 * HALO, width), lambda i: (0, 0))),
        name="pack",
    )(byte_ids, seg_ids, cotangent)
    from_left = neighbour(to_right, "seq", 1)
    from_right = neighbour(to_left, "seq", -1)

    hi, lo, q_rows = pl.pallas_call(
        tap_kernel,
        out_shape=(shape((taps * vocab, width), BF), shape((taps * vocab, width), BF), shape((16, width), BF)),
        grid=(taps,),
        in_specs=[
            pl.BlockSpec((vocab, width), lambda k: (0, 0)),
            pl.BlockSpec((1, width, width), lambda k: (k, 0, 0)),
            pl.BlockSpec((width,), lambda k: (0,)),
        ],
        out_specs=(
            pl.BlockSpec((vocab, width), lambda k: (k, 0)),
            pl.BlockSpec((vocab, width), lambda k: (k, 0)),
            pl.BlockSpec((16, width), lambda k: (0, 0)),
        ),
        name="taps",
        compiler_params=pltpu.CompilerParams(vmem_limit_bytes=VMEM_LIMIT),
    )(embed_table, conv_weight, scorer)

    blocks, keep, send, ext, idt = call(
        functools.partial(local_kernel, seq_size=seq_size, taps=taps),
        (
            shape((1, span // 2, width), BF),
            shape((span, half), BF),
            shape((span + 32, half), BF),
            shape((16, half), F32),
            shape((16, span // 2), BF),
        ),
        "local",
        in_specs=[sspec(), sspec()] + [vspec()] * 9,
        out_specs=(vspec(),) * 5,
        scratch_shapes=[
            pltpu.VMEM((lanes, width), BF),
            pltpu.VMEM((span // 2 + 2 * HALO, width), BF),
            pltpu.VMEM((taps * vocab, lanes), BF),
        ],
    )(row_len, calibration, byte_ids, seg_ids, from_left, from_right, hi, lo, conv_bias, cotangent, q_rows)

    got = swap(send, 1, count)
    a_keep, a_send, b_keep, b_send, ext = call(
        functools.partial(table_kernel, seq_size=seq_size, part=part),
        (
            shape((taps, quarter, half), F32),
            shape((taps * quarter + 16, half), BF),
            shape((taps, quarter, half), F32),
            shape((taps * quarter, half), BF),
            shape((16, half), F32),
        ),
        "by_value",
        in_specs=[vspec()] * 4,
        out_specs=(vspec(),) * 5,
    )(keep, idt, got, ext)
    table_t = call(
        functools.partial(order_kernel, seq_size=seq_size, part=part),
        shape((width, vocab), BF),
        "order",
        in_specs=[vspec()] * 2,
        out_specs=vspec(),
    )(embed_table, ext)

    a_got, b_got = swap(a_send, 2, count), swap(b_send, 4, count)
    a_keep, a_send, b_keep, b_send, ext = call(
        second_kernel,
        (
            shape((taps, eighth, half), F32),
            shape((taps * eighth + 16, half), BF),
            shape((taps, eighth, half), F32),
            shape((taps * eighth, half), BF),
            shape((16, half), F32),
        ),
        "second",
        in_specs=[vspec()] * 5,
        out_specs=(vspec(),) * 5,
    )(a_keep, b_keep, a_got, b_got, ext)

    a_got, b_got = swap(a_send, 4, count), swap(b_send, 2, count)
    outs = call(
        third_kernel,
        (shape((size, half), F32), shape((16, half), F32)) + (shape((size + 16, half), BF),) * (depth - 1),
        "third",
        in_specs=[vspec()] * 5,
        out_specs=(vspec(),) * (depth + 1),
    )(a_keep, b_keep, a_got, b_got, ext)
    mine, ext, sends = outs[0], outs[1], outs[2:]
    gots = [swap(s, 8 * (t + 1), count) for t, s in enumerate(sends)]
    shard, loss, grad_bias, grad_scorer, grad_calib = call(
        functools.partial(shard_kernel, seq_size=seq_size, taps=taps, vocab=vocab),
        (shape((size, half), BF), shape((1, 1), F32), shape((width,), F32), shape((width,), F32), shape((4, 4), F32)),
        "shard",
        in_specs=[vspec()] * (3 + len(gots)),
        out_specs=(vspec(),) * 5,
    )(mine, ext, scorer, *gots)

    gathered = [shard] + [swap(shard, 8 * t, count) for t in range(1, depth)]
    a_out, b_out = call(
        functools.partial(gather_kernel, taps=taps),
        (shape((taps * eighth, half), BF),) * 2,
        "gather",
        in_specs=[vspec()] * depth,
        out_specs=(vspec(),) * 2,
    )(*gathered)
    a_got, b_got = swap(a_out, 4, count), swap(b_out, 2, count)
    early, a_out, b_out = call(
        functools.partial(double_kernel, taps=taps),
        (shape((2, taps * quarter, half), BF),) + (shape((taps * quarter, half), BF),) * 2,
        "double",
        in_specs=[vspec()] * 4,
        out_specs=(vspec(),) * 3,
    )(a_out, b_out, a_got, b_got)
    a_late, b_late = swap(a_out, 2, count), swap(b_out, 4, count)
    far_early = swap(early, 1, count)
    far_a, far_b = swap(a_late, 1, count), swap(b_late, 1, count)

    conv, table = call(
        functools.partial(final_kernel, seq_size=seq_size, part=part),
        (shape((taps, width, width), F32), shape((vocab, width), F32)),
        "final",
        in_specs=[vspec()] * 8,
        out_specs=(pl.BlockSpec(memory_space=pl.ANY), vspec()),
        scratch_shapes=[pltpu.VMEM((taps, width, width), F32), pltpu.SemaphoreType.DMA((taps,))],
    )(early, a_late, b_late, far_early, far_a, far_b, table_t, conv_weight)
    return (blocks, loss.reshape(()), table, conv, grad_bias, grad_scorer, grad_calib)


def solution(mesh):
    return jax.shard_map(
        body,
        mesh=mesh,
        in_specs=(
            P("rows", "seq"),
            P("rows", "seq"),
            P("rows"),
            P(),
            P(),
            P(),
            P(),
            P(),
            P("rows", "seq", None),
        ),
        out_specs=(P("rows", "seq", None), P(), P(), P(), P(), P(), P()),
        check_vma=False,
    )
```

time: 103 us -> 86.9 us (0.84)
  local copies, waits for them, and re-layouts: 10.9 us -> 1.7 us
  Pallas kernels: 31.7 us -> 26.5 us
  other arithmetic: 2.86 us -> 0 us
  waiting for transfers between devices: 29.4 us -> 30.7 us
    pallas_call x6 -> x9, Pallas kernels: 31.5 us -> 26.4 us  [the longest x1 8.79 us: body(): call(functools.partial(final_kernel, seq_size=seq_size, part=part), (shap...]
    slice x12 -> x0, local copies, waits for them, and re-layouts: 2.37 us -> none  [the longest x1 0.74 us: body(): cot[:HALO]]
    unnamed x21 -> x16, local copies, waits for them, and re-layouts: 4.04 us -> 1.7 us
    convert_element_type x5 -> x0, other arithmetic: 1.39 us -> none  [the longest x1 0.69 us: body(): ids = byte_ids[0].astype(F32)]
    broadcast_in_dim x3 -> x0, local copies, waits for them, and re-layouts: 1.38 us -> none  [the longest x1 0.69 us: body(): conv_bias[None]]
    ppermute x18, waiting for transfers between devices: 29.4 us -> 30.7 us  [swap(): return lax.ppermute(shard, AXES, [(i, i ^ flip) for i in range(count)])]
    reshape x3 -> x0, local copies, waits for them, and re-layouts: 1.21 us -> none  [the longest x1 0.6 us: body(): grad_scorer = small[0:2].reshape(width)]
    another operation x22 -> x0, local copies, waits for them, and re-layouts: 1.1 us -> none  [the longest x1 0.66 us: body(): grad_calib = small[4, 0:16].reshape(4, 4)]
  transfers between devices with their start and end apart: 20 -> 20, of which waited for: 11 -> 13; matrix products, arithmetic and copies ran while one was open for 7% -> 0% of each run, Pallas kernels for 13% -> 7%
where the time goes in v2:
time: 86.9 us; the launch traced here: 86.5 us
  waiting for transfers between devices  30.7 us (35%)
  Pallas kernels  26.5 us (30%)
  starting transfers between devices  26.1 us (30%)
  local copies, waits for them, and re-layouts  1.7 us (2%)
  between operations  1.47 us (2%)
    ppermute x18, waiting for transfers between devices, swap(): return lax.ppermute(shard, AXES, [(i, i ^ flip) for i in range(count)])  30.7 us
    ppermute x18, starting transfers between devices, swap(): return lax.ppermute(shard, AXES, [(i, i ^ flip) for i in range(count)])  21.8 us
    pallas_call x1, Pallas kernels, body(): call(functools.partial(final_kernel, seq_size=seq_size, part=part), (shap...  8.79 us
    pallas_call x1, Pallas kernels, body(): call(functools.partial(local_kernel, seq_size=seq_size, taps=taps), (shap...  8.11 us
    pallas_call x1, Pallas kernels, body(): pl.pallas_call(tap_kernel, out_shape=(shape((taps * vocab, width), BF), s...  5.35 us
    ppermute x2, starting transfers between devices, neighbour(): lax.ppermute(shard, axis, [(i, i + by) for i in range(length) if 0 <= i +...  4.31 us
  transfers between devices with their start and end apart: 20, of which 13 were waited for; matrix products, arithmetic and copies ran while one was open for 0% of the time, Pallas kernels for 7%

profile of v2, /device:TPU:0, one launch (start us, length us, event | category | flops | bytes accessed | tf_op | source)
XLA Modules:
  0.0 86.5 jit_solution(3960291253756183908)
XLA Ops:
  0.7 1.4 %pack.1 = (bf16[16,512]{1,0:T(8,128)(2,1)}, bf16[32,768]{1,0:T(8,128)(2,1)}) custom-call(s32[1,512]{1,0:T(1,128)} %ids_ref.3, s32[1,512]{1,0:T(1,128)} %seg_ref.3, bf16[1,256,768]{2,1,0:T(8,128)(2,1)} %cot_ref.3), custom_call_target="tpu_custom_call" | custom-call | tf_op jit(solution)/shard_map/pack/pallas_call | solution.py:464
  2.1 1.3 %collective-permute-start.1 = (bf16[32,768]{1,0:T(8,128)(2,1)}, bf16[32,768]{1,0:T(8,128)(2,1)S(1)}, u32[]{:S(2)}, u32[]{:S(2)}) collective-permute-start(bf16[32,768]{1,0:T(8,128)(2,1)} %get-tuple-element.45), channel_id=1, source_target_pairs={{1,0},{2,1},{3,2},{5,4},{6,5},{7,6},{9,8},{10,9},{11,10},{13,12},{... | collective-permute-start | bytes 147464 | tf_op jit(solution)/shard_map/ppermute | solution.py:439
  3.4 3.0 %collective-permute-start = (bf16[16,512]{1,0:T(8,128)(2,1)}, bf16[16,512]{1,0:T(8,128)(2,1)S(1)}, u32[]{:S(2)}, u32[]{:S(2)}) collective-permute-start(bf16[16,512]{1,0:T(8,128)(2,1)} %get-tuple-element.44), channel_id=1, source_target_pairs={{0,1},{1,2},{2,3},{4,5},{5,6},{6,7},{8,9},{9,10},{10,11},{12,13},{... | collective-permute-start | bytes 49160 | tf_op jit(solution)/shard_map/ppermute | solution.py:439
  7.1 1.0 %copy-done.1 = bf16[256,768]{1,0:T(8,128)(2,1)S(1)} copy-done((bf16[256,768]{1,0:T(8,128)(2,1)S(1)}, bf16[256,768]{1,0:T(8,128)(2,1)}, u32[]{:S(2)}) %copy-start.1) | copy-done | bytes 393240
  8.8 5.4 %taps.1 = (bf16[1280,768]{1,0:T(8,128)(2,1)S(1)}, bf16[1280,768]{1,0:T(8,128)(2,1)S(1)}, bf16[16,768]{1,0:T(8,128)(2,1)S(1)}) custom-call(bf16[256,768]{1,0:T(8,128)(2,1)S(1)} %copy-done.1, bf16[5,768,768]{2,1,0:T(8,128)(2,1)} %weight_ref.3, f32[768]{0:T(1024)S(1)} %copy-done.3), custom_call_target="tpu_custom_call" | custom-call | tf_op jit(solution)/shard_map/taps/pallas_call | solution.py:479
  14.2 8.1 %local.1 = (bf16[1,256,768]{2,1,0:T(8,128)(2,1)}, bf16[512,384]{1,0:T(8,128)(2,1)S(1)}, bf16[544,384]{1,0:T(8,128)(2,1)S(1)}, f32[16,384]{1,0:T(8,128)S(1)}, bf16[16,256]{1,0:T(8,128)(2,1)S(1)}) custom-call(s32[1]{0:T(128)S(6)} %copy.16.row_len_ref, f32[4,4]{1,0:T(4,128)S(1)} %copy-done.7, s32[1,512]{1,0:T(1,128)S(1)} %copy-done.4, s32[1,512]{1,0:T(1,128)S(1)} %copy-done.5, ...), custom_call_target="tpu_custom_call" | custom-call | tf_op jit(solution)/shard_map/local/pallas_call | solution.py:497
  22.3 2.7 %collective-permute-start.2 = (bf16[544,384]{1,0:T(8,128)(2,1)S(1)}, bf16[544,384]{1,0:T(8,128)(2,1)S(1)}, u32[]{:S(2)}, u32[]{:S(2)}) collective-permute-start(bf16[544,384]{1,0:T(8,128)(2,1)S(1)} %get-tuple-element.52), channel_id=1, source_target_pairs={{0,1},{1,0},{2,3},{3,2},{4,5},{5,4},{6,7},{7,6},{8,9},{9,8},{10,11... | collective-permute-start | bytes 1253384 | tf_op jit(solution)/shard_map/ppermute | solution.py:443
  25.0 1.4 %collective-permute-done.2.got_ref = bf16[544,384]{1,0:T(8,128)(2,1)S(1)} collective-permute-done((bf16[544,384]{1,0:T(8,128)(2,1)S(1)}, bf16[544,384]{1,0:T(8,128)(2,1)S(1)}, u32[]{:S(2)}, u32[]{:S(2)}) %collective-permute-start.2) | collective-permute-done | bytes 417824 | tf_op jit(solution)/shard_map/ppermute | solution.py:443
  26.4 1.5 %by_value.1 = (f32[5,64,384]{2,1,0:T(8,128)S(1)}, bf16[336,384]{1,0:T(8,128)(2,1)S(1)}, f32[5,64,384]{2,1,0:T(8,128)S(1)}, bf16[320,384]{1,0:T(8,128)(2,1)S(1)}, f32[16,384]{1,0:T(8,128)S(1)}) custom-call(bf16[512,384]{1,0:T(8,128)(2,1)S(1)} %get-tuple-element.50.keep_ref, bf16[16,256]{1,0:T(8,128)(2,1)S(1)} %get-tuple-element.51.idt_ref, ...), custom_call_target="tpu_custom_call" | custom-call | tf_op jit(solution)/shard_map/by_value/pallas_call | solution.py:517
  27.9 0.8 collective-permute-start.3
  28.7 1.5 %collective-permute-start.4 = (bf16[320,384]{1,0:T(8,128)(2,1)S(1)}, bf16[320,384]{1,0:T(8,128)(2,1)S(1)}, u32[]{:S(2)}, u32[]{:S(2)}) collective-permute-start(bf16[320,384]{1,0:T(8,128)(2,1)S(1)} %get-tuple-element.57), channel_id=1, source_target_pairs={{0,4},{1,5},{2,6},{3,7},{4,0},{5,1},{6,2},{7,3},{8,12},{9,13},{10,... | collective-permute-start | bytes 737288 | tf_op jit(solution)/shard_map/ppermute | solution.py:443
  30.2 6.2 %collective-permute-done.4.b_got = bf16[320,384]{1,0:T(8,128)(2,1)S(1)} collective-permute-done((bf16[320,384]{1,0:T(8,128)(2,1)S(1)}, bf16[320,384]{1,0:T(8,128)(2,1)S(1)}, u32[]{:S(2)}, u32[]{:S(2)}) %collective-permute-start.4) | collective-permute-done | bytes 245792 | tf_op jit(solution)/shard_map/ppermute | solution.py:443
  36.6 1.6 %collective-permute-start.5 = (bf16[176,384]{1,0:T(8,128)(2,1)S(1)}, bf16[176,384]{1,0:T(8,128)(2,1)S(1)}, u32[]{:S(2)}, u32[]{:S(2)}) collective-permute-start(bf16[176,384]{1,0:T(8,128)(2,1)S(1)} %get-tuple-element.61), channel_id=1, source_target_pairs={{0,4},{1,5},{2,6},{3,7},{4,0},{5,1},{6,2},{7,3},{8,12},{9,13},{10,... | collective-permute-start | bytes 405512 | tf_op jit(solution)/shard_map/ppermute | solution.py:443
  38.2 1.5 %collective-permute-start.6 = (bf16[160,384]{1,0:T(8,128)(2,1)S(1)}, bf16[160,384]{1,0:T(8,128)(2,1)S(1)}, u32[]{:S(2)}, u32[]{:S(2)}) collective-permute-start(bf16[160,384]{1,0:T(8,128)(2,1)S(1)} %get-tuple-element.62), channel_id=1, source_target_pairs={{0,2},{1,3},{2,0},{3,1},{4,6},{5,7},{6,4},{7,5},{8,10},{9,11},{10,... | collective-permute-start | bytes 368648 | tf_op jit(solution)/shard_map/ppermute | solution.py:443
  39.7 3.4 %collective-permute-done.6.b_got = bf16[160,384]{1,0:T(8,128)(2,1)S(1)} collective-permute-done((bf16[160,384]{1,0:T(8,128)(2,1)S(1)}, bf16[160,384]{1,0:T(8,128)(2,1)S(1)}, u32[]{:S(2)}, u32[]{:S(2)}) %collective-permute-start.6) | collective-permute-done | bytes 122912 | tf_op jit(solution)/shard_map/ppermute | solution.py:443
  43.1 1.6 %collective-permute-start.7 = (bf16[96,384]{1,0:T(8,128)(2,1)S(1)}, bf16[96,384]{1,0:T(8,128)(2,1)S(1)}, u32[]{:S(2)}, u32[]{:S(2)}) collective-permute-start(bf16[96,384]{1,0:T(8,128)(2,1)S(1)} %get-tuple-element.66), channel_id=1, source_target_pairs={{0,8},{1,9},{2,10},{3,11},{4,12},{5,13},{6,14},{7,15},{8,0},{9,1},... | collective-permute-start | bytes 221192 | tf_op jit(solution)/shard_map/ppermute | solution.py:443
  44.8 2.6 %collective-permute-start.8 = (bf16[96,384]{1,0:T(8,128)(2,1)S(1)}, bf16[96,384]{1,0:T(8,128)(2,1)S(1)}, u32[]{:S(2)}, u32[]{:S(2)}) collective-permute-start(bf16[96,384]{1,0:T(8,128)(2,1)S(1)} %get-tuple-element.67), channel_id=1, source_target_pairs={{0,16},{1,17},{2,18},{3,19},{4,20},{5,21},{6,22},{7,23},{8,24},{9,... | collective-permute-start | bytes 221192 | tf_op jit(solution)/shard_map/ppermute | solution.py:443
  47.9 3.7 %collective-permute-done.8.refs_1_ = bf16[96,384]{1,0:T(8,128)(2,1)S(1)} collective-permute-done((bf16[96,384]{1,0:T(8,128)(2,1)S(1)}, bf16[96,384]{1,0:T(8,128)(2,1)S(1)}, u32[]{:S(2)}, u32[]{:S(2)}) %collective-permute-start.8) | collective-permute-done | bytes 73760 | tf_op jit(solution)/shard_map/ppermute | solution.py:443
  51.6 2.0 %collective-permute-done.9.refs_2_ = bf16[96,384]{1,0:T(8,128)(2,1)S(1)} collective-permute-done((bf16[96,384]{1,0:T(8,128)(2,1)S(1)}, bf16[96,384]{1,0:T(8,128)(2,1)S(1)}, u32[]{:S(2)}, u32[]{:S(2)}) %collective-permute-start.9) | collective-permute-done | bytes 73760 | tf_op jit(solution)/shard_map/ppermute | solution.py:443
  54.3 1.1 %collective-permute-start.12 = (bf16[80,384]{1,0:T(8,128)(2,1)S(1)}, bf16[80,384]{1,0:T(8,128)(2,1)S(1)}, u32[]{:S(2)}, u32[]{:S(2)}) collective-permute-start(bf16[80,384]{1,0:T(8,128)(2,1)S(1)} %get-tuple-element.70.refs_0_), channel_id=1, source_target_pairs={{0,24},{1,25},{2,26},{3,27},{4,28},{5,29},{6,30},{7,31},{8,16},{9,... | collective-permute-start | bytes 184328 | tf_op jit(solution)/shard_map/ppermute | solution.py:443
  55.9 2.9 %collective-permute-start.10 = (bf16[80,384]{1,0:T(8,128)(2,1)S(1)}, bf16[80,384]{1,0:T(8,128)(2,1)S(1)}, u32[]{:S(2)}, u32[]{:S(2)}) collective-permute-start(bf16[80,384]{1,0:T(8,128)(2,1)S(1)} %get-tuple-element.70.refs_0_), channel_id=1, source_target_pairs={{0,8},{1,9},{2,10},{3,11},{4,12},{5,13},{6,14},{7,15},{8,0},{9,1},... | collective-permute-start | bytes 184328 | tf_op jit(solution)/shard_map/ppermute | solution.py:443
  58.7 1.7 %collective-permute-done.12.refs_3_ = bf16[80,384]{1,0:T(8,128)(2,1)S(1)} collective-permute-done((bf16[80,384]{1,0:T(8,128)(2,1)S(1)}, bf16[80,384]{1,0:T(8,128)(2,1)S(1)}, u32[]{:S(2)}, u32[]{:S(2)}) %collective-permute-start.12) | collective-permute-done | bytes 61472 | tf_op jit(solution)/shard_map/ppermute | solution.py:443
  60.4 1.3 %collective-permute-done.11.refs_2_ = bf16[80,384]{1,0:T(8,128)(2,1)S(1)} collective-permute-done((bf16[80,384]{1,0:T(8,128)(2,1)S(1)}, bf16[80,384]{1,0:T(8,128)(2,1)S(1)}, u32[]{:S(2)}, u32[]{:S(2)}) %collective-permute-start.11) | collective-permute-done | bytes 61472 | tf_op jit(solution)/shard_map/ppermute | solution.py:443
  62.3 1.4 %collective-permute-start.14 = (bf16[160,384]{1,0:T(8,128)(2,1)S(1)}, bf16[160,384]{1,0:T(8,128)(2,1)S(1)}, u32[]{:S(2)}, u32[]{:S(2)}) collective-permute-start(bf16[160,384]{1,0:T(8,128)(2,1)S(1)} %get-tuple-element.72.b_ref), channel_id=1, source_target_pairs={{0,2},{1,3},{2,0},{3,1},{4,6},{5,7},{6,4},{7,5},{8,10},{9,11},{10,... | collective-permute-start | bytes 368648 | tf_op jit(solution)/shard_map/ppermute | solution.py:443
  63.6 3.9 %collective-permute-done.13.a_got = bf16[160,384]{1,0:T(8,128)(2,1)S(1)} collective-permute-done((bf16[160,384]{1,0:T(8,128)(2,1)S(1)}, bf16[160,384]{1,0:T(8,128)(2,1)S(1)}, u32[]{:S(2)}, u32[]{:S(2)}) %collective-permute-start.13) | collective-permute-done | bytes 122912 | tf_op jit(solution)/shard_map/ppermute | solution.py:443
  67.6 0.9 %collective-permute-done.14.b_got = bf16[160,384]{1,0:T(8,128)(2,1)S(1)} collective-permute-done((bf16[160,384]{1,0:T(8,128)(2,1)S(1)}, bf16[160,384]{1,0:T(8,128)(2,1)S(1)}, u32[]{:S(2)}, u32[]{:S(2)}) %collective-permute-start.14) | collective-permute-done | bytes 122912 | tf_op jit(solution)/shard_map/ppermute | solution.py:443
  68.5 1.4 %collective-permute-start.15 = (bf16[320,384]{1,0:T(8,128)(2,1)S(1)}, bf16[320,384]{1,0:T(8,128)(2,1)S(1)}, u32[]{:S(2)}, u32[]{:S(2)}) collective-permute-start(bf16[320,384]{1,0:T(8,128)(2,1)S(1)} %get-tuple-element.74), channel_id=1, source_target_pairs={{0,2},{1,3},{2,0},{3,1},{4,6},{5,7},{6,4},{7,5},{8,10},{9,11},{10,... | collective-permute-start | bytes 737288 | tf_op jit(solution)/shard_map/ppermute | solution.py:443
  70.0 1.5 %collective-permute-start.16 = (bf16[320,384]{1,0:T(8,128)(2,1)S(1)}, bf16[320,384]{1,0:T(8,128)(2,1)S(1)}, u32[]{:S(2)}, u32[]{:S(2)}) collective-permute-start(bf16[320,384]{1,0:T(8,128)(2,1)S(1)} %get-tuple-element.75), channel_id=1, source_target_pairs={{0,4},{1,5},{2,6},{3,7},{4,0},{5,1},{6,2},{7,3},{8,12},{9,13},{10,... | collective-permute-start | bytes 737288 | tf_op jit(solution)/shard_map/ppermute | solution.py:443
  71.5 3.3 %collective-permute-done.15.a_late = bf16[320,384]{1,0:T(8,128)(2,1)S(1)} collective-permute-done((bf16[320,384]{1,0:T(8,128)(2,1)S(1)}, bf16[320,384]{1,0:T(8,128)(2,1)S(1)}, u32[]{:S(2)}, u32[]{:S(2)}) %collective-permute-start.15) | collective-permute-done | bytes 245792 | tf_op jit(solution)/shard_map/ppermute | solution.py:443
  74.8 1.4 %collective-permute-done.16.b_late = bf16[320,384]{1,0:T(8,128)(2,1)S(1)} collective-permute-done((bf16[320,384]{1,0:T(8,128)(2,1)S(1)}, bf16[320,384]{1,0:T(8,128)(2,1)S(1)}, u32[]{:S(2)}, u32[]{:S(2)}) %collective-permute-start.16) | collective-permute-done | bytes 245792 | tf_op jit(solution)/shard_map/ppermute | solution.py:443
  76.5 1.2 %collective-permute-done.19.far_b = bf16[320,384]{1,0:T(8,128)(2,1)S(1)} collective-permute-done((bf16[320,384]{1,0:T(8,128)(2,1)S(1)}, bf16[320,384]{1,0:T(8,128)(2,1)S(1)}, u32[]{:S(2)}, u32[]{:S(2)}) %collective-permute-start.19) | collective-permute-done | bytes 245792 | tf_op jit(solution)/shard_map/ppermute | solution.py:443
  77.7 8.8 %final.1 = (f32[5,768,768]{2,1,0:T(8,128)}, f32[256,768]{1,0:T(8,128)}) custom-call(bf16[2,320,384]{2,1,0:T(8,128)(2,1)S(1)} %get-tuple-element.73.early, bf16[320,384]{1,0:T(8,128)(2,1)S(1)} %collective-permute-done.15.a_late, bf16[320,384]{1,0:T(8,128)(2,1)S(1)} %collective-permute-done.16.b_late, ...), custom_call_target="tpu_custom_call" | custom-call | tf_op jit(solution)/shard_map/final/pallas_call | solution.py:591
  (35 shorter events, 3.6 us)
Async XLA Ops:
  0.6 13.5 %copy-start = (bf16[1,256,768]{2,1,0:T(8,128)(2,1)S(1)}, bf16[1,256,768]{2,1,0:T(8,128)(2,1)}, u32[]{:S(2)}) copy-start(bf16[1,256,768]{2,1,0:T(8,128)(2,1)} %cot_ref.3) | copy-start | bytes 1179652
  0.6 13.5 %copy-start.5 = (s32[1,512]{1,0:T(1,128)S(1)}, s32[1,512]{1,0:T(1,128)}, u32[]{:S(2)}) copy-start(s32[1,512]{1,0:T(1,128)} %seg_ref.3) | copy-start | bytes 6148
  0.7 13.5 %copy-start.4 = (s32[1,512]{1,0:T(1,128)S(1)}, s32[1,512]{1,0:T(1,128)}, u32[]{:S(2)}) copy-start(s32[1,512]{1,0:T(1,128)} %ids_ref.3) | copy-start | bytes 6148
  0.7 13.5 %copy-start.6 = (f32[768]{0:T(1024)S(1)}, f32[768]{0:T(1024)}, u32[]{:S(2)}) copy-start(f32[768]{0:T(1024)} %bias_ref.1) | copy-start | bytes 9220
  2.1 12.0 %collective-permute-start.1 = (bf16[32,768]{1,0:T(8,128)(2,1)}, bf16[32,768]{1,0:T(8,128)(2,1)S(1)}, u32[]{:S(2)}, u32[]{:S(2)}) collective-permute-start(bf16[32,768]{1,0:T(8,128)(2,1)} %get-tuple-element.45), channel_id=1, source_target_pairs={{1,0},{2,1},{3,2},{5,4},{6,5},{7,6},{9,8},{10,9},{11,10},{13,12},{... | collective-permute-start | bytes 147464 | tf_op jit(solution)/shard_map/ppermute | solution.py:439
  3.4 10.7 %collective-permute-start = (bf16[16,512]{1,0:T(8,128)(2,1)}, bf16[16,512]{1,0:T(8,128)(2,1)S(1)}, u32[]{:S(2)}, u32[]{:S(2)}) collective-permute-start(bf16[16,512]{1,0:T(8,128)(2,1)} %get-tuple-element.44), channel_id=1, source_target_pairs={{0,1},{1,2},{2,3},{4,5},{5,6},{6,7},{8,9},{9,10},{10,11},{12,13},{... | collective-permute-start | bytes 49160 | tf_op jit(solution)/shard_map/ppermute | solution.py:439
  7.1 1.0 %copy-start.1 = (bf16[256,768]{1,0:T(8,128)(2,1)S(1)}, bf16[256,768]{1,0:T(8,128)(2,1)}, u32[]{:S(2)}) copy-start(bf16[256,768]{1,0:T(8,128)(2,1)} %table_ref.3) | copy-start | bytes 1179652
  8.1 0.7 copy-start.3
  8.8 5.4 %copy-start.7 = (f32[4,4]{1,0:T(4,128)S(1)}, f32[4,4]{1,0:T(4,128)}, u32[]{:S(2)}) copy-start(f32[4,4]{1,0:T(4,128)} %calib_ref.1) | copy-start | bytes 196
  14.1 62.1 %copy-start.2 = (bf16[256,768]{1,0:T(8,128)(2,1)S(1)}, bf16[256,768]{1,0:T(8,128)(2,1)}, u32[]{:S(2)}) copy-start(bf16[256,768]{1,0:T(8,128)(2,1)} %table_ref.3) | copy-start | bytes 1179652
  22.3 4.0 %collective-permute-start.2 = (bf16[544,384]{1,0:T(8,128)(2,1)S(1)}, bf16[544,384]{1,0:T(8,128)(2,1)S(1)}, u32[]{:S(2)}, u32[]{:S(2)}) collective-permute-start(bf16[544,384]{1,0:T(8,128)(2,1)S(1)} %get-tuple-element.52), channel_id=1, source_target_pairs={{0,1},{1,0},{2,3},{3,2},{4,5},{5,4},{6,7},{7,6},{8,9},{9,8},{10,11... | collective-permute-start | bytes 1253384 | tf_op jit(solution)/shard_map/ppermute | solution.py:443
  27.9 8.6 %collective-permute-start.3 = (bf16[336,384]{1,0:T(8,128)(2,1)S(1)}, bf16[336,384]{1,0:T(8,128)(2,1)S(1)}, u32[]{:S(2)}, u32[]{:S(2)}) collective-permute-start(bf16[336,384]{1,0:T(8,128)(2,1)S(1)} %get-tuple-element.56), channel_id=1, source_target_pairs={{0,2},{1,3},{2,0},{3,1},{4,6},{5,7},{6,4},{7,5},{8,10},{9,11},{10,... | collective-permute-start | bytes 774152 | tf_op jit(solution)/shard_map/ppermute | solution.py:443
  28.7 7.7 %collective-permute-start.4 = (bf16[320,384]{1,0:T(8,128)(2,1)S(1)}, bf16[320,384]{1,0:T(8,128)(2,1)S(1)}, u32[]{:S(2)}, u32[]{:S(2)}) collective-permute-start(bf16[320,384]{1,0:T(8,128)(2,1)S(1)} %get-tuple-element.57), channel_id=1, source_target_pairs={{0,4},{1,5},{2,6},{3,7},{4,0},{5,1},{6,2},{7,3},{8,12},{9,13},{10,... | collective-permute-start | bytes 737288 | tf_op jit(solution)/shard_map/ppermute | solution.py:443
  36.6 6.5 %collective-permute-start.5 = (bf16[176,384]{1,0:T(8,128)(2,1)S(1)}, bf16[176,384]{1,0:T(8,128)(2,1)S(1)}, u32[]{:S(2)}, u32[]{:S(2)}) collective-permute-start(bf16[176,384]{1,0:T(8,128)(2,1)S(1)} %get-tuple-element.61), channel_id=1, source_target_pairs={{0,4},{1,5},{2,6},{3,7},{4,0},{5,1},{6,2},{7,3},{8,12},{9,13},{10,... | collective-permute-start | bytes 405512 | tf_op jit(solution)/shard_map/ppermute | solution.py:443
  38.2 4.9 %collective-permute-start.6 = (bf16[160,384]{1,0:T(8,128)(2,1)S(1)}, bf16[160,384]{1,0:T(8,128)(2,1)S(1)}, u32[]{:S(2)}, u32[]{:S(2)}) collective-permute-start(bf16[160,384]{1,0:T(8,128)(2,1)S(1)} %get-tuple-element.62), channel_id=1, source_target_pairs={{0,2},{1,3},{2,0},{3,1},{4,6},{5,7},{6,4},{7,5},{8,10},{9,11},{10,... | collective-permute-start | bytes 368648 | tf_op jit(solution)/shard_map/ppermute | solution.py:443
  43.1 4.8 %collective-permute-start.7 = (bf16[96,384]{1,0:T(8,128)(2,1)S(1)}, bf16[96,384]{1,0:T(8,128)(2,1)S(1)}, u32[]{:S(2)}, u32[]{:S(2)}) collective-permute-start(bf16[96,384]{1,0:T(8,128)(2,1)S(1)} %get-tuple-element.66), channel_id=1, source_target_pairs={{0,8},{1,9},{2,10},{3,11},{4,12},{5,13},{6,14},{7,15},{8,0},{9,1},... | collective-permute-start | bytes 221192 | tf_op jit(solution)/shard_map/ppermute | solution.py:443
  44.8 6.8 %collective-permute-start.8 = (bf16[96,384]{1,0:T(8,128)(2,1)S(1)}, bf16[96,384]{1,0:T(8,128)(2,1)S(1)}, u32[]{:S(2)}, u32[]{:S(2)}) collective-permute-start(bf16[96,384]{1,0:T(8,128)(2,1)S(1)} %get-tuple-element.67), channel_id=1, source_target_pairs={{0,16},{1,17},{2,18},{3,19},{4,20},{5,21},{6,22},{7,23},{8,24},{9,... | collective-permute-start | bytes 221192 | tf_op jit(solution)/shard_map/ppermute | solution.py:443
  47.4 6.3 %collective-permute-start.9 = (bf16[96,384]{1,0:T(8,128)(2,1)S(1)}, bf16[96,384]{1,0:T(8,128)(2,1)S(1)}, u32[]{:S(2)}, u32[]{:S(2)}) collective-permute-start(bf16[96,384]{1,0:T(8,128)(2,1)S(1)} %get-tuple-element.68), channel_id=1, source_target_pairs={{0,24},{1,25},{2,26},{3,27},{4,28},{5,29},{6,30},{7,31},{8,16},{9,... | collective-permute-start | bytes 221192 | tf_op jit(solution)/shard_map/ppermute | solution.py:443
  54.3 6.1 %collective-permute-start.12 = (bf16[80,384]{1,0:T(8,128)(2,1)S(1)}, bf16[80,384]{1,0:T(8,128)(2,1)S(1)}, u32[]{:S(2)}, u32[]{:S(2)}) collective-permute-start(bf16[80,384]{1,0:T(8,128)(2,1)S(1)} %get-tuple-element.70.refs_0_), channel_id=1, source_target_pairs={{0,24},{1,25},{2,26},{3,27},{4,28},{5,29},{6,30},{7,31},{8,16},{9,... | collective-permute-start | bytes 184328 | tf_op jit(solution)/shard_map/ppermute | solution.py:443
  55.4 6.2 %collective-permute-start.11 = (bf16[80,384]{1,0:T(8,128)(2,1)S(1)}, bf16[80,384]{1,0:T(8,128)(2,1)S(1)}, u32[]{:S(2)}, u32[]{:S(2)}) collective-permute-start(bf16[80,384]{1,0:T(8,128)(2,1)S(1)} %get-tuple-element.70.refs_0_), channel_id=1, source_target_pairs={{0,16},{1,17},{2,18},{3,19},{4,20},{5,21},{6,22},{7,23},{8,24},{9,... | collective-permute-start | bytes 184328 | tf_op jit(solution)/shard_map/ppermute | solution.py:443
  55.9 5.8 %collective-permute-start.10 = (bf16[80,384]{1,0:T(8,128)(2,1)S(1)}, bf16[80,384]{1,0:T(8,128)(2,1)S(1)}, u32[]{:S(2)}, u32[]{:S(2)}) collective-permute-start(bf16[80,384]{1,0:T(8,128)(2,1)S(1)} %get-tuple-element.70.refs_0_), channel_id=1, source_target_pairs={{0,8},{1,9},{2,10},{3,11},{4,12},{5,13},{6,14},{7,15},{8,0},{9,1},... | collective-permute-start | bytes 184328 | tf_op jit(solution)/shard_map/ppermute | solution.py:443
  61.7 5.9 %collective-permute-start.13 = (bf16[160,384]{1,0:T(8,128)(2,1)S(1)}, bf16[160,384]{1,0:T(8,128)(2,1)S(1)}, u32[]{:S(2)}, u32[]{:S(2)}) collective-permute-start(bf16[160,384]{1,0:T(8,128)(2,1)S(1)} %get-tuple-element.71.a_ref), channel_id=1, source_target_pairs={{0,4},{1,5},{2,6},{3,7},{4,0},{5,1},{6,2},{7,3},{8,12},{9,13},{10,... | collective-permute-start | bytes 368648 | tf_op jit(solution)/shard_map/ppermute | solution.py:443
  62.3 6.2 %collective-permute-start.14 = (bf16[160,384]{1,0:T(8,128)(2,1)S(1)}, bf16[160,384]{1,0:T(8,128)(2,1)S(1)}, u32[]{:S(2)}, u32[]{:S(2)}) collective-permute-start(bf16[160,384]{1,0:T(8,128)(2,1)S(1)} %get-tuple-element.72.b_ref), channel_id=1, source_target_pairs={{0,2},{1,3},{2,0},{3,1},{4,6},{5,7},{6,4},{7,5},{8,10},{9,11},{10,... | collective-permute-start | bytes 368648 | tf_op jit(solution)/shard_map/ppermute | solution.py:443
  68.5 6.3 %collective-permute-start.15 = (bf16[320,384]{1,0:T(8,128)(2,1)S(1)}, bf16[320,384]{1,0:T(8,128)(2,1)S(1)}, u32[]{:S(2)}, u32[]{:S(2)}) collective-permute-start(bf16[320,384]{1,0:T(8,128)(2,1)S(1)} %get-tuple-element.74), channel_id=1, source_target_pairs={{0,2},{1,3},{2,0},{3,1},{4,6},{5,7},{6,4},{7,5},{8,10},{9,11},{10,... | collective-permute-start | bytes 737288 | tf_op jit(solution)/shard_map/ppermute | solution.py:443
  70.0 6.2 %collective-permute-start.16 = (bf16[320,384]{1,0:T(8,128)(2,1)S(1)}, bf16[320,384]{1,0:T(8,128)(2,1)S(1)}, u32[]{:S(2)}, u32[]{:S(2)}) collective-permute-start(bf16[320,384]{1,0:T(8,128)(2,1)S(1)} %get-tuple-element.75), channel_id=1, source_target_pairs={{0,4},{1,5},{2,6},{3,7},{4,0},{5,1},{6,2},{7,3},{8,12},{9,13},{10,... | collective-permute-start | bytes 737288 | tf_op jit(solution)/shard_map/ppermute | solution.py:443
  71.5 6.2 %collective-permute-start.17 = (bf16[2,320,384]{2,1,0:T(8,128)(2,1)S(1)}, bf16[2,320,384]{2,1,0:T(8,128)(2,1)S(1)}, u32[]{:S(2)}, u32[]{:S(2)}) collective-permute-start(bf16[2,320,384]{2,1,0:T(8,128)(2,1)S(1)} %get-tuple-element.73.early), channel_id=1, source_target_pairs={{0,1},{1,0},{2,3},{3,2},{4,5},{5,4},{6,7},{7,6},{8,9},{9,8},{10,11... | collective-permute-start | bytes 1474568 | tf_op jit(solution)/shard_map/ppermute | solution.py:443
  74.8 1.7 %collective-permute-start.18 = (bf16[320,384]{1,0:T(8,128)(2,1)S(1)}, bf16[320,384]{1,0:T(8,128)(2,1)S(1)}, u32[]{:S(2)}, u32[]{:S(2)}) collective-permute-start(bf16[320,384]{1,0:T(8,128)(2,1)S(1)} %collective-permute-done.15.a_late), channel_id=1, source_target_pairs={{0,1},{1,0},{2,3},{3,2},{4,5},{5,4},{6,7},{7,6},{8,9},{9,8},{10,11... | collective-permute-start | bytes 737288 | tf_op jit(solution)/shard_map/ppermute | solution.py:443
  76.2 1.5 %collective-permute-start.19 = (bf16[320,384]{1,0:T(8,128)(2,1)S(1)}, bf16[320,384]{1,0:T(8,128)(2,1)S(1)}, u32[]{:S(2)}, u32[]{:S(2)}) collective-permute-start(bf16[320,384]{1,0:T(8,128)(2,1)S(1)} %collective-permute-done.16.b_late), channel_id=1, source_target_pairs={{0,1},{1,0},{2,3},{3,2},{4,5},{5,4},{6,7},{7,6},{8,9},{9,8},{10,11... | collective-permute-start | bytes 737288 | tf_op jit(solution)/shard_map/ppermute | solution.py:443

commit v3 on v2

--- a/solution.py
+++ b/solution.py
@@ -11,7 +11,8 @@
 BF = jnp.bfloat16
 F32 = jnp.float32
 HALO = 16
-VMEM_LIMIT = 48 * 1024 * 1024
+VMEM_LIMIT = 20 * 1024 * 1024
+TAPS_LIMIT = 50331648
 
 
 def dot_nn(a, b):
@@ -52,6 +53,10 @@
     return pl.BlockSpec(memory_space=pltpu.VMEM)
 
 
+def hspec():
+    return pl.BlockSpec(memory_space=pltpu.HBM)
+
+
 def sspec():
     return pl.BlockSpec(memory_space=pltpu.SMEM)
 
@@ -70,30 +75,39 @@
     return (device & 1) == 1, a_mine, b_mine
 
 
-def pack_kernel(ids_ref, seg_ref, cot_ref, right_ref, left_ref):
+def pack_kernel(row_len_ref, ids_ref, seg_ref, cot_ref, scorer_ref, right_ref, left_ref, q_ref):
     span = ids_ref.shape[1]
     width = cot_ref.shape[2]
     row = lax.broadcasted_iota(jnp.int32, (HALO, span), 0)
     ids = ids_ref[...].astype(F32)
     segs = seg_ref[...].astype(F32)
-    both = jnp.where(row == 0, ids, jnp.where(row == 1, segs, 0.0)).astype(BF)
+    length = row_len_ref[...]
+    both = jnp.where(row == 0, ids, jnp.where(row == 1, segs, 0.0))
+    size = jnp.where(row == 2, lax.shift_right_logical(length, 8), length & 255).astype(F32)
+    both = jnp.where((row == 2) | (row == 3), size, both).astype(BF)
     right_ref[...] = both
     left_ref[0:HALO] = cot_ref[0]
     left_ref[HALO : 2 * HALO, 0:span] = both
     left_ref[HALO : 2 * HALO, span:width] = jnp.zeros((HALO, width - span), BF)
-
-
-def tap_kernel(table_ref, weight_ref, scorer_ref, hi_ref, lo_ref, q_ref):
-    hi, lo = split2(dot_nn(table_ref[...], weight_ref[0]))
-    hi_ref[...] = hi
-    lo_ref[...] = lo
-
-    @pl.when(pl.program_id(0) == 0)
-    def _():
-        s1, s2, s3 = split3(scorer_ref[...].reshape(1, q_ref.shape[1]))
-        row = lax.broadcasted_iota(jnp.int32, q_ref.shape, 0)
-        pick = jnp.where(row == 0, s1.astype(F32), jnp.where(row == 1, s2.astype(F32), s3.astype(F32)))
-        q_ref[...] = jnp.where(row < 3, pick, 0.0).astype(BF)
+    s1, s2, s3 = split3(scorer_ref[...].reshape(1, width))
+    row = lax.broadcasted_iota(jnp.int32, q_ref.shape, 0)
+    pick = jnp.where(row == 0, s1.astype(F32), jnp.where(row == 1, s2.astype(F32), s3.astype(F32)))
+    q_ref[...] = jnp.where(row < 3, pick, 0.0).astype(BF)
+
+
+def tap_kernel(table_hbm, weight_hbm, hi_ref, lo_ref, table_ref, weight_ref, sem):
+    taps = weight_ref.shape[0]
+    vocab = table_ref.shape[0]
+    copies = [pltpu.make_async_copy(weight_hbm.at[k], weight_ref.at[k], sem.at[k]) for k in range(taps)]
+    copies.insert(0, pltpu.make_async_copy(table_hbm, table_ref, sem.at[taps]))
+    for copy in copies:
+        copy.start()
+    copies[0].wait()
+    for k in range(taps):
+        copies[1 + k].wait()
+        hi, lo = split2(dot_nn(table_ref[...], weight_ref[k]))
+        hi_ref[k * vocab : (k + 1) * vocab] = hi
+        lo_ref[k * vocab : (k + 1) * vocab] = lo
 
 
 def roll(v, by):
@@ -102,8 +116,8 @@
 
 
 def local_kernel(
-    row_len_ref, calib_ref, ids_ref, seg_ref, from_left_ref, from_right_ref, hi_ref, lo_ref, bias_ref, cot_ref,
-    q_ref, blocks_ref, keep_ref, send_ref, ext_ref, idt_ref, y_ref, full_q_ref, oh_ref, *, seq_size, taps,
+    calib_ref, mine_ref, from_left_ref, from_right_ref, hi_ref, lo_ref, bias_ref, cot_ref,
+    q_ref, keep_ref, send_ref, ext_ref, idt_ref, band_ref, y_ref, full_q_ref, *, seq_size, taps,
 ):
     span = keep_ref.shape[0]
     width = hi_ref.shape[1]
@@ -116,31 +130,43 @@
     upper = place(seq_size, 1, 1)[0]
     spare = lax.broadcasted_iota(jnp.int32, (1, lanes - span), 1)
 
-    def line_up(own, at):
+    mine = mine_ref[...].astype(F32)
+    length = (256.0 * mine[2:3, 0:1] + mine[3:4, 0:1]).astype(jnp.int32)
+
+    def line_up(at):
         near_right = from_right_ref[HALO : 2 * HALO, 0 : lanes - span].astype(F32)[at : at + 1]
         near_left = from_left_ref[:, 2 * span - lanes : span].astype(F32)[at : at + 1]
         rest = jnp.where(spare < HALO, near_right, jnp.where(spare >= lanes - span - HALO, near_left, 0.0))
-        return jnp.concatenate([own.astype(F32), rest], axis=1)
+        return jnp.concatenate([mine[at : at + 1], rest], axis=1)
 
     pos = lax.broadcasted_iota(jnp.int32, (1, lanes), 1)
     own = jnp.where(pos < span, 1.0, 0.0)
     place_in_row = lax.axis_index("seq") * span + jnp.where(pos < front, pos, pos - lanes)
     near = (pos < front) | (pos >= lanes - HALO)
-    mask = jnp.where(near & (place_in_row >= 0) & (place_in_row < row_len_ref[0]), 1.0, 0.0)
-    seg = line_up(seg_ref[...], 1)
-    known = jnp.where(mask > 0.5, line_up(ids_ref[...], 0), -1.0)
-    value = lax.broadcasted_iota(jnp.int32, (vocab, 1), 0).astype(F32)
+    mask = jnp.where(near & (place_in_row >= 0) & (place_in_row < length), 1.0, 0.0)
+    seg = line_up(1)
+    known = jnp.where(mask > 0.5, line_up(0), -1.0)
     row16 = lax.broadcasted_iota(jnp.int32, (16, span // 2), 0)
+    row8 = lax.broadcasted_iota(jnp.int32, (8, lanes), 0)
     idt = jnp.zeros((16, span // 2), F32)
+    by_tap = jnp.zeros((8, lanes), F32)
     for k in range(taps):
         moved = roll(known, taps - 1 - k)
-        oh_ref[k * vocab : (k + 1) * vocab] = jnp.where(moved == value, 1.0, 0.0).astype(BF)
+        by_tap = jnp.where(row8 == k, moved, by_tap)
         for i in range(2):
             idt = jnp.where(row16 == 2 * k + i, moved[:, i * (span // 2) : (i + 1) * (span // 2)], idt)
     idt = idt.astype(BF)
     idt_ref[...] = idt
-    y = dot_tn(oh_ref[...], hi_ref[...]) + dot_tn(oh_ref[...], lo_ref[...])
-    y_ref[...] = (y + bias_ref[...].reshape(1, width)).astype(BF)
+    column = jnp.transpose(by_tap)
+    column = jnp.concatenate([column[0:front], column[lanes - HALO : lanes]], axis=0)
+    value = lax.broadcasted_iota(jnp.int32, (front + HALO, vocab), 1).astype(F32)
+    one_hot = [jnp.where(column[:, k : k + 1] == value, 1.0, 0.0).astype(BF) for k in range(taps)]
+    one_hot = jnp.concatenate(one_hot, axis=1)
+    y = dot_nn(one_hot, hi_ref[...]) + dot_nn(one_hot, lo_ref[...])
+    y = (y + bias_ref[...].reshape(1, width)).astype(BF)
+    y_ref[0:front] = y[0:front]
+    y_ref[front : lanes - HALO] = jnp.zeros((lanes - HALO - front, width), BF)
+    y_ref[lanes - HALO : lanes] = y[front : front + HALO]
     full_q_ref[0:own_blocks] = cot_ref[0]
     full_q_ref[own_blocks : own_blocks + HALO] = from_right_ref[0:HALO]
     full_q_ref[own_blocks + HALO : own_blocks + 2 * HALO] = q_ref[...]
@@ -202,8 +228,8 @@
     for d in range(sizes):
         band = band + jnp.where(match[d], 0.5 * roll(alpha[d], -d), 0.0)
     band_hi, band_lo = split2(band)
-    mixed = dot_nn(band_hi[0:own_blocks], y_ref[...]) + dot_nn(band_lo[0:own_blocks], y_ref[...])
-    blocks_ref[0] = mixed.astype(BF)
+    band_ref[0] = band_hi[0:own_blocks]
+    band_ref[1] = band_lo[0:own_blocks]
     dy = dot_tn(band_hi[:, 0:span], full_q_ref[...]) + dot_tn(band_lo[:, 0:span], full_q_ref[...])
     dy = dy.astype(BF)
     left, right = dy[:, 0:half], dy[:, half:width]
@@ -211,11 +237,11 @@
     send_ref[0:span] = jnp.where(upper, left, right)
     grad_bias = jnp.sum(dy.astype(F32), axis=0, keepdims=True)
 
-    row8 = lax.broadcasted_iota(jnp.int32, (16, lanes), 0)
+    row16 = lax.broadcasted_iota(jnp.int32, (16, lanes), 0)
     stack = jnp.zeros((16, lanes), F32)
     pieces = split3(rhos[0]) + split3(rhos[1]) + split3(gammas[1] * own)
     for i, piece in enumerate(pieces):
-        stack = jnp.where(row8 == i, piece.astype(F32), stack)
+        stack = jnp.where(row16 == i, piece.astype(F32), stack)
     stack = stack.astype(BF)
     by_y = dot_nn(stack, y_ref[...])
     grad_scorer = [by_y[3 * i : 3 * i + 1] + by_y[3 * i + 1 : 3 * i + 2] + by_y[3 * i + 2 : 3 * i + 3] for i in range(2)]
@@ -223,10 +249,11 @@
     for i, row in enumerate(grad_scorer + [grad_bias]):
         ext_ref[2 * i : 2 * i + 1] = row[:, 0:half]
         ext_ref[2 * i + 1 : 2 * i + 2] = row[:, half:width]
-    by_tap = dot_nt(stack, oh_ref[...])
+    by_tap = dot_nn(stack[:, 0:span], one_hot[0:span])
     by_tap = by_tap[6:7] + by_tap[7:8] + by_tap[8:9]
-    for k in range(taps):
-        ext_ref[6 + k : 7 + k, 0:vocab] = by_tap[:, k * vocab : (k + 1) * vocab]
+    by_tap = jnp.concatenate([by_tap, jnp.zeros((1, 4 * half - taps * vocab), F32)], axis=1)
+    for i in range(4):
+        ext_ref[6 + i : 7 + i] = by_tap[:, i * half : (i + 1) * half]
     spot = lax.broadcasted_iota(jnp.int32, (1, half), 1)
     misc = jnp.zeros((1, half), F32)
     sums = [calibs[i][b][c] for i in range(2) for b in range(sizes) for c in range(sizes)]
@@ -235,21 +262,26 @@
     sums.append(jnp.sum(own * gammas[1], axis=1, keepdims=True))
     for i, one in enumerate(sums):
         misc = jnp.where(spot == i, one, misc)
-    ext_ref[11:12] = misc
+    ext_ref[10:11] = misc
     send_ref[span : span + 16] = coded(ext_ref[...])
     send_ref[span + 16 : span + 32] = jnp.concatenate([idt, jnp.zeros((16, half - idt.shape[1]), BF)], axis=1)
 
 
+def mix_kernel(band_ref, y_ref, blocks_ref, token_ref):
+    blocks_ref[0] = (dot_nn(band_ref[0], y_ref[...]) + dot_nn(band_ref[1], y_ref[...])).astype(BF)
+    token_ref[...] = jnp.zeros(token_ref.shape, F32)
+
+
 def coded(ext):
     hi = ext.astype(BF).astype(F32)
-    row = lax.broadcasted_iota(jnp.int32, ext.shape, 0)
-    return jnp.where(row == 12, ext[11:12] - hi[11:12], hi).astype(BF)
+    lo = ext - hi
+    return jnp.concatenate([hi[0:11], lo[0:2], lo[4:6], lo[10:11]], axis=0).astype(BF)
 
 
 def decoded(code):
-    wide = code.astype(F32)
-    row = lax.broadcasted_iota(jnp.int32, wide.shape, 0)
-    return wide + jnp.where(row == 11, wide[12:13], 0.0)
+    w = code.astype(F32)
+    rows = [w[0:2] + w[11:13], w[2:4], w[4:6] + w[13:15], w[6:10], w[10:11] + w[15:16], jnp.zeros((5, w.shape[1]), F32)]
+    return jnp.concatenate(rows, axis=0)
 
 
 def joined(ext_ref):
@@ -291,7 +323,8 @@
     a_send[taps * quarter : taps * quarter + 16] = coded(ext)
 
 
-def second_kernel(a_in, b_in, a_got, b_got, ext_ref, a_keep, a_send, b_keep, b_send, ext_out):
+def second_kernel(a_in, b_in, a_got, b_got, ext_ref, mixed_ref, order_ref, a_keep, a_send, b_keep, b_send, ext_out):
+    del mixed_ref, order_ref
     taps, rows, _ = a_in.shape
     part = rows // 2
     for src, got, keep, send in ((a_in, a_got, a_keep, a_send), (b_in, b_got, b_keep, b_send)):
@@ -341,13 +374,15 @@
     ext = tree_sum([joined(ext_ref)] + [pair(g, size) for g in gots])
     total = tree_sum([keep[...]] + [g[0:size].astype(F32) for g in gots])
     spot = lax.broadcasted_iota(jnp.int32, (1, half), 1)
-    misc = ext[11:12]
+    misc = ext[10:11]
+    by_tap = jnp.concatenate([ext[i : i + 1] for i in range(6, 10)], axis=1)
 
     def one(i):
         return jnp.sum(jnp.where(spot == i, misc, 0.0), axis=1, keepdims=True)
 
     count = one(33)
-    scorer = scorer_ref[...].reshape(1, 2 * half)
+    scorer = scorer_ref[...].astype(F32)
+    scorer = scorer[0:1] + scorer[1:2] + scorer[2:3]
     mine = jnp.where(upper, scorer[:, half:], scorer[:, :half])
     step = lax.broadcasted_iota(jnp.int32, (part, vocab), 0)
     lane = lax.broadcasted_iota(jnp.int32, (part, vocab), 1)
@@ -355,7 +390,7 @@
     for g in range(2):
         hit = lane == step + (a_mine if g == 0 else vocab // 2 + b_mine)
         for k in range(taps):
-            column = jnp.sum(jnp.where(hit, ext[6 + k : 7 + k, 0:vocab], 0.0), axis=1, keepdims=True)
+            column = jnp.sum(jnp.where(hit, by_tap[:, k * vocab : (k + 1) * vocab], 0.0), axis=1, keepdims=True)
             at = (g * taps + k) * part
             pieces.append(total[at : at + part] - (column / count) * mine)
     shard[...] = jnp.concatenate(pieces, axis=0).astype(BF)
@@ -395,8 +430,9 @@
                 early_ref[g, first : first + rows] = piece
 
 
-def order_kernel(table_ref, after_ref, out_ref, *, seq_size, part):
+def order_kernel(table_ref, after_ref, out_ref, token_ref, *, seq_size, part):
     del after_ref
+    token_ref[...] = jnp.zeros(token_ref.shape, F32)
     vocab = table_ref.shape[0]
     _, a_mine, b_mine = place(seq_size, vocab // 4, part)
     value = local_value((1, vocab), 1, a_mine, b_mine, vocab)
@@ -424,8 +460,8 @@
         rows.append(rows_of(k))
         buffer[k] = dot_nn(table_t_ref[...], rows[k])
         pltpu.make_async_copy(buffer.at[k], conv_ref.at[k], sem.at[k]).start()
-    acc = dot_nt(rows[0], weight_ref[0])
-    for k in range(1, taps):
+    acc = 0.0
+    for k in range(taps):
         acc = acc + dot_nt(rows[k], weight_ref[k])
     for at in range(0, vocab, part):
         to = (at ^ a_mine) if at < vocab // 2 else vocab // 2 + ((at - vocab // 2) ^ b_mine)
@@ -461,57 +497,56 @@
     size = 2 * taps * part
     lanes = span + 128
 
-    to_right, to_left = pl.pallas_call(
+    to_right, to_left, q_rows = pl.pallas_call(
         pack_kernel,
-        out_shape=(shape((HALO, span), BF), shape((2 * HALO, width), BF)),
+        out_shape=(shape((HALO, span), BF), shape((2 * HALO, width), BF), shape((16, width), BF)),
         grid=(1,),
         in_specs=[
+            pl.BlockSpec((1, 1), lambda i: (0, 0)),
             pl.BlockSpec((1, span), lambda i: (0, 0)),
             pl.BlockSpec((1, span), lambda i: (0, 0)),
             pl.BlockSpec((1, HALO, width), lambda i: (0, 0, 0)),
+            pl.BlockSpec((width,), lambda i: (0,)),
         ],
-        out_specs=(pl.BlockSpec((HALO, span), lambda i: (0, 0)), pl.BlockSpec((2 * HALO, width), lambda i: (0, 0))),
+        out_specs=(
+            pl.BlockSpec((HALO, span), lambda i: (0, 0)),
+            pl.BlockSpec((2 * HALO, width), lambda i: (0, 0)),
+            pl.BlockSpec((16, width), lambda i: (0, 0)),
+        ),
         name="pack",
-    )(byte_ids, seg_ids, cotangent)
+    )(row_len.reshape(1, 1), byte_ids, seg_ids, cotangent, scorer)
     from_left = neighbour(to_right, "seq", 1)
     from_right = neighbour(to_left, "seq", -1)
 
-    hi, lo, q_rows = pl.pallas_call(
+    hi, lo = pl.pallas_call(
         tap_kernel,
-        out_shape=(shape((taps * vocab, width), BF), shape((taps * vocab, width), BF), shape((16, width), BF)),
-        grid=(taps,),
-        in_specs=[
-            pl.BlockSpec((vocab, width), lambda k: (0, 0)),
-            pl.BlockSpec((1, width, width), lambda k: (k, 0, 0)),
-            pl.BlockSpec((width,), lambda k: (0,)),
+        out_shape=(shape((taps * vocab, width), BF),) * 2,
+        name="taps",
+        in_specs=[hspec()] * 2,
+        out_specs=(vspec(),) * 2,
+        scratch_shapes=[
+            pltpu.VMEM((vocab, width), BF),
+            pltpu.VMEM((taps, width, width), BF),
+            pltpu.SemaphoreType.DMA((taps + 1,)),
         ],
-        out_specs=(
-            pl.BlockSpec((vocab, width), lambda k: (k, 0)),
-            pl.BlockSpec((vocab, width), lambda k: (k, 0)),
-            pl.BlockSpec((16, width), lambda k: (0, 0)),
-        ),
-        name="taps",
-        compiler_params=pltpu.CompilerParams(vmem_limit_bytes=VMEM_LIMIT),
-    )(embed_table, conv_weight, scorer)
-
-    blocks, keep, send, ext, idt = call(
+        compiler_params=pltpu.CompilerParams(vmem_limit_bytes=TAPS_LIMIT),
+    )(embed_table, conv_weight)
+
+    keep, send, ext, idt, band, y = call(
         functools.partial(local_kernel, seq_size=seq_size, taps=taps),
         (
-            shape((1, span // 2, width), BF),
             shape((span, half), BF),
             shape((span + 32, half), BF),
             shape((16, half), F32),
             shape((16, span // 2), BF),
+            shape((2, span // 2, lanes), BF),
+            shape((lanes, width), BF),
         ),
         "local",
-        in_specs=[sspec(), sspec()] + [vspec()] * 9,
-        out_specs=(vspec(),) * 5,
-        scratch_shapes=[
-            pltpu.VMEM((lanes, width), BF),
-            pltpu.VMEM((span // 2 + 2 * HALO, width), BF),
-            pltpu.VMEM((taps * vocab, lanes), BF),
-        ],
-    )(row_len, calibration, byte_ids, seg_ids, from_left, from_right, hi, lo, conv_bias, cotangent, q_rows)
+        in_specs=[sspec()] + [vspec()] * 8,
+        out_specs=(vspec(),) * 6,
+        scratch_shapes=[pltpu.VMEM((span // 2 + 2 * HALO, width), BF)],
+    )(calibration, to_right, from_left, from_right, hi, lo, conv_bias, cotangent, q_rows)
 
     got = swap(send, 1, count)
     a_keep, a_send, b_keep, b_send, ext = call(
@@ -527,12 +562,20 @@
         in_specs=[vspec()] * 4,
         out_specs=(vspec(),) * 5,
     )(keep, idt, got, ext)
-    table_t = call(
+    token = shape((8, 128), F32)
+    blocks, mixed = call(
+        mix_kernel,
+        (shape((1, span // 2, width), BF), token),
+        "mix",
+        in_specs=[vspec()] * 2,
+        out_specs=(vspec(),) * 2,
+    )(band, y)
+    table_t, ordered = call(
         functools.partial(order_kernel, seq_size=seq_size, part=part),
-        shape((width, vocab), BF),
+        (shape((width, vocab), BF), token),
         "order",
         in_specs=[vspec()] * 2,
-        out_specs=vspec(),
+        out_specs=(vspec(),) * 2,
     )(embed_table, ext)
 
     a_got, b_got = swap(a_send, 2, count), swap(b_send, 4, count)
@@ -546,9 +589,9 @@
             shape((16, half), F32),
         ),
         "second",
-        in_specs=[vspec()] * 5,
+        in_specs=[vspec()] * 7,
         out_specs=(vspec(),) * 5,
-    )(a_keep, b_keep, a_got, b_got, ext)
+    )(a_keep, b_keep, a_got, b_got, ext, mixed, ordered)
 
     a_got, b_got = swap(a_send, 4, count), swap(b_send, 2, count)
     outs = call(
@@ -566,7 +609,7 @@
         "shard",
         in_specs=[vspec()] * (3 + len(gots)),
         out_specs=(vspec(),) * 5,
-    )(mine, ext, scorer, *gots)
+    )(mine, ext, q_rows, *gots)
 
     gathered = [shard] + [swap(shard, 8 * t, count) for t in range(1, depth)]
     a_out, b_out = call(
@@ -588,15 +631,18 @@
     far_early = swap(early, 1, count)
     far_a, far_b = swap(a_late, 1, count), swap(b_late, 1, count)
 
-    conv, table = call(
+    conv, grad_table = call(
         functools.partial(final_kernel, seq_size=seq_size, part=part),
         (shape((taps, width, width), F32), shape((vocab, width), F32)),
         "final",
         in_specs=[vspec()] * 8,
-        out_specs=(pl.BlockSpec(memory_space=pl.ANY), vspec()),
-        scratch_shapes=[pltpu.VMEM((taps, width, width), F32), pltpu.SemaphoreType.DMA((taps,))],
+        out_specs=(hspec(), vspec()),
+        scratch_shapes=[
+            pltpu.VMEM((taps, width, width), F32),
+            pltpu.SemaphoreType.DMA((taps,)),
+        ],
     )(early, a_late, b_late, far_early, far_a, far_b, table_t, conv_weight)
-    return (blocks, loss.reshape(()), table, conv, grad_bias, grad_scorer, grad_calib)
+    return (blocks, loss.reshape(()), grad_table, conv, grad_bias, grad_scorer, grad_calib)
 
 
 def solution(mesh):

time: 86.9 us -> 81.5 us (0.938)
  Pallas kernels: 26.5 us -> 23.5 us
  waiting for transfers between devices: 30.7 us -> 29.1 us
    pallas_call x1, Pallas kernels: 8.79 us -> 6.1 us  [body(): call(functools.partial(final_kernel, seq_size=seq_size, part=part), (shap...]
    ppermute x18, waiting for transfers between devices: 30.7 us -> 29.1 us  [swap(): return lax.ppermute(shard, AXES, [(i, i ^ flip) for i in range(count)])]
    pallas_call x1, Pallas kernels: 8.11 us -> 7.1 us  [body(): call(functools.partial(local_kernel, seq_size=seq_size, taps=taps), (shap...]
    pallas_call x2 -> x3, Pallas kernels: 5.66 us -> 6.22 us  [the longest x1 4.4 us: body(): pl.pallas_call(tap_kernel, out_shape=(shape((taps * vocab, width), BF),)...]
  transfers between devices with their start and end apart: 20 -> 20, of which waited for: 13 -> 14; matrix products, arithmetic and copies ran while one was open for 0% -> 0% of each run, Pallas kernels for 7% -> 8%
where the time goes in v3:
time: 81.5 us; the launch traced here: 81.3 us
  waiting for transfers between devices  29.1 us (36%)
  starting transfers between devices  26.1 us (32%)
  Pallas kernels  23.5 us (29%)
  between operations  1.51 us (2%)
  local copies, waits for them, and re-layouts  1.02 us (1%)
    ppermute x18, waiting for transfers between devices, swap(): return lax.ppermute(shard, AXES, [(i, i ^ flip) for i in range(count)])  29.1 us
    ppermute x18, starting transfers between devices, swap(): return lax.ppermute(shard, AXES, [(i, i ^ flip) for i in range(count)])  21.8 us
    pallas_call x1, Pallas kernels, body(): call(functools.partial(local_kernel, seq_size=seq_size, taps=taps), (shap...  7.1 us
    pallas_call x1, Pallas kernels, body(): call(functools.partial(final_kernel, seq_size=seq_size, part=part), (shap...  6.1 us
    pallas_call x1, Pallas kernels, body(): pl.pallas_call(tap_kernel, out_shape=(shape((taps * vocab, width), BF),)...  4.4 us
    ppermute x2, starting transfers between devices, neighbour(): lax.ppermute(shard, axis, [(i, i + by) for i in range(length) if 0 <= i +...  4.31 us
  transfers between devices with their start and end apart: 20, of which 14 were waited for; matrix products, arithmetic and copies ran while one was open for 0% of the time, Pallas kernels for 8%

profile of v3, /device:TPU:0, one launch (start us, length us, event | category | flops | bytes accessed | tf_op | source)
XLA Modules:
  0.0 81.3 jit_solution(7196507266317546643)
XLA Ops:
  1.4 1.5 %pack.1 = (bf16[16,512]{1,0:T(8,128)(2,1)}, bf16[32,768]{1,0:T(8,128)(2,1)}, bf16[16,768]{1,0:T(8,128)(2,1)}) custom-call(s32[1,1]{1,0:T(1,128)} %bitcast.2.row_len_ref, s32[1,512]{1,0:T(1,128)} %ids_ref.1, s32[1,512]{1,0:T(1,128)} %seg_ref.1, bf16[1,256,768]{2,1,0:T(8,128)(2,1)} %cot_ref.3, f32[768]{0:T(1024)} %scorer_ref.1), custom_call_target="tpu_custom_call" | custom-call | tf_op jit(solution)/shard_map/pack/pallas_call | solution.py:500
  2.8 1.3 %collective-permute-start.1 = (bf16[32,768]{1,0:T(8,128)(2,1)}, bf16[32,768]{1,0:T(8,128)(2,1)S(1)}, u32[]{:S(2)}, u32[]{:S(2)}) collective-permute-start(bf16[32,768]{1,0:T(8,128)(2,1)} %get-tuple-element.50), channel_id=1, source_target_pairs={{1,0},{2,1},{3,2},{5,4},{6,5},{7,6},{9,8},{10,9},{11,10},{13,12},{... | collective-permute-start | bytes 147464 | tf_op jit(solution)/shard_map/ppermute | solution.py:475
  4.1 3.0 %collective-permute-start = (bf16[16,512]{1,0:T(8,128)(2,1)}, bf16[16,512]{1,0:T(8,128)(2,1)S(1)}, u32[]{:S(2)}, u32[]{:S(2)}) collective-permute-start(bf16[16,512]{1,0:T(8,128)(2,1)} %get-tuple-element.49.mine_ref), channel_id=1, source_target_pairs={{0,1},{1,2},{2,3},{4,5},{5,6},{6,7},{8,9},{9,10},{10,11},{12,13},{... | collective-permute-start | bytes 49160 | tf_op jit(solution)/shard_map/ppermute | solution.py:475
  7.2 1.0 %copy-done.1 = bf16[256,768]{1,0:T(8,128)(2,1)S(1)} copy-done((bf16[256,768]{1,0:T(8,128)(2,1)S(1)}, bf16[256,768]{1,0:T(8,128)(2,1)}, u32[]{:S(2)}) %copy-start.1) | copy-done | bytes 393240
  8.2 4.4 %taps.1 = (bf16[1280,768]{1,0:T(8,128)(2,1)S(1)}, bf16[1280,768]{1,0:T(8,128)(2,1)S(1)}) custom-call(bf16[256,768]{1,0:T(8,128)(2,1)S(1)} %copy-done.1, bf16[5,768,768]{2,1,0:T(8,128)(2,1)} %weight_ref.1), custom_call_target="tpu_custom_call" | custom-call | tf_op jit(solution)/shard_map/taps/pallas_call | solution.py:521
  12.7 7.1 %local.1 = (bf16[512,384]{1,0:T(8,128)(2,1)S(1)}, bf16[544,384]{1,0:T(8,128)(2,1)S(1)}, f32[16,384]{1,0:T(8,128)S(1)}, bf16[16,256]{1,0:T(8,128)(2,1)S(1)}, bf16...) custom-call(f32[4,4]{1,0:T(4,128)S(1)} %copy-done.5, bf16[16,512]{1,0:T(8,128)(2,1)S(1)} %copy-done.3, ...), custom_call_target="tpu_custom_call" | custom-call | tf_op jit(solution)/shard_map/local/pallas_call | solution.py:535
  19.8 2.7 %collective-permute-start.2 = (bf16[544,384]{1,0:T(8,128)(2,1)S(1)}, bf16[544,384]{1,0:T(8,128)(2,1)S(1)}, u32[]{:S(2)}, u32[]{:S(2)}) collective-permute-start(bf16[544,384]{1,0:T(8,128)(2,1)S(1)} %get-tuple-element.59), channel_id=1, source_target_pairs={{0,1},{1,0},{2,3},{3,2},{4,5},{5,4},{6,7},{7,6},{8,9},{9,8},{10,11... | collective-permute-start | bytes 1253384 | tf_op jit(solution)/shard_map/ppermute | solution.py:479
  22.4 1.4 %collective-permute-done.2.got_ref = bf16[544,384]{1,0:T(8,128)(2,1)S(1)} collective-permute-done((bf16[544,384]{1,0:T(8,128)(2,1)S(1)}, bf16[544,384]{1,0:T(8,128)(2,1)S(1)}, u32[]{:S(2)}, u32[]{:S(2)}) %collective-permute-start.2) | collective-permute-done | bytes 417824 | tf_op jit(solution)/shard_map/ppermute | solution.py:479
  23.8 1.5 %by_value.1 = (f32[5,64,384]{2,1,0:T(8,128)S(1)}, bf16[336,384]{1,0:T(8,128)(2,1)S(1)}, f32[5,64,384]{2,1,0:T(8,128)S(1)}, bf16[320,384]{1,0:T(8,128)(2,1)S(1)}, f32[16,384]{1,0:T(8,128)S(1)}) custom-call(bf16[512,384]{1,0:T(8,128)(2,1)S(1)} %get-tuple-element.57.keep_ref, bf16[16,256]{1,0:T(8,128)(2,1)S(1)} %get-tuple-element.58.idt_ref, ...), custom_call_target="tpu_custom_call" | custom-call | tf_op jit(solution)/shard_map/by_value/pallas_call | solution.py:552
  26.2 1.5 %collective-permute-start.4 = (bf16[320,384]{1,0:T(8,128)(2,1)S(1)}, bf16[320,384]{1,0:T(8,128)(2,1)S(1)}, u32[]{:S(2)}, u32[]{:S(2)}) collective-permute-start(bf16[320,384]{1,0:T(8,128)(2,1)S(1)} %get-tuple-element.64), channel_id=1, source_target_pairs={{0,4},{1,5},{2,6},{3,7},{4,0},{5,1},{6,2},{7,3},{8,12},{9,13},{10,... | collective-permute-start | bytes 737288 | tf_op jit(solution)/shard_map/ppermute | solution.py:479
  27.7 1.5 %mix.1 = (bf16[1,256,768]{2,1,0:T(8,128)(2,1)}, f32[8,128]{1,0:T(8,128)S(1)}) custom-call(bf16[2,256,640]{2,1,0:T(8,128)(2,1)S(1)} %get-tuple-element.54.band_ref, bf16[640,768]{1,0:T(8,128)(2,1)S(1)} %get-tuple-element.55.y_ref), custom_call_target="tpu_custom_call" | custom-call | tf_op jit(solution)/shard_map/mix/pallas_call | solution.py:566
  29.5 4.4 %collective-permute-done.4.b_got = bf16[320,384]{1,0:T(8,128)(2,1)S(1)} collective-permute-done((bf16[320,384]{1,0:T(8,128)(2,1)S(1)}, bf16[320,384]{1,0:T(8,128)(2,1)S(1)}, u32[]{:S(2)}, u32[]{:S(2)}) %collective-permute-start.4) | collective-permute-done | bytes 245792 | tf_op jit(solution)/shard_map/ppermute | solution.py:479
  34.0 1.6 %collective-permute-start.5 = (bf16[176,384]{1,0:T(8,128)(2,1)S(1)}, bf16[176,384]{1,0:T(8,128)(2,1)S(1)}, u32[]{:S(2)}, u32[]{:S(2)}) collective-permute-start(bf16[176,384]{1,0:T(8,128)(2,1)S(1)} %get-tuple-element.70), channel_id=1, source_target_pairs={{0,4},{1,5},{2,6},{3,7},{4,0},{5,1},{6,2},{7,3},{8,12},{9,13},{10,... | collective-permute-start | bytes 405512 | tf_op jit(solution)/shard_map/ppermute | solution.py:479
  35.6 1.5 %collective-permute-start.6 = (bf16[160,384]{1,0:T(8,128)(2,1)S(1)}, bf16[160,384]{1,0:T(8,128)(2,1)S(1)}, u32[]{:S(2)}, u32[]{:S(2)}) collective-permute-start(bf16[160,384]{1,0:T(8,128)(2,1)S(1)} %get-tuple-element.71), channel_id=1, source_target_pairs={{0,2},{1,3},{2,0},{3,1},{4,6},{5,7},{6,4},{7,5},{8,10},{9,11},{10,... | collective-permute-start | bytes 368648 | tf_op jit(solution)/shard_map/ppermute | solution.py:479
  37.1 3.4 %collective-permute-done.6.b_got = bf16[160,384]{1,0:T(8,128)(2,1)S(1)} collective-permute-done((bf16[160,384]{1,0:T(8,128)(2,1)S(1)}, bf16[160,384]{1,0:T(8,128)(2,1)S(1)}, u32[]{:S(2)}, u32[]{:S(2)}) %collective-permute-start.6) | collective-permute-done | bytes 122912 | tf_op jit(solution)/shard_map/ppermute | solution.py:479
  40.6 1.6 %collective-permute-start.7 = (bf16[96,384]{1,0:T(8,128)(2,1)S(1)}, bf16[96,384]{1,0:T(8,128)(2,1)S(1)}, u32[]{:S(2)}, u32[]{:S(2)}) collective-permute-start(bf16[96,384]{1,0:T(8,128)(2,1)S(1)} %get-tuple-element.75), channel_id=1, source_target_pairs={{0,8},{1,9},{2,10},{3,11},{4,12},{5,13},{6,14},{7,15},{8,0},{9,1},... | collective-permute-start | bytes 221192 | tf_op jit(solution)/shard_map/ppermute | solution.py:479
  42.2 2.6 %collective-permute-start.8 = (bf16[96,384]{1,0:T(8,128)(2,1)S(1)}, bf16[96,384]{1,0:T(8,128)(2,1)S(1)}, u32[]{:S(2)}, u32[]{:S(2)}) collective-permute-start(bf16[96,384]{1,0:T(8,128)(2,1)S(1)} %get-tuple-element.76), channel_id=1, source_target_pairs={{0,16},{1,17},{2,18},{3,19},{4,20},{5,21},{6,22},{7,23},{8,24},{9,... | collective-permute-start | bytes 221192 | tf_op jit(solution)/shard_map/ppermute | solution.py:479
  45.3 3.7 %collective-permute-done.8.refs_1_ = bf16[96,384]{1,0:T(8,128)(2,1)S(1)} collective-permute-done((bf16[96,384]{1,0:T(8,128)(2,1)S(1)}, bf16[96,384]{1,0:T(8,128)(2,1)S(1)}, u32[]{:S(2)}, u32[]{:S(2)}) %collective-permute-start.8) | collective-permute-done | bytes 73760 | tf_op jit(solution)/shard_map/ppermute | solution.py:479
  49.0 2.0 %collective-permute-done.9.refs_2_ = bf16[96,384]{1,0:T(8,128)(2,1)S(1)} collective-permute-done((bf16[96,384]{1,0:T(8,128)(2,1)S(1)}, bf16[96,384]{1,0:T(8,128)(2,1)S(1)}, u32[]{:S(2)}, u32[]{:S(2)}) %collective-permute-start.9) | collective-permute-done | bytes 73760 | tf_op jit(solution)/shard_map/ppermute | solution.py:479
  51.8 1.1 %collective-permute-start.12 = (bf16[80,384]{1,0:T(8,128)(2,1)S(1)}, bf16[80,384]{1,0:T(8,128)(2,1)S(1)}, u32[]{:S(2)}, u32[]{:S(2)}) collective-permute-start(bf16[80,384]{1,0:T(8,128)(2,1)S(1)} %get-tuple-element.79.refs_0_), channel_id=1, source_target_pairs={{0,24},{1,25},{2,26},{3,27},{4,28},{5,29},{6,30},{7,31},{8,16},{9,... | collective-permute-start | bytes 184328 | tf_op jit(solution)/shard_map/ppermute | solution.py:479
  53.3 2.9 %collective-permute-start.10 = (bf16[80,384]{1,0:T(8,128)(2,1)S(1)}, bf16[80,384]{1,0:T(8,128)(2,1)S(1)}, u32[]{:S(2)}, u32[]{:S(2)}) collective-permute-start(bf16[80,384]{1,0:T(8,128)(2,1)S(1)} %get-tuple-element.79.refs_0_), channel_id=1, source_target_pairs={{0,8},{1,9},{2,10},{3,11},{4,12},{5,13},{6,14},{7,15},{8,0},{9,1},... | collective-permute-start | bytes 184328 | tf_op jit(solution)/shard_map/ppermute | solution.py:479
  56.2 1.7 %collective-permute-done.12.refs_3_ = bf16[80,384]{1,0:T(8,128)(2,1)S(1)} collective-permute-done((bf16[80,384]{1,0:T(8,128)(2,1)S(1)}, bf16[80,384]{1,0:T(8,128)(2,1)S(1)}, u32[]{:S(2)}, u32[]{:S(2)}) %collective-permute-start.12) | collective-permute-done | bytes 61472 | tf_op jit(solution)/shard_map/ppermute | solution.py:479
  57.9 1.3 %collective-permute-done.11.refs_2_ = bf16[80,384]{1,0:T(8,128)(2,1)S(1)} collective-permute-done((bf16[80,384]{1,0:T(8,128)(2,1)S(1)}, bf16[80,384]{1,0:T(8,128)(2,1)S(1)}, u32[]{:S(2)}, u32[]{:S(2)}) %collective-permute-start.11) | collective-permute-done | bytes 61472 | tf_op jit(solution)/shard_map/ppermute | solution.py:479
  59.7 1.4 %collective-permute-start.14 = (bf16[160,384]{1,0:T(8,128)(2,1)S(1)}, bf16[160,384]{1,0:T(8,128)(2,1)S(1)}, u32[]{:S(2)}, u32[]{:S(2)}) collective-permute-start(bf16[160,384]{1,0:T(8,128)(2,1)S(1)} %get-tuple-element.81.b_ref), channel_id=1, source_target_pairs={{0,2},{1,3},{2,0},{3,1},{4,6},{5,7},{6,4},{7,5},{8,10},{9,11},{10,... | collective-permute-start | bytes 368648 | tf_op jit(solution)/shard_map/ppermute | solution.py:479
  61.1 3.9 %collective-permute-done.13.a_got = bf16[160,384]{1,0:T(8,128)(2,1)S(1)} collective-permute-done((bf16[160,384]{1,0:T(8,128)(2,1)S(1)}, bf16[160,384]{1,0:T(8,128)(2,1)S(1)}, u32[]{:S(2)}, u32[]{:S(2)}) %collective-permute-start.13) | collective-permute-done | bytes 122912 | tf_op jit(solution)/shard_map/ppermute | solution.py:479
  65.0 0.9 %collective-permute-done.14.b_got = bf16[160,384]{1,0:T(8,128)(2,1)S(1)} collective-permute-done((bf16[160,384]{1,0:T(8,128)(2,1)S(1)}, bf16[160,384]{1,0:T(8,128)(2,1)S(1)}, u32[]{:S(2)}, u32[]{:S(2)}) %collective-permute-start.14) | collective-permute-done | bytes 122912 | tf_op jit(solution)/shard_map/ppermute | solution.py:479
  66.0 1.4 %collective-permute-start.15 = (bf16[320,384]{1,0:T(8,128)(2,1)S(1)}, bf16[320,384]{1,0:T(8,128)(2,1)S(1)}, u32[]{:S(2)}, u32[]{:S(2)}) collective-permute-start(bf16[320,384]{1,0:T(8,128)(2,1)S(1)} %get-tuple-element.83), channel_id=1, source_target_pairs={{0,2},{1,3},{2,0},{3,1},{4,6},{5,7},{6,4},{7,5},{8,10},{9,11},{10,... | collective-permute-start | bytes 737288 | tf_op jit(solution)/shard_map/ppermute | solution.py:479
  67.4 1.5 %collective-permute-start.16 = (bf16[320,384]{1,0:T(8,128)(2,1)S(1)}, bf16[320,384]{1,0:T(8,128)(2,1)S(1)}, u32[]{:S(2)}, u32[]{:S(2)}) collective-permute-start(bf16[320,384]{1,0:T(8,128)(2,1)S(1)} %get-tuple-element.84), channel_id=1, source_target_pairs={{0,4},{1,5},{2,6},{3,7},{4,0},{5,1},{6,2},{7,3},{8,12},{9,13},{10,... | collective-permute-start | bytes 737288 | tf_op jit(solution)/shard_map/ppermute | solution.py:479
  69.0 3.3 %collective-permute-done.15.a_late = bf16[320,384]{1,0:T(8,128)(2,1)S(1)} collective-permute-done((bf16[320,384]{1,0:T(8,128)(2,1)S(1)}, bf16[320,384]{1,0:T(8,128)(2,1)S(1)}, u32[]{:S(2)}, u32[]{:S(2)}) %collective-permute-start.15) | collective-permute-done | bytes 245792 | tf_op jit(solution)/shard_map/ppermute | solution.py:479
  72.3 1.4 %collective-permute-done.16.b_late = bf16[320,384]{1,0:T(8,128)(2,1)S(1)} collective-permute-done((bf16[320,384]{1,0:T(8,128)(2,1)S(1)}, bf16[320,384]{1,0:T(8,128)(2,1)S(1)}, u32[]{:S(2)}, u32[]{:S(2)}) %collective-permute-start.16) | collective-permute-done | bytes 245792 | tf_op jit(solution)/shard_map/ppermute | solution.py:479
  73.8 1.4 %collective-permute-done.19.far_b = bf16[320,384]{1,0:T(8,128)(2,1)S(1)} collective-permute-done((bf16[320,384]{1,0:T(8,128)(2,1)S(1)}, bf16[320,384]{1,0:T(8,128)(2,1)S(1)}, u32[]{:S(2)}, u32[]{:S(2)}) %collective-permute-start.19) | collective-permute-done | bytes 245792 | tf_op jit(solution)/shard_map/ppermute | solution.py:479
  75.2 6.1 %final.1 = (f32[5,768,768]{2,1,0:T(8,128)}, f32[256,768]{1,0:T(8,128)}) custom-call(bf16[2,320,384]{2,1,0:T(8,128)(2,1)S(1)} %get-tuple-element.82.early, bf16[320,384]{1,0:T(8,128)(2,1)S(1)} %collective-permute-done.15.a_late, bf16[320,384]{1,0:T(8,128)(2,1)S(1)} %collective-permute-done.16.b_late, ...), custom_call_target="tpu_custom_call" | custom-call | tf_op jit(solution)/shard_map/final/pallas_call | solution.py:634
  (37 shorter events, 3.9 us)
Async XLA Ops:
  0.6 12.0 %copy-start = (bf16[1,256,768]{2,1,0:T(8,128)(2,1)S(1)}, bf16[1,256,768]{2,1,0:T(8,128)(2,1)}, u32[]{:S(2)}) copy-start(bf16[1,256,768]{2,1,0:T(8,128)(2,1)} %cot_ref.3) | copy-start | bytes 1179652
  0.6 12.0 %copy-start.5 = (f32[4,4]{1,0:T(4,128)S(1)}, f32[4,4]{1,0:T(4,128)}, u32[]{:S(2)}) copy-start(f32[4,4]{1,0:T(4,128)} %calib_ref.1) | copy-start | bytes 196
  0.7 12.0 %copy-start.4 = (f32[768]{0:T(1024)S(1)}, f32[768]{0:T(1024)}, u32[]{:S(2)}) copy-start(f32[768]{0:T(1024)} %bias_ref.1) | copy-start | bytes 9220
  2.8 9.8 %collective-permute-start.1 = (bf16[32,768]{1,0:T(8,128)(2,1)}, bf16[32,768]{1,0:T(8,128)(2,1)S(1)}, u32[]{:S(2)}, u32[]{:S(2)}) collective-permute-start(bf16[32,768]{1,0:T(8,128)(2,1)} %get-tuple-element.50), channel_id=1, source_target_pairs={{1,0},{2,1},{3,2},{5,4},{6,5},{7,6},{9,8},{10,9},{11,10},{13,12},{... | collective-permute-start | bytes 147464 | tf_op jit(solution)/shard_map/ppermute | solution.py:475
  4.1 8.5 %collective-permute-start = (bf16[16,512]{1,0:T(8,128)(2,1)}, bf16[16,512]{1,0:T(8,128)(2,1)S(1)}, u32[]{:S(2)}, u32[]{:S(2)}) collective-permute-start(bf16[16,512]{1,0:T(8,128)(2,1)} %get-tuple-element.49.mine_ref), channel_id=1, source_target_pairs={{0,1},{1,2},{2,3},{4,5},{5,6},{6,7},{8,9},{9,10},{10,11},{12,13},{... | collective-permute-start | bytes 49160 | tf_op jit(solution)/shard_map/ppermute | solution.py:475
  7.2 1.0 %copy-start.1 = (bf16[256,768]{1,0:T(8,128)(2,1)S(1)}, bf16[256,768]{1,0:T(8,128)(2,1)}, u32[]{:S(2)}) copy-start(bf16[256,768]{1,0:T(8,128)(2,1)} %table_ref.1) | copy-start | bytes 1179652
  8.2 4.5 %copy-start.2 = (bf16[16,768]{1,0:T(8,128)(2,1)S(1)}, bf16[16,768]{1,0:T(8,128)(2,1)}, u32[]{:S(2)}) copy-start(bf16[16,768]{1,0:T(8,128)(2,1)} %get-tuple-element.53.q_ref.scorer_ref) | copy-start | bytes 73732
  8.2 4.5 %copy-start.3 = (bf16[16,512]{1,0:T(8,128)(2,1)S(1)}, bf16[16,512]{1,0:T(8,128)(2,1)}, u32[]{:S(2)}) copy-start(bf16[16,512]{1,0:T(8,128)(2,1)} %get-tuple-element.49.mine_ref) | copy-start | bytes 49156
  8.2 67.0 %slice-start = ((s8[5898240]{0:T(1024)(128)(4,1)}), s8[1703936]{0:T(1024)(128)(4,1)S(1)}, s32[]{:S(2)}) async-start(s8[5898240]{0:T(1024)(128)(4,1)} %bitcast.3), calls=%async_computation | async-start | bytes 3407872
  12.7 62.5 %slice-start.1 = ((s8[5898240]{0:T(1024)(128)(4,1)}), s8[4194304]{0:T(1024)(128)(4,1)S(1)}, s32[]{:S(2)}) async-start(s8[5898240]{0:T(1024)(128)(4,1)} %bitcast.3), calls=%async_computation.1 | async-start | bytes 8388608
  19.8 4.0 %collective-permute-start.2 = (bf16[544,384]{1,0:T(8,128)(2,1)S(1)}, bf16[544,384]{1,0:T(8,128)(2,1)S(1)}, u32[]{:S(2)}, u32[]{:S(2)}) collective-permute-start(bf16[544,384]{1,0:T(8,128)(2,1)S(1)} %get-tuple-element.59), channel_id=1, source_target_pairs={{0,1},{1,0},{2,3},{3,2},{4,5},{5,4},{6,7},{7,6},{8,9},{9,8},{10,11... | collective-permute-start | bytes 1253384 | tf_op jit(solution)/shard_map/ppermute | solution.py:479
  25.3 8.6 %collective-permute-start.3 = (bf16[336,384]{1,0:T(8,128)(2,1)S(1)}, bf16[336,384]{1,0:T(8,128)(2,1)S(1)}, u32[]{:S(2)}, u32[]{:S(2)}) collective-permute-start(bf16[336,384]{1,0:T(8,128)(2,1)S(1)} %get-tuple-element.63), channel_id=1, source_target_pairs={{0,2},{1,3},{2,0},{3,1},{4,6},{5,7},{6,4},{7,5},{8,10},{9,11},{10,... | collective-permute-start | bytes 774152 | tf_op jit(solution)/shard_map/ppermute | solution.py:479
  26.2 7.7 %collective-permute-start.4 = (bf16[320,384]{1,0:T(8,128)(2,1)S(1)}, bf16[320,384]{1,0:T(8,128)(2,1)S(1)}, u32[]{:S(2)}, u32[]{:S(2)}) collective-permute-start(bf16[320,384]{1,0:T(8,128)(2,1)S(1)} %get-tuple-element.64), channel_id=1, source_target_pairs={{0,4},{1,5},{2,6},{3,7},{4,0},{5,1},{6,2},{7,3},{8,12},{9,13},{10,... | collective-permute-start | bytes 737288 | tf_op jit(solution)/shard_map/ppermute | solution.py:479
  34.0 6.5 %collective-permute-start.5 = (bf16[176,384]{1,0:T(8,128)(2,1)S(1)}, bf16[176,384]{1,0:T(8,128)(2,1)S(1)}, u32[]{:S(2)}, u32[]{:S(2)}) collective-permute-start(bf16[176,384]{1,0:T(8,128)(2,1)S(1)} %get-tuple-element.70), channel_id=1, source_target_pairs={{0,4},{1,5},{2,6},{3,7},{4,0},{5,1},{6,2},{7,3},{8,12},{9,13},{10,... | collective-permute-start | bytes 405512 | tf_op jit(solution)/shard_map/ppermute | solution.py:479
  35.6 4.9 %collective-permute-start.6 = (bf16[160,384]{1,0:T(8,128)(2,1)S(1)}, bf16[160,384]{1,0:T(8,128)(2,1)S(1)}, u32[]{:S(2)}, u32[]{:S(2)}) collective-permute-start(bf16[160,384]{1,0:T(8,128)(2,1)S(1)} %get-tuple-element.71), channel_id=1, source_target_pairs={{0,2},{1,3},{2,0},{3,1},{4,6},{5,7},{6,4},{7,5},{8,10},{9,11},{10,... | collective-permute-start | bytes 368648 | tf_op jit(solution)/shard_map/ppermute | solution.py:479
  40.6 4.7 %collective-permute-start.7 = (bf16[96,384]{1,0:T(8,128)(2,1)S(1)}, bf16[96,384]{1,0:T(8,128)(2,1)S(1)}, u32[]{:S(2)}, u32[]{:S(2)}) collective-permute-start(bf16[96,384]{1,0:T(8,128)(2,1)S(1)} %get-tuple-element.75), channel_id=1, source_target_pairs={{0,8},{1,9},{2,10},{3,11},{4,12},{5,13},{6,14},{7,15},{8,0},{9,1},... | collective-permute-start | bytes 221192 | tf_op jit(solution)/shard_map/ppermute | solution.py:479
  42.2 6.8 %collective-permute-start.8 = (bf16[96,384]{1,0:T(8,128)(2,1)S(1)}, bf16[96,384]{1,0:T(8,128)(2,1)S(1)}, u32[]{:S(2)}, u32[]{:S(2)}) collective-permute-start(bf16[96,384]{1,0:T(8,128)(2,1)S(1)} %get-tuple-element.76), channel_id=1, source_target_pairs={{0,16},{1,17},{2,18},{3,19},{4,20},{5,21},{6,22},{7,23},{8,24},{9,... | collective-permute-start | bytes 221192 | tf_op jit(solution)/shard_map/ppermute | solution.py:479
  44.8 6.3 %collective-permute-start.9 = (bf16[96,384]{1,0:T(8,128)(2,1)S(1)}, bf16[96,384]{1,0:T(8,128)(2,1)S(1)}, u32[]{:S(2)}, u32[]{:S(2)}) collective-permute-start(bf16[96,384]{1,0:T(8,128)(2,1)S(1)} %get-tuple-element.77), channel_id=1, source_target_pairs={{0,24},{1,25},{2,26},{3,27},{4,28},{5,29},{6,30},{7,31},{8,16},{9,... | collective-permute-start | bytes 221192 | tf_op jit(solution)/shard_map/ppermute | solution.py:479
  51.8 6.1 %collective-permute-start.12 = (bf16[80,384]{1,0:T(8,128)(2,1)S(1)}, bf16[80,384]{1,0:T(8,128)(2,1)S(1)}, u32[]{:S(2)}, u32[]{:S(2)}) collective-permute-start(bf16[80,384]{1,0:T(8,128)(2,1)S(1)} %get-tuple-element.79.refs_0_), channel_id=1, source_target_pairs={{0,24},{1,25},{2,26},{3,27},{4,28},{5,29},{6,30},{7,31},{8,16},{9,... | collective-permute-start | bytes 184328 | tf_op jit(solution)/shard_map/ppermute | solution.py:479
  52.9 6.2 %collective-permute-start.11 = (bf16[80,384]{1,0:T(8,128)(2,1)S(1)}, bf16[80,384]{1,0:T(8,128)(2,1)S(1)}, u32[]{:S(2)}, u32[]{:S(2)}) collective-permute-start(bf16[80,384]{1,0:T(8,128)(2,1)S(1)} %get-tuple-element.79.refs_0_), channel_id=1, source_target_pairs={{0,16},{1,17},{2,18},{3,19},{4,20},{5,21},{6,22},{7,23},{8,24},{9,... | collective-permute-start | bytes 184328 | tf_op jit(solution)/shard_map/ppermute | solution.py:479
  53.3 5.8 %collective-permute-start.10 = (bf16[80,384]{1,0:T(8,128)(2,1)S(1)}, bf16[80,384]{1,0:T(8,128)(2,1)S(1)}, u32[]{:S(2)}, u32[]{:S(2)}) collective-permute-start(bf16[80,384]{1,0:T(8,128)(2,1)S(1)} %get-tuple-element.79.refs_0_), channel_id=1, source_target_pairs={{0,8},{1,9},{2,10},{3,11},{4,12},{5,13},{6,14},{7,15},{8,0},{9,1},... | collective-permute-start | bytes 184328 | tf_op jit(solution)/shard_map/ppermute | solution.py:479
  59.1 5.9 %collective-permute-start.13 = (bf16[160,384]{1,0:T(8,128)(2,1)S(1)}, bf16[160,384]{1,0:T(8,128)(2,1)S(1)}, u32[]{:S(2)}, u32[]{:S(2)}) collective-permute-start(bf16[160,384]{1,0:T(8,128)(2,1)S(1)} %get-tuple-element.80.a_ref), channel_id=1, source_target_pairs={{0,4},{1,5},{2,6},{3,7},{4,0},{5,1},{6,2},{7,3},{8,12},{9,13},{10,... | collective-permute-start | bytes 368648 | tf_op jit(solution)/shard_map/ppermute | solution.py:479
  59.7 6.2 %collective-permute-start.14 = (bf16[160,384]{1,0:T(8,128)(2,1)S(1)}, bf16[160,384]{1,0:T(8,128)(2,1)S(1)}, u32[]{:S(2)}, u32[]{:S(2)}) collective-permute-start(bf16[160,384]{1,0:T(8,128)(2,1)S(1)} %get-tuple-element.81.b_ref), channel_id=1, source_target_pairs={{0,2},{1,3},{2,0},{3,1},{4,6},{5,7},{6,4},{7,5},{8,10},{9,11},{10,... | collective-permute-start | bytes 368648 | tf_op jit(solution)/shard_map/ppermute | solution.py:479
  66.0 6.3 %collective-permute-start.15 = (bf16[320,384]{1,0:T(8,128)(2,1)S(1)}, bf16[320,384]{1,0:T(8,128)(2,1)S(1)}, u32[]{:S(2)}, u32[]{:S(2)}) collective-permute-start(bf16[320,384]{1,0:T(8,128)(2,1)S(1)} %get-tuple-element.83), channel_id=1, source_target_pairs={{0,2},{1,3},{2,0},{3,1},{4,6},{5,7},{6,4},{7,5},{8,10},{9,11},{10,... | collective-permute-start | bytes 737288 | tf_op jit(solution)/shard_map/ppermute | solution.py:479
  67.4 6.2 %collective-permute-start.16 = (bf16[320,384]{1,0:T(8,128)(2,1)S(1)}, bf16[320,384]{1,0:T(8,128)(2,1)S(1)}, u32[]{:S(2)}, u32[]{:S(2)}) collective-permute-start(bf16[320,384]{1,0:T(8,128)(2,1)S(1)} %get-tuple-element.84), channel_id=1, source_target_pairs={{0,4},{1,5},{2,6},{3,7},{4,0},{5,1},{6,2},{7,3},{8,12},{9,13},{10,... | collective-permute-start | bytes 737288 | tf_op jit(solution)/shard_map/ppermute | solution.py:479
  69.0 6.2 %collective-permute-start.17 = (bf16[2,320,384]{2,1,0:T(8,128)(2,1)S(1)}, bf16[2,320,384]{2,1,0:T(8,128)(2,1)S(1)}, u32[]{:S(2)}, u32[]{:S(2)}) collective-permute-start(bf16[2,320,384]{2,1,0:T(8,128)(2,1)S(1)} %get-tuple-element.82.early), channel_id=1, source_target_pairs={{0,1},{1,0},{2,3},{3,2},{4,5},{5,4},{6,7},{7,6},{8,9},{9,8},{10,11... | collective-permute-start | bytes 1474568 | tf_op jit(solution)/shard_map/ppermute | solution.py:479
  72.3 1.5 %collective-permute-start.18 = (bf16[320,384]{1,0:T(8,128)(2,1)S(1)}, bf16[320,384]{1,0:T(8,128)(2,1)S(1)}, u32[]{:S(2)}, u32[]{:S(2)}) collective-permute-start(bf16[320,384]{1,0:T(8,128)(2,1)S(1)} %collective-permute-done.15.a_late), channel_id=1, source_target_pairs={{0,1},{1,0},{2,3},{3,2},{4,5},{5,4},{6,7},{7,6},{8,9},{9,8},{10,11... | collective-permute-start | bytes 737288 | tf_op jit(solution)/shard_map/ppermute | solution.py:479
  73.6 1.5 %collective-permute-start.19 = (bf16[320,384]{1,0:T(8,128)(2,1)S(1)}, bf16[320,384]{1,0:T(8,128)(2,1)S(1)}, u32[]{:S(2)}, u32[]{:S(2)}) collective-permute-start(bf16[320,384]{1,0:T(8,128)(2,1)S(1)} %collective-permute-done.16.b_late), channel_id=1, source_target_pairs={{0,1},{1,0},{2,3},{3,2},{4,5},{5,4},{6,7},{7,6},{8,9},{9,8},{10,11... | collective-permute-start | bytes 737288 | tf_op jit(solution)/shard_map/ppermute | solution.py:479

commit v4 on v3

--- a/solution.py
+++ b/solution.py
@@ -75,24 +75,11 @@
     return (device & 1) == 1, a_mine, b_mine
 
 
-def pack_kernel(row_len_ref, ids_ref, seg_ref, cot_ref, scorer_ref, right_ref, left_ref, q_ref):
-    span = ids_ref.shape[1]
-    width = cot_ref.shape[2]
-    row = lax.broadcasted_iota(jnp.int32, (HALO, span), 0)
-    ids = ids_ref[...].astype(F32)
-    segs = seg_ref[...].astype(F32)
-    length = row_len_ref[...]
-    both = jnp.where(row == 0, ids, jnp.where(row == 1, segs, 0.0))
-    size = jnp.where(row == 2, lax.shift_right_logical(length, 8), length & 255).astype(F32)
-    both = jnp.where((row == 2) | (row == 3), size, both).astype(BF)
-    right_ref[...] = both
-    left_ref[0:HALO] = cot_ref[0]
-    left_ref[HALO : 2 * HALO, 0:span] = both
-    left_ref[HALO : 2 * HALO, span:width] = jnp.zeros((HALO, width - span), BF)
-    s1, s2, s3 = split3(scorer_ref[...].reshape(1, width))
-    row = lax.broadcasted_iota(jnp.int32, q_ref.shape, 0)
+def three_rows(scorer, rows):
+    s1, s2, s3 = split3(scorer.reshape(1, scorer.shape[0]))
+    row = lax.broadcasted_iota(jnp.int32, (rows, scorer.shape[0]), 0)
     pick = jnp.where(row == 0, s1.astype(F32), jnp.where(row == 1, s2.astype(F32), s3.astype(F32)))
-    q_ref[...] = jnp.where(row < 3, pick, 0.0).astype(BF)
+    return jnp.where(row < 3, pick, 0.0).astype(BF)
 
 
 def tap_kernel(table_hbm, weight_hbm, hi_ref, lo_ref, table_ref, weight_ref, sem):
@@ -116,17 +103,17 @@
 
 
 def local_kernel(
-    calib_ref, mine_ref, from_left_ref, from_right_ref, hi_ref, lo_ref, bias_ref, cot_ref,
-    q_ref, keep_ref, send_ref, ext_ref, idt_ref, band_ref, y_ref, full_q_ref, *, seq_size, taps,
+    calib_ref, mine_ref, from_left_ref, hi_ref, lo_ref, bias_ref, cot_ref,
+    scorer_ref, keep_ref, send_ref, ext_ref, idt_ref, band_ref, y_ref, full_q_ref, *, seq_size, taps,
 ):
-    span = keep_ref.shape[0]
+    span = keep_ref.shape[0] - HALO
     width = hi_ref.shape[1]
     vocab = hi_ref.shape[0] // taps
     half = width // 2
     own_blocks = span // 2
     lanes = y_ref.shape[0]
     sizes = calib_ref.shape[0]
-    front = span + HALO
+    front = span
     upper = place(seq_size, 1, 1)[0]
     spare = lax.broadcasted_iota(jnp.int32, (1, lanes - span), 1)
 
@@ -134,9 +121,8 @@
     length = (256.0 * mine[2:3, 0:1] + mine[3:4, 0:1]).astype(jnp.int32)
 
     def line_up(at):
-        near_right = from_right_ref[HALO : 2 * HALO, 0 : lanes - span].astype(F32)[at : at + 1]
         near_left = from_left_ref[:, 2 * span - lanes : span].astype(F32)[at : at + 1]
-        rest = jnp.where(spare < HALO, near_right, jnp.where(spare >= lanes - span - HALO, near_left, 0.0))
+        rest = jnp.where(spare >= lanes - span - HALO, near_left, 0.0)
         return jnp.concatenate([mine[at : at + 1], rest], axis=1)
 
     pos = lax.broadcasted_iota(jnp.int32, (1, lanes), 1)
@@ -155,6 +141,9 @@
         by_tap = jnp.where(row8 == k, moved, by_tap)
         for i in range(2):
             idt = jnp.where(row16 == 2 * k + i, moved[:, i * (span // 2) : (i + 1) * (span // 2)], idt)
+        before = pltpu.roll(moved[:, span:lanes], HALO, 1)
+        before = jnp.concatenate([before] * (span // 2 // (lanes - span)), axis=1)
+        idt = jnp.where(row16 == 2 * taps + k, before, idt)
     idt = idt.astype(BF)
     idt_ref[...] = idt
     column = jnp.transpose(by_tap)
@@ -168,10 +157,9 @@
     y_ref[front : lanes - HALO] = jnp.zeros((lanes - HALO - front, width), BF)
     y_ref[lanes - HALO : lanes] = y[front : front + HALO]
     full_q_ref[0:own_blocks] = cot_ref[0]
-    full_q_ref[own_blocks : own_blocks + HALO] = from_right_ref[0:HALO]
-    full_q_ref[own_blocks + HALO : own_blocks + 2 * HALO] = q_ref[...]
-    tail = own_blocks + HALO
-    q_rows = own_blocks + 2 * HALO
+    full_q_ref[own_blocks : own_blocks + HALO] = three_rows(scorer_ref[...], HALO)
+    tail = own_blocks
+    q_rows = own_blocks + HALO
     dots = dot_nt(full_q_ref[...], y_ref[...])
     u = dots[tail : tail + 1] + dots[tail + 1 : tail + 2] + dots[tail + 2 : tail + 3]
 
@@ -212,17 +200,14 @@
     for d in reversed(range(sizes)):
         later = later + probs[d] * inv[d]
         alpha[d] = valid[d] * later
-    gammas, rhos, calibs = [], [], []
+    gammas, calibs = [], []
     for part in parts:
         dscores = [sum(part[c] * calib_ref[b, c] for c in range(sizes)) for b in range(sizes)]
-        later, gamma, rho = 0.0, 0.0, 0.0
+        later, gamma = 0.0, 0.0
         for d in reversed(range(sizes)):
             later = later + inv[d] * dscores[d]
-            beta = valid[d] * later
-            gamma = gamma + roll(beta, -d)
-            rho = rho + roll(beta * own, -d)
+            gamma = gamma + roll(own * valid[d] * later, -d)
         gammas.append(gamma)
-        rhos.append(rho)
         calibs.append([[jnp.sum(own * scores[b] * part[c], axis=1, keepdims=True) for c in range(sizes)] for b in range(sizes)])
     band = jnp.where((line >= tail) & (line < tail + 3), gammas[0], 0.0)
     for d in range(sizes):
@@ -230,16 +215,16 @@
     band_hi, band_lo = split2(band)
     band_ref[0] = band_hi[0:own_blocks]
     band_ref[1] = band_lo[0:own_blocks]
-    dy = dot_tn(band_hi[:, 0:span], full_q_ref[...]) + dot_tn(band_lo[:, 0:span], full_q_ref[...])
-    dy = dy.astype(BF)
+    dy = dot_tn(band_hi, full_q_ref[...]) + dot_tn(band_lo, full_q_ref[...])
+    dy = jnp.concatenate([dy[0:span], dy[lanes - HALO : lanes]], axis=0).astype(BF)
     left, right = dy[:, 0:half], dy[:, half:width]
     keep_ref[...] = jnp.where(upper, right, left)
-    send_ref[0:span] = jnp.where(upper, left, right)
+    send_ref[0 : span + HALO] = jnp.where(upper, left, right)
     grad_bias = jnp.sum(dy.astype(F32), axis=0, keepdims=True)
 
     row16 = lax.broadcasted_iota(jnp.int32, (16, lanes), 0)
     stack = jnp.zeros((16, lanes), F32)
-    pieces = split3(rhos[0]) + split3(rhos[1]) + split3(gammas[1] * own)
+    pieces = split3(gammas[0]) + split3(gammas[1])
     for i, piece in enumerate(pieces):
         stack = jnp.where(row16 == i, piece.astype(F32), stack)
     stack = stack.astype(BF)
@@ -250,7 +235,8 @@
         ext_ref[2 * i : 2 * i + 1] = row[:, 0:half]
         ext_ref[2 * i + 1 : 2 * i + 2] = row[:, half:width]
     by_tap = dot_nn(stack[:, 0:span], one_hot[0:span])
-    by_tap = by_tap[6:7] + by_tap[7:8] + by_tap[8:9]
+    last = dot_nn(jnp.roll(stack[:, span:lanes], HALO, 1)[:, 0:HALO], one_hot[span : span + HALO])
+    by_tap = by_tap[3:4] + by_tap[4:5] + by_tap[5:6] + (last[3:4] + last[4:5] + last[5:6])
     by_tap = jnp.concatenate([by_tap, jnp.zeros((1, 4 * half - taps * vocab), F32)], axis=1)
     for i in range(4):
         ext_ref[6 + i : 7 + i] = by_tap[:, i * half : (i + 1) * half]
@@ -259,12 +245,12 @@
     sums = [calibs[i][b][c] for i in range(2) for b in range(sizes) for c in range(sizes)]
     sums.append(jnp.sum(entropy, axis=1, keepdims=True))
     sums.append(jnp.sum(own * mask, axis=1, keepdims=True))
-    sums.append(jnp.sum(own * gammas[1], axis=1, keepdims=True))
+    sums.append(jnp.sum(gammas[1], axis=1, keepdims=True))
     for i, one in enumerate(sums):
         misc = jnp.where(spot == i, one, misc)
     ext_ref[10:11] = misc
-    send_ref[span : span + 16] = coded(ext_ref[...])
-    send_ref[span + 16 : span + 32] = jnp.concatenate([idt, jnp.zeros((16, half - idt.shape[1]), BF)], axis=1)
+    send_ref[span + HALO : span + HALO + 16] = coded(ext_ref[...])
+    send_ref[span + HALO + 16 : span + HALO + 32] = jnp.concatenate([idt, jnp.zeros((16, half - idt.shape[1]), BF)], axis=1)
 
 
 def mix_kernel(band_ref, y_ref, blocks_ref, token_ref):
@@ -298,27 +284,31 @@
 
 
 def table_kernel(keep_ref, idt_ref, got_ref, ext_ref, a_keep, a_send, b_keep, b_send, ext_out, *, seq_size, part):
-    span, half = keep_ref.shape
+    span, half = keep_ref.shape[0] - HALO, keep_ref.shape[1]
     taps, quarter, _ = a_keep.shape
     vocab = 4 * quarter
     _, a_mine, b_mine = place(seq_size, quarter, part)
     value = local_value((vocab, 1), 0, a_mine, b_mine, vocab).astype(F32)
     mine = idt_ref[...].astype(F32)
-    theirs = got_ref[span + 16 : span + 32].astype(F32)
+    theirs = got_ref[span + HALO + 16 : span + HALO + 32].astype(F32)
     wide = mine.shape[1]
+    near = lax.broadcasted_iota(jnp.int32, (1, 128), 1) < HALO
+    both = jnp.concatenate([keep_ref[span : span + HALO], got_ref[span : span + HALO], jnp.zeros((128 - 2 * HALO, half), BF)], axis=0)
     for k in range(taps):
-        acc = None
+        at = 2 * taps + k
+        row = jnp.where(near, mine[at : at + 1, 0:128], pltpu.roll(theirs[at : at + 1, 0:128], HALO, 1))
+        acc = dot_nn(jnp.where(row == value, 1.0, 0.0).astype(BF), both)
         for i in range(span // wide):
             for ids, grad in ((mine, keep_ref), (theirs, got_ref)):
                 row = ids[2 * k + i : 2 * k + i + 1, 0:wide]
                 one_hot = jnp.where(row == value, 1.0, 0.0).astype(BF)
                 term = dot_nn(one_hot, grad[i * wide : (i + 1) * wide])
-                acc = term if acc is None else acc + term
+                acc = acc + term
         a_keep[k] = acc[0:quarter]
         a_send[k * quarter : (k + 1) * quarter] = acc[quarter : 2 * quarter].astype(BF)
         b_keep[k] = acc[2 * quarter : 3 * quarter]
         b_send[k * quarter : (k + 1) * quarter] = acc[3 * quarter : 4 * quarter].astype(BF)
-    ext = joined(ext_ref) + pair(got_ref, span)
+    ext = joined(ext_ref) + pair(got_ref, span + HALO)
     ext_out[...] = ext
     a_send[taps * quarter : taps * quarter + 16] = coded(ext)
 
@@ -367,7 +357,7 @@
 
 
 def shard_kernel(keep, ext_ref, scorer_ref, *refs, seq_size, taps, vocab):
-    gots, (shard, loss_ref, bias_ref, grad_scorer_ref, calib_ref) = refs[:-5], refs[-5:]
+    gots, (shard, loss_ref, bias_ref, grad_scorer_ref, calib_ref) = refs[:-5][::-1], refs[-5:]
     size, half = keep.shape
     part = size // (2 * taps)
     upper, a_mine, b_mine = place(seq_size, vocab // 4, part)
@@ -381,8 +371,7 @@
         return jnp.sum(jnp.where(spot == i, misc, 0.0), axis=1, keepdims=True)
 
     count = one(33)
-    scorer = scorer_ref[...].astype(F32)
-    scorer = scorer[0:1] + scorer[1:2] + scorer[2:3]
+    scorer = scorer_ref[...].reshape(1, 2 * half)
     mine = jnp.where(upper, scorer[:, half:], scorer[:, :half])
     step = lax.broadcasted_iota(jnp.int32, (part, vocab), 0)
     lane = lax.broadcasted_iota(jnp.int32, (part, vocab), 1)
@@ -462,7 +451,8 @@
         pltpu.make_async_copy(buffer.at[k], conv_ref.at[k], sem.at[k]).start()
     acc = 0.0
     for k in range(taps):
-        acc = acc + dot_nt(rows[k], weight_ref[k])
+        acc = acc + dot_nt(weight_ref[k], rows[k])
+    acc = jnp.transpose(acc)
     for at in range(0, vocab, part):
         to = (at ^ a_mine) if at < vocab // 2 else vocab // 2 + ((at - vocab // 2) ^ b_mine)
         table_ref[pl.ds(pl.multiple_of(to, part), part)] = acc[at : at + part]
@@ -497,26 +487,10 @@
     size = 2 * taps * part
     lanes = span + 128
 
-    to_right, to_left, q_rows = pl.pallas_call(
-        pack_kernel,
-        out_shape=(shape((HALO, span), BF), shape((2 * HALO, width), BF), shape((16, width), BF)),
-        grid=(1,),
-        in_specs=[
-            pl.BlockSpec((1, 1), lambda i: (0, 0)),
-            pl.BlockSpec((1, span), lambda i: (0, 0)),
-            pl.BlockSpec((1, span), lambda i: (0, 0)),
-            pl.BlockSpec((1, HALO, width), lambda i: (0, 0, 0)),
-            pl.BlockSpec((width,), lambda i: (0,)),
-        ],
-        out_specs=(
-            pl.BlockSpec((HALO, span), lambda i: (0, 0)),
-            pl.BlockSpec((2 * HALO, width), lambda i: (0, 0)),
-            pl.BlockSpec((16, width), lambda i: (0, 0)),
-        ),
-        name="pack",
-    )(row_len.reshape(1, 1), byte_ids, seg_ids, cotangent, scorer)
+    row = lax.broadcasted_iota(jnp.int32, (HALO, span), 0)
+    digit = jnp.where(row == 2, lax.shift_right_logical(row_len[0], 8), row_len[0] & 255)
+    to_right = jnp.where(row == 0, byte_ids, jnp.where(row == 1, seg_ids, digit)).astype(BF)
     from_left = neighbour(to_right, "seq", 1)
-    from_right = neighbour(to_left, "seq", -1)
 
     hi, lo = pl.pallas_call(
         tap_kernel,
@@ -535,18 +509,18 @@
     keep, send, ext, idt, band, y = call(
         functools.partial(local_kernel, seq_size=seq_size, taps=taps),
         (
-            shape((span, half), BF),
-            shape((span + 32, half), BF),
+            shape((span + HALO, half), BF),
+            shape((span + HALO + 32, half), BF),
             shape((16, half), F32),
             shape((16, span // 2), BF),
             shape((2, span // 2, lanes), BF),
             shape((lanes, width), BF),
         ),
         "local",
-        in_specs=[sspec()] + [vspec()] * 8,
+        in_specs=[sspec()] + [vspec()] * 7,
         out_specs=(vspec(),) * 6,
-        scratch_shapes=[pltpu.VMEM((span // 2 + 2 * HALO, width), BF)],
-    )(calibration, to_right, from_left, from_right, hi, lo, conv_bias, cotangent, q_rows)
+        scratch_shapes=[pltpu.VMEM((span // 2 + HALO, width), BF)],
+    )(calibration, to_right, from_left, hi, lo, conv_bias, cotangent, scorer)
 
     got = swap(send, 1, count)
     a_keep, a_send, b_keep, b_send, ext = call(
@@ -609,7 +583,7 @@
         "shard",
         in_specs=[vspec()] * (3 + len(gots)),
         out_specs=(vspec(),) * 5,
-    )(mine, ext, q_rows, *gots)
+    )(mine, ext, scorer, *gots[::-1])
 
     gathered = [shard] + [swap(shard, 8 * t, count) for t in range(1, depth)]
     a_out, b_out = call(

time: 81.5 us -> 77.9 us (0.956)
  starting transfers between devices: 26.1 us -> 23.6 us
  Pallas kernels: 23.5 us -> 22.2 us
    ppermute x2 -> x1, starting transfers between devices: 4.31 us -> 2.39 us  [neighbour(): lax.ppermute(shard, axis, [(i, i + by) for i in range(length) if 0 <= i +...]
    pallas_call x1 -> x0, Pallas kernels: 1.48 us -> none  [body(): pl.pallas_call(pack_kernel, out_shape=(shape((HALO, span), BF), shape((2...]
  transfers between devices with their start and end apart: 20 -> 19, of which waited for: 14 -> 14; matrix products, arithmetic and copies ran while one was open for 0% -> 0% of each run, Pallas kernels for 8% -> 8%
where the time goes in v4:
time: 77.9 us; the launch traced here: 77.7 us
  waiting for transfers between devices  28.6 us (37%)
  starting transfers between devices  23.6 us (30%)
  Pallas kernels  22.2 us (28%)
  between operations  1.47 us (2%)
  local copies, waits for them, and re-layouts  1.02 us (1%)
  other arithmetic  0.79 us (1%)
    ppermute x18, waiting for transfers between devices, swap(): return lax.ppermute(shard, AXES, [(i, i ^ flip) for i in range(count)])  28.6 us
    ppermute x18, starting transfers between devices, swap(): return lax.ppermute(shard, AXES, [(i, i ^ flip) for i in range(count)])  21.2 us
    pallas_call x1, Pallas kernels, body(): call(functools.partial(local_kernel, seq_size=seq_size, taps=taps), (shap...  7.07 us
    pallas_call x1, Pallas kernels, body(): call(functools.partial(final_kernel, seq_size=seq_size, part=part), (shap...  6.09 us
    pallas_call x1, Pallas kernels, body(): pl.pallas_call(tap_kernel, out_shape=(shape((taps * vocab, width), BF),)...  4.42 us
    ppermute x1, starting transfers between devices, neighbour(): lax.ppermute(shard, axis, [(i, i + by) for i in range(length) if 0 <= i +...  2.39 us
    pallas_call x1, Pallas kernels, body(): call(functools.partial(table_kernel, seq_size=seq_size, part=part), (shap...  1.77 us
  transfers between devices with their start and end apart: 19, of which 14 were waited for; matrix products, arithmetic and copies ran while one was open for 0% of the time, Pallas kernels for 8%

profile of v4, /device:TPU:0, one launch (start us, length us, event | category | flops | bytes accessed | tf_op | source)
XLA Modules:
  0.0 77.7 jit_solution(12339807224514836206)
XLA Ops:
  1.3 0.8 select_convert_fusion.mine_ref
  2.1 2.4 %collective-permute-start = (bf16[16,512]{1,0:T(8,128)(2,1)S(1)}, bf16[16,512]{1,0:T(8,128)(2,1)S(1)}, u32[]{:S(2)}, u32[]{:S(2)}) collective-permute-start(bf16[16,512]{1,0:T(8,128)(2,1)S(1)} %select_convert_fusion.mine_ref), channel_id=1, source_target_pairs={{0,1},{1,2},{2,3},{4,5},{5,6},{6,7},{8,9},{9,10},{10,11},{12,13},{... | collective-permute-start | bytes 49160 | tf_op jit(solution)/shard_map/ppermute | solution.py:465
  4.5 1.0 %copy-done = bf16[256,768]{1,0:T(8,128)(2,1)S(1)} copy-done((bf16[256,768]{1,0:T(8,128)(2,1)S(1)}, bf16[256,768]{1,0:T(8,128)(2,1)}, u32[]{:S(2)}) %copy-start) | copy-done | bytes 393240
  5.5 4.4 %taps.1 = (bf16[1280,768]{1,0:T(8,128)(2,1)S(1)}, bf16[1280,768]{1,0:T(8,128)(2,1)S(1)}) custom-call(bf16[256,768]{1,0:T(8,128)(2,1)S(1)} %copy-done, bf16[5,768,768]{2,1,0:T(8,128)(2,1)} %weight_ref.1), custom_call_target="tpu_custom_call" | custom-call | tf_op jit(solution)/shard_map/taps/pallas_call | solution.py:495
  10.0 7.1 %local.1 = (bf16[528,384]{1,0:T(8,128)(2,1)S(1)}, bf16[560,384]{1,0:T(8,128)(2,1)S(1)}, f32[16,384]{1,0:T(8,128)S(1)}, bf16[16,256]{1,0:T(8,128)(2,1)S(1)}, bf16...) custom-call(f32[4,4]{1,0:T(4,128)S(1)} %copy-done.5, bf16[16,512]{1,0:T(8,128)(2,1)S(1)} %select_convert_fusion.mine_ref, ...), custom_call_target="tpu_custom_call" | custom-call | tf_op jit(solution)/shard_map/local/pallas_call | solution.py:509
  17.1 2.7 %collective-permute-start.1 = (bf16[560,384]{1,0:T(8,128)(2,1)S(1)}, bf16[560,384]{1,0:T(8,128)(2,1)S(1)}, u32[]{:S(2)}, u32[]{:S(2)}) collective-permute-start(bf16[560,384]{1,0:T(8,128)(2,1)S(1)} %get-tuple-element.53), channel_id=1, source_target_pairs={{0,1},{1,0},{2,3},{3,2},{4,5},{5,4},{6,7},{7,6},{8,9},{9,8},{10,11... | collective-permute-start | bytes 1290248 | tf_op jit(solution)/shard_map/ppermute | solution.py:469
  19.8 1.4 %collective-permute-done.1.got_ref = bf16[560,384]{1,0:T(8,128)(2,1)S(1)} collective-permute-done((bf16[560,384]{1,0:T(8,128)(2,1)S(1)}, bf16[560,384]{1,0:T(8,128)(2,1)S(1)}, u32[]{:S(2)}, u32[]{:S(2)}) %collective-permute-start.1) | collective-permute-done | bytes 430112 | tf_op jit(solution)/shard_map/ppermute | solution.py:469
  21.2 1.8 %by_value.1 = (f32[5,64,384]{2,1,0:T(8,128)S(1)}, bf16[336,384]{1,0:T(8,128)(2,1)S(1)}, f32[5,64,384]{2,1,0:T(8,128)S(1)}, bf16[320,384]{1,0:T(8,128)(2,1)S(1)}, f32[16,384]{1,0:T(8,128)S(1)}) custom-call(bf16[528,384]{1,0:T(8,128)(2,1)S(1)} %get-tuple-element.51.keep_ref, bf16[16,256]{1,0:T(8,128)(2,1)S(1)} %get-tuple-element.52.idt_ref, ...), custom_call_target="tpu_custom_call" | custom-call | tf_op jit(solution)/shard_map/by_value/pallas_call | solution.py:526
  23.3 1.5 %collective-permute-start.3 = (bf16[320,384]{1,0:T(8,128)(2,1)S(1)}, bf16[320,384]{1,0:T(8,128)(2,1)S(1)}, u32[]{:S(2)}, u32[]{:S(2)}) collective-permute-start(bf16[320,384]{1,0:T(8,128)(2,1)S(1)} %get-tuple-element.58), channel_id=1, source_target_pairs={{0,4},{1,5},{2,6},{3,7},{4,0},{5,1},{6,2},{7,3},{8,12},{9,13},{10,... | collective-permute-start | bytes 737288 | tf_op jit(solution)/shard_map/ppermute | solution.py:469
  24.8 1.5 %mix.1 = (bf16[1,256,768]{2,1,0:T(8,128)(2,1)}, f32[8,128]{1,0:T(8,128)S(1)}) custom-call(bf16[2,256,640]{2,1,0:T(8,128)(2,1)S(1)} %get-tuple-element.48.band_ref, bf16[640,768]{1,0:T(8,128)(2,1)S(1)} %get-tuple-element.49.y_ref), custom_call_target="tpu_custom_call" | custom-call | tf_op jit(solution)/shard_map/mix/pallas_call | solution.py:540
  26.6 4.7 %collective-permute-done.3.b_got = bf16[320,384]{1,0:T(8,128)(2,1)S(1)} collective-permute-done((bf16[320,384]{1,0:T(8,128)(2,1)S(1)}, bf16[320,384]{1,0:T(8,128)(2,1)S(1)}, u32[]{:S(2)}, u32[]{:S(2)}) %collective-permute-start.3) | collective-permute-done | bytes 245792 | tf_op jit(solution)/shard_map/ppermute | solution.py:469
  31.6 1.6 %collective-permute-start.4 = (bf16[176,384]{1,0:T(8,128)(2,1)S(1)}, bf16[176,384]{1,0:T(8,128)(2,1)S(1)}, u32[]{:S(2)}, u32[]{:S(2)}) collective-permute-start(bf16[176,384]{1,0:T(8,128)(2,1)S(1)} %get-tuple-element.64), channel_id=1, source_target_pairs={{0,4},{1,5},{2,6},{3,7},{4,0},{5,1},{6,2},{7,3},{8,12},{9,13},{10,... | collective-permute-start | bytes 405512 | tf_op jit(solution)/shard_map/ppermute | solution.py:469
  33.2 1.5 %collective-permute-start.5 = (bf16[160,384]{1,0:T(8,128)(2,1)S(1)}, bf16[160,384]{1,0:T(8,128)(2,1)S(1)}, u32[]{:S(2)}, u32[]{:S(2)}) collective-permute-start(bf16[160,384]{1,0:T(8,128)(2,1)S(1)} %get-tuple-element.65), channel_id=1, source_target_pairs={{0,2},{1,3},{2,0},{3,1},{4,6},{5,7},{6,4},{7,5},{8,10},{9,11},{10,... | collective-permute-start | bytes 368648 | tf_op jit(solution)/shard_map/ppermute | solution.py:469
  34.7 3.4 %collective-permute-done.5.b_got = bf16[160,384]{1,0:T(8,128)(2,1)S(1)} collective-permute-done((bf16[160,384]{1,0:T(8,128)(2,1)S(1)}, bf16[160,384]{1,0:T(8,128)(2,1)S(1)}, u32[]{:S(2)}, u32[]{:S(2)}) %collective-permute-start.5) | collective-permute-done | bytes 122912 | tf_op jit(solution)/shard_map/ppermute | solution.py:469
  38.2 3.7 %collective-permute-start.6 = (bf16[96,384]{1,0:T(8,128)(2,1)S(1)}, bf16[96,384]{1,0:T(8,128)(2,1)S(1)}, u32[]{:S(2)}, u32[]{:S(2)}) collective-permute-start(bf16[96,384]{1,0:T(8,128)(2,1)S(1)} %get-tuple-element.69), channel_id=1, source_target_pairs={{0,24},{1,25},{2,26},{3,27},{4,28},{5,29},{6,30},{7,31},{8,16},{9,... | collective-permute-start | bytes 221192 | tf_op jit(solution)/shard_map/ppermute | solution.py:469
  41.9 0.8 %collective-permute-start.8 = (bf16[96,384]{1,0:T(8,128)(2,1)S(1)}, bf16[96,384]{1,0:T(8,128)(2,1)S(1)}, u32[]{:S(2)}, u32[]{:S(2)}) collective-permute-start(bf16[96,384]{1,0:T(8,128)(2,1)S(1)} %get-tuple-element.71), channel_id=1, source_target_pairs={{0,8},{1,9},{2,10},{3,11},{4,12},{5,13},{6,14},{7,15},{8,0},{9,1},... | collective-permute-start | bytes 221192 | tf_op jit(solution)/shard_map/ppermute | solution.py:469
  42.6 1.8 %collective-permute-done.6.refs_0_ = bf16[96,384]{1,0:T(8,128)(2,1)S(1)} collective-permute-done((bf16[96,384]{1,0:T(8,128)(2,1)S(1)}, bf16[96,384]{1,0:T(8,128)(2,1)S(1)}, u32[]{:S(2)}, u32[]{:S(2)}) %collective-permute-start.6) | collective-permute-done | bytes 73760 | tf_op jit(solution)/shard_map/ppermute | solution.py:469
  44.4 2.8 %collective-permute-done.7.refs_1_ = bf16[96,384]{1,0:T(8,128)(2,1)S(1)} collective-permute-done((bf16[96,384]{1,0:T(8,128)(2,1)S(1)}, bf16[96,384]{1,0:T(8,128)(2,1)S(1)}, u32[]{:S(2)}, u32[]{:S(2)}) %collective-permute-start.7) | collective-permute-done | bytes 73760 | tf_op jit(solution)/shard_map/ppermute | solution.py:469
  47.2 0.7 shard.1
  48.0 2.1 %collective-permute-start.11 = (bf16[80,384]{1,0:T(8,128)(2,1)S(1)}, bf16[80,384]{1,0:T(8,128)(2,1)S(1)}, u32[]{:S(2)}, u32[]{:S(2)}) collective-permute-start(bf16[80,384]{1,0:T(8,128)(2,1)S(1)} %get-tuple-element.73.refs_0_), channel_id=1, source_target_pairs={{0,24},{1,25},{2,26},{3,27},{4,28},{5,29},{6,30},{7,31},{8,16},{9,... | collective-permute-start | bytes 184328 | tf_op jit(solution)/shard_map/ppermute | solution.py:469
  50.1 2.2 %collective-permute-start.9 = (bf16[80,384]{1,0:T(8,128)(2,1)S(1)}, bf16[80,384]{1,0:T(8,128)(2,1)S(1)}, u32[]{:S(2)}, u32[]{:S(2)}) collective-permute-start(bf16[80,384]{1,0:T(8,128)(2,1)S(1)} %get-tuple-element.73.refs_0_), channel_id=1, source_target_pairs={{0,8},{1,9},{2,10},{3,11},{4,12},{5,13},{6,14},{7,15},{8,0},{9,1},... | collective-permute-start | bytes 184328 | tf_op jit(solution)/shard_map/ppermute | solution.py:469
  52.3 2.1 %collective-permute-done.11.refs_3_ = bf16[80,384]{1,0:T(8,128)(2,1)S(1)} collective-permute-done((bf16[80,384]{1,0:T(8,128)(2,1)S(1)}, bf16[80,384]{1,0:T(8,128)(2,1)S(1)}, u32[]{:S(2)}, u32[]{:S(2)}) %collective-permute-start.11) | collective-permute-done | bytes 61472 | tf_op jit(solution)/shard_map/ppermute | solution.py:469
  54.5 1.2 %collective-permute-done.10.refs_2_ = bf16[80,384]{1,0:T(8,128)(2,1)S(1)} collective-permute-done((bf16[80,384]{1,0:T(8,128)(2,1)S(1)}, bf16[80,384]{1,0:T(8,128)(2,1)S(1)}, u32[]{:S(2)}, u32[]{:S(2)}) %collective-permute-start.10) | collective-permute-done | bytes 61472 | tf_op jit(solution)/shard_map/ppermute | solution.py:469
  56.3 1.2 %collective-permute-start.13 = (bf16[160,384]{1,0:T(8,128)(2,1)S(1)}, bf16[160,384]{1,0:T(8,128)(2,1)S(1)}, u32[]{:S(2)}, u32[]{:S(2)}) collective-permute-start(bf16[160,384]{1,0:T(8,128)(2,1)S(1)} %get-tuple-element.75.b_ref), channel_id=1, source_target_pairs={{0,2},{1,3},{2,0},{3,1},{4,6},{5,7},{6,4},{7,5},{8,10},{9,11},{10,... | collective-permute-start | bytes 368648 | tf_op jit(solution)/shard_map/ppermute | solution.py:469
  57.5 4.0 %collective-permute-done.12.a_got = bf16[160,384]{1,0:T(8,128)(2,1)S(1)} collective-permute-done((bf16[160,384]{1,0:T(8,128)(2,1)S(1)}, bf16[160,384]{1,0:T(8,128)(2,1)S(1)}, u32[]{:S(2)}, u32[]{:S(2)}) %collective-permute-start.12) | collective-permute-done | bytes 122912 | tf_op jit(solution)/shard_map/ppermute | solution.py:469
  61.5 1.0 %collective-permute-done.13.b_got = bf16[160,384]{1,0:T(8,128)(2,1)S(1)} collective-permute-done((bf16[160,384]{1,0:T(8,128)(2,1)S(1)}, bf16[160,384]{1,0:T(8,128)(2,1)S(1)}, u32[]{:S(2)}, u32[]{:S(2)}) %collective-permute-start.13) | collective-permute-done | bytes 122912 | tf_op jit(solution)/shard_map/ppermute | solution.py:469
  62.6 1.3 %collective-permute-start.14 = (bf16[320,384]{1,0:T(8,128)(2,1)S(1)}, bf16[320,384]{1,0:T(8,128)(2,1)S(1)}, u32[]{:S(2)}, u32[]{:S(2)}) collective-permute-start(bf16[320,384]{1,0:T(8,128)(2,1)S(1)} %get-tuple-element.77), channel_id=1, source_target_pairs={{0,2},{1,3},{2,0},{3,1},{4,6},{5,7},{6,4},{7,5},{8,10},{9,11},{10,... | collective-permute-start | bytes 737288 | tf_op jit(solution)/shard_map/ppermute | solution.py:469
  63.9 1.7 %collective-permute-start.15 = (bf16[320,384]{1,0:T(8,128)(2,1)S(1)}, bf16[320,384]{1,0:T(8,128)(2,1)S(1)}, u32[]{:S(2)}, u32[]{:S(2)}) collective-permute-start(bf16[320,384]{1,0:T(8,128)(2,1)S(1)} %get-tuple-element.78), channel_id=1, source_target_pairs={{0,4},{1,5},{2,6},{3,7},{4,0},{5,1},{6,2},{7,3},{8,12},{9,13},{10,... | collective-permute-start | bytes 737288 | tf_op jit(solution)/shard_map/ppermute | solution.py:469
  65.6 3.3 %collective-permute-done.14.a_late = bf16[320,384]{1,0:T(8,128)(2,1)S(1)} collective-permute-done((bf16[320,384]{1,0:T(8,128)(2,1)S(1)}, bf16[320,384]{1,0:T(8,128)(2,1)S(1)}, u32[]{:S(2)}, u32[]{:S(2)}) %collective-permute-start.14) | collective-permute-done | bytes 245792 | tf_op jit(solution)/shard_map/ppermute | solution.py:469
  68.9 1.2 %collective-permute-done.15.b_late = bf16[320,384]{1,0:T(8,128)(2,1)S(1)} collective-permute-done((bf16[320,384]{1,0:T(8,128)(2,1)S(1)}, bf16[320,384]{1,0:T(8,128)(2,1)S(1)}, u32[]{:S(2)}, u32[]{:S(2)}) %collective-permute-start.15) | collective-permute-done | bytes 245792 | tf_op jit(solution)/shard_map/ppermute | solution.py:469
  70.4 1.2 %collective-permute-done.18.far_b = bf16[320,384]{1,0:T(8,128)(2,1)S(1)} collective-permute-done((bf16[320,384]{1,0:T(8,128)(2,1)S(1)}, bf16[320,384]{1,0:T(8,128)(2,1)S(1)}, u32[]{:S(2)}, u32[]{:S(2)}) %collective-permute-start.18) | collective-permute-done | bytes 245792 | tf_op jit(solution)/shard_map/ppermute | solution.py:469
  71.6 6.1 %final.1 = (f32[5,768,768]{2,1,0:T(8,128)}, f32[256,768]{1,0:T(8,128)}) custom-call(bf16[2,320,384]{2,1,0:T(8,128)(2,1)S(1)} %get-tuple-element.76.early, bf16[320,384]{1,0:T(8,128)(2,1)S(1)} %collective-permute-done.14.a_late, bf16[320,384]{1,0:T(8,128)(2,1)S(1)} %collective-permute-done.15.b_late, ...), custom_call_target="tpu_custom_call" | custom-call | tf_op jit(solution)/shard_map/final/pallas_call | solution.py:608
  (37 shorter events, 2.1 us)
Async XLA Ops:
  0.6 9.3 %copy-start.3 = (f32[768]{0:T(1024)S(1)}, f32[768]{0:T(1024)}, u32[]{:S(2)}) copy-start(f32[768]{0:T(1024)} %scorer_ref.3) | copy-start | bytes 9220
  0.6 9.3 %copy-start.5 = (f32[4,4]{1,0:T(4,128)S(1)}, f32[4,4]{1,0:T(4,128)}, u32[]{:S(2)}) copy-start(f32[4,4]{1,0:T(4,128)} %calib_ref.1) | copy-start | bytes 196
  0.7 9.3 %copy-start.4 = (f32[768]{0:T(1024)S(1)}, f32[768]{0:T(1024)}, u32[]{:S(2)}) copy-start(f32[768]{0:T(1024)} %bias_ref.1) | copy-start | bytes 9220
  2.1 7.8 %collective-permute-start = (bf16[16,512]{1,0:T(8,128)(2,1)S(1)}, bf16[16,512]{1,0:T(8,128)(2,1)S(1)}, u32[]{:S(2)}, u32[]{:S(2)}) collective-permute-start(bf16[16,512]{1,0:T(8,128)(2,1)S(1)} %select_convert_fusion.mine_ref), channel_id=1, source_target_pairs={{0,1},{1,2},{2,3},{4,5},{5,6},{6,7},{8,9},{9,10},{10,11},{12,13},{... | collective-permute-start | bytes 49160 | tf_op jit(solution)/shard_map/ppermute | solution.py:465
  4.5 1.0 %copy-start = (bf16[256,768]{1,0:T(8,128)(2,1)S(1)}, bf16[256,768]{1,0:T(8,128)(2,1)}, u32[]{:S(2)}) copy-start(bf16[256,768]{1,0:T(8,128)(2,1)} %table_ref.1) | copy-start | bytes 1179652
  5.5 4.5 %copy-start.2 = (bf16[1,256,768]{2,1,0:T(8,128)(2,1)S(1)}, bf16[1,256,768]{2,1,0:T(8,128)(2,1)}, u32[]{:S(2)}) copy-start(bf16[1,256,768]{2,1,0:T(8,128)(2,1)} %cot_ref.1) | copy-start | bytes 1179652
  5.5 20.8 %copy-start.1 = (bf16[256,768]{1,0:T(8,128)(2,1)S(1)}, bf16[256,768]{1,0:T(8,128)(2,1)}, u32[]{:S(2)}) copy-start(bf16[256,768]{1,0:T(8,128)(2,1)} %table_ref.1) | copy-start | bytes 1179652
  5.5 66.1 %slice-start = ((s8[5898240]{0:T(1024)(128)(4,1)}), s8[1703936]{0:T(1024)(128)(4,1)S(1)}, s32[]{:S(2)}) async-start(s8[5898240]{0:T(1024)(128)(4,1)} %bitcast.5), calls=%async_computation | async-start | bytes 3407872
  10.0 61.6 %slice-start.1 = ((s8[5898240]{0:T(1024)(128)(4,1)}), s8[4194304]{0:T(1024)(128)(4,1)S(1)}, s32[]{:S(2)}) async-start(s8[5898240]{0:T(1024)(128)(4,1)} %bitcast.5), calls=%async_computation.1 | async-start | bytes 8388608
  17.1 4.1 %collective-permute-start.1 = (bf16[560,384]{1,0:T(8,128)(2,1)S(1)}, bf16[560,384]{1,0:T(8,128)(2,1)S(1)}, u32[]{:S(2)}, u32[]{:S(2)}) collective-permute-start(bf16[560,384]{1,0:T(8,128)(2,1)S(1)} %get-tuple-element.53), channel_id=1, source_target_pairs={{0,1},{1,0},{2,3},{3,2},{4,5},{5,4},{6,7},{7,6},{8,9},{9,8},{10,11... | collective-permute-start | bytes 1290248 | tf_op jit(solution)/shard_map/ppermute | solution.py:469
  23.0 8.6 %collective-permute-start.2 = (bf16[336,384]{1,0:T(8,128)(2,1)S(1)}, bf16[336,384]{1,0:T(8,128)(2,1)S(1)}, u32[]{:S(2)}, u32[]{:S(2)}) collective-permute-start(bf16[336,384]{1,0:T(8,128)(2,1)S(1)} %get-tuple-element.57), channel_id=1, source_target_pairs={{0,2},{1,3},{2,0},{3,1},{4,6},{5,7},{6,4},{7,5},{8,10},{9,11},{10,... | collective-permute-start | bytes 774152 | tf_op jit(solution)/shard_map/ppermute | solution.py:469
  23.3 8.1 %collective-permute-start.3 = (bf16[320,384]{1,0:T(8,128)(2,1)S(1)}, bf16[320,384]{1,0:T(8,128)(2,1)S(1)}, u32[]{:S(2)}, u32[]{:S(2)}) collective-permute-start(bf16[320,384]{1,0:T(8,128)(2,1)S(1)} %get-tuple-element.58), channel_id=1, source_target_pairs={{0,4},{1,5},{2,6},{3,7},{4,0},{5,1},{6,2},{7,3},{8,12},{9,13},{10,... | collective-permute-start | bytes 737288 | tf_op jit(solution)/shard_map/ppermute | solution.py:469
  31.6 6.5 %collective-permute-start.4 = (bf16[176,384]{1,0:T(8,128)(2,1)S(1)}, bf16[176,384]{1,0:T(8,128)(2,1)S(1)}, u32[]{:S(2)}, u32[]{:S(2)}) collective-permute-start(bf16[176,384]{1,0:T(8,128)(2,1)S(1)} %get-tuple-element.64), channel_id=1, source_target_pairs={{0,4},{1,5},{2,6},{3,7},{4,0},{5,1},{6,2},{7,3},{8,12},{9,13},{10,... | collective-permute-start | bytes 405512 | tf_op jit(solution)/shard_map/ppermute | solution.py:469
  33.2 4.9 %collective-permute-start.5 = (bf16[160,384]{1,0:T(8,128)(2,1)S(1)}, bf16[160,384]{1,0:T(8,128)(2,1)S(1)}, u32[]{:S(2)}, u32[]{:S(2)}) collective-permute-start(bf16[160,384]{1,0:T(8,128)(2,1)S(1)} %get-tuple-element.65), channel_id=1, source_target_pairs={{0,2},{1,3},{2,0},{3,1},{4,6},{5,7},{6,4},{7,5},{8,10},{9,11},{10,... | collective-permute-start | bytes 368648 | tf_op jit(solution)/shard_map/ppermute | solution.py:469
  38.2 6.2 %collective-permute-start.6 = (bf16[96,384]{1,0:T(8,128)(2,1)S(1)}, bf16[96,384]{1,0:T(8,128)(2,1)S(1)}, u32[]{:S(2)}, u32[]{:S(2)}) collective-permute-start(bf16[96,384]{1,0:T(8,128)(2,1)S(1)} %get-tuple-element.69), channel_id=1, source_target_pairs={{0,24},{1,25},{2,26},{3,27},{4,28},{5,29},{6,30},{7,31},{8,16},{9,... | collective-permute-start | bytes 221192 | tf_op jit(solution)/shard_map/ppermute | solution.py:469
  41.9 5.4 %collective-permute-start.7 = (bf16[96,384]{1,0:T(8,128)(2,1)S(1)}, bf16[96,384]{1,0:T(8,128)(2,1)S(1)}, u32[]{:S(2)}, u32[]{:S(2)}) collective-permute-start(bf16[96,384]{1,0:T(8,128)(2,1)S(1)} %get-tuple-element.70), channel_id=1, source_target_pairs={{0,16},{1,17},{2,18},{3,19},{4,20},{5,21},{6,22},{7,23},{8,24},{9,... | collective-permute-start | bytes 221192 | tf_op jit(solution)/shard_map/ppermute | solution.py:469
  41.9 5.4 %collective-permute-start.8 = (bf16[96,384]{1,0:T(8,128)(2,1)S(1)}, bf16[96,384]{1,0:T(8,128)(2,1)S(1)}, u32[]{:S(2)}, u32[]{:S(2)}) collective-permute-start(bf16[96,384]{1,0:T(8,128)(2,1)S(1)} %get-tuple-element.71), channel_id=1, source_target_pairs={{0,8},{1,9},{2,10},{3,11},{4,12},{5,13},{6,14},{7,15},{8,0},{9,1},... | collective-permute-start | bytes 221192 | tf_op jit(solution)/shard_map/ppermute | solution.py:469
  48.0 6.5 %collective-permute-start.11 = (bf16[80,384]{1,0:T(8,128)(2,1)S(1)}, bf16[80,384]{1,0:T(8,128)(2,1)S(1)}, u32[]{:S(2)}, u32[]{:S(2)}) collective-permute-start(bf16[80,384]{1,0:T(8,128)(2,1)S(1)} %get-tuple-element.73.refs_0_), channel_id=1, source_target_pairs={{0,24},{1,25},{2,26},{3,27},{4,28},{5,29},{6,30},{7,31},{8,16},{9,... | collective-permute-start | bytes 184328 | tf_op jit(solution)/shard_map/ppermute | solution.py:469
  50.1 5.6 %collective-permute-start.10 = (bf16[80,384]{1,0:T(8,128)(2,1)S(1)}, bf16[80,384]{1,0:T(8,128)(2,1)S(1)}, u32[]{:S(2)}, u32[]{:S(2)}) collective-permute-start(bf16[80,384]{1,0:T(8,128)(2,1)S(1)} %get-tuple-element.73.refs_0_), channel_id=1, source_target_pairs={{0,16},{1,17},{2,18},{3,19},{4,20},{5,21},{6,22},{7,23},{8,24},{9,... | collective-permute-start | bytes 184328 | tf_op jit(solution)/shard_map/ppermute | solution.py:469
  50.1 5.6 %collective-permute-start.9 = (bf16[80,384]{1,0:T(8,128)(2,1)S(1)}, bf16[80,384]{1,0:T(8,128)(2,1)S(1)}, u32[]{:S(2)}, u32[]{:S(2)}) collective-permute-start(bf16[80,384]{1,0:T(8,128)(2,1)S(1)} %get-tuple-element.73.refs_0_), channel_id=1, source_target_pairs={{0,8},{1,9},{2,10},{3,11},{4,12},{5,13},{6,14},{7,15},{8,0},{9,1},... | collective-permute-start | bytes 184328 | tf_op jit(solution)/shard_map/ppermute | solution.py:469
  55.7 5.8 %collective-permute-start.12 = (bf16[160,384]{1,0:T(8,128)(2,1)S(1)}, bf16[160,384]{1,0:T(8,128)(2,1)S(1)}, u32[]{:S(2)}, u32[]{:S(2)}) collective-permute-start(bf16[160,384]{1,0:T(8,128)(2,1)S(1)} %get-tuple-element.74.a_ref), channel_id=1, source_target_pairs={{0,4},{1,5},{2,6},{3,7},{4,0},{5,1},{6,2},{7,3},{8,12},{9,13},{10,... | collective-permute-start | bytes 368648 | tf_op jit(solution)/shard_map/ppermute | solution.py:469
  56.3 6.2 %collective-permute-start.13 = (bf16[160,384]{1,0:T(8,128)(2,1)S(1)}, bf16[160,384]{1,0:T(8,128)(2,1)S(1)}, u32[]{:S(2)}, u32[]{:S(2)}) collective-permute-start(bf16[160,384]{1,0:T(8,128)(2,1)S(1)} %get-tuple-element.75.b_ref), channel_id=1, source_target_pairs={{0,2},{1,3},{2,0},{3,1},{4,6},{5,7},{6,4},{7,5},{8,10},{9,11},{10,... | collective-permute-start | bytes 368648 | tf_op jit(solution)/shard_map/ppermute | solution.py:469
  62.6 6.3 %collective-permute-start.14 = (bf16[320,384]{1,0:T(8,128)(2,1)S(1)}, bf16[320,384]{1,0:T(8,128)(2,1)S(1)}, u32[]{:S(2)}, u32[]{:S(2)}) collective-permute-start(bf16[320,384]{1,0:T(8,128)(2,1)S(1)} %get-tuple-element.77), channel_id=1, source_target_pairs={{0,2},{1,3},{2,0},{3,1},{4,6},{5,7},{6,4},{7,5},{8,10},{9,11},{10,... | collective-permute-start | bytes 737288 | tf_op jit(solution)/shard_map/ppermute | solution.py:469
  63.9 6.2 %collective-permute-start.15 = (bf16[320,384]{1,0:T(8,128)(2,1)S(1)}, bf16[320,384]{1,0:T(8,128)(2,1)S(1)}, u32[]{:S(2)}, u32[]{:S(2)}) collective-permute-start(bf16[320,384]{1,0:T(8,128)(2,1)S(1)} %get-tuple-element.78), channel_id=1, source_target_pairs={{0,4},{1,5},{2,6},{3,7},{4,0},{5,1},{6,2},{7,3},{8,12},{9,13},{10,... | collective-permute-start | bytes 737288 | tf_op jit(solution)/shard_map/ppermute | solution.py:469
  65.6 6.0 %collective-permute-start.16 = (bf16[2,320,384]{2,1,0:T(8,128)(2,1)S(1)}, bf16[2,320,384]{2,1,0:T(8,128)(2,1)S(1)}, u32[]{:S(2)}, u32[]{:S(2)}) collective-permute-start(bf16[2,320,384]{2,1,0:T(8,128)(2,1)S(1)} %get-tuple-element.76.early), channel_id=1, source_target_pairs={{0,1},{1,0},{2,3},{3,2},{4,5},{5,4},{6,7},{7,6},{8,9},{9,8},{10,11... | collective-permute-start | bytes 1474568 | tf_op jit(solution)/shard_map/ppermute | solution.py:469
  68.9 1.5 %collective-permute-start.17 = (bf16[320,384]{1,0:T(8,128)(2,1)S(1)}, bf16[320,384]{1,0:T(8,128)(2,1)S(1)}, u32[]{:S(2)}, u32[]{:S(2)}) collective-permute-start(bf16[320,384]{1,0:T(8,128)(2,1)S(1)} %collective-permute-done.14.a_late), channel_id=1, source_target_pairs={{0,1},{1,0},{2,3},{3,2},{4,5},{5,4},{6,7},{7,6},{8,9},{9,8},{10,11... | collective-permute-start | bytes 737288 | tf_op jit(solution)/shard_map/ppermute | solution.py:469
  70.1 1.5 %collective-permute-start.18 = (bf16[320,384]{1,0:T(8,128)(2,1)S(1)}, bf16[320,384]{1,0:T(8,128)(2,1)S(1)}, u32[]{:S(2)}, u32[]{:S(2)}) collective-permute-start(bf16[320,384]{1,0:T(8,128)(2,1)S(1)} %collective-permute-done.15.b_late), channel_id=1, source_target_pairs={{0,1},{1,0},{2,3},{3,2},{4,5},{5,4},{6,7},{7,6},{8,9},{9,8},{10,11... | collective-permute-start | bytes 737288 | tf_op jit(solution)/shard_map/ppermute | solution.py:469
